TPU v7x, 512 devices: a whole 4x8x8 slice. The times are simulated.
512 devices in a mesh: row: 16 (over z, core), col: 32 (over x, y).
Axes of the slice: x: 4, y: 8, z: 8, core: 2. Of those that a mesh axis runs over, the one named last changes fastest.
Arguments:
- tokens: bfloat16 [512, 8192], P('col', 'row'), may hold values from -24 to 24
- scales: float32 [8192], P('row'), may hold values from 0.25 to 4
- gate_weight: bfloat16 [8192, 16384], P('row', 'col'), may hold values from -0.0625 to 0.0625
- up_weight: bfloat16 [8192, 16384], P('row', 'col'), may hold values from -0.0625 to 0.0625
- down_weight: bfloat16 [16384, 8192], P('col', 'row'), may hold values from -0.046875 to 0.046875
- gate_mask: int32 [64, 128], P('row', 'col'), may hold values 0 or 1
- up_mask: int32 [64, 128], P('row', 'col'), may hold values 0 or 1
- down_mask: int32 [128, 64], P('col', 'row'), may hold values 0 or 1
- cotangent: bfloat16 [512, 8192], P('col', 'row'), may hold values from -4 to 4
Outputs:
- output: bfloat16 [512, 8192], P('col', 'row')
- input_grad: bfloat16 [512, 8192], P('col', 'row')
- gate_grad: bfloat16 [8192, 16384], P('row', 'col')
- up_grad: bfloat16 [8192, 16384], P('row', 'col')
- down_grad: bfloat16 [16384, 8192], P('col', 'row')
Inputs may be any that keep to these rules, and one draw needn't show every extreme that they name: gate_mask is 1 where a 128 x 128 tile of gate_weight is kept and 0 where it is pruned. up_mask is 1 where a tile of up_weight is kept and 0 where it is pruned. down_mask is 1 where a tile of down_weight is kept and 0 where it is pruned.
All inputs are finite; a program needn't handle non-finite values. No bound on the sum of `gate_mask` or of `up_mask` or of `down_mask` on one device may be relied on, other than what follows from the above.
Results may differ from a plain program's by a relative error of at most 0.039.
Values may be sent and summed in bfloat16 or wider, within the bound.
No kernel may reach another device: no remote copies, remote signals or barrier semaphores. Data moves between devices by JAX's collectives and lax.ppermute only.
A program may use at most 64 MiB of HBM per device.

v0:
```python
import jax
import jax.numpy as jnp
from jax import lax
from jax.sharding import PartitionSpec as P

D = 8192
TILE = 128


clip_ratio = 1.5


def expand(mask):
    return jnp.repeat(jnp.repeat(mask, TILE, axis=0), TILE, axis=1).astype(jnp.float32)


def contract_last(left, right):
    return lax.dot_general(
        left, right, (((1,), (1,)), ((), ())), preferred_element_type=jnp.float32
    )


def contract_first(left, right):
    return lax.dot_general(
        left, right, (((0,), (0,)), ((), ())), preferred_element_type=jnp.float32
    )


def clip_tokens(smoothed, squares):
    limits = clip_ratio * jnp.sqrt(squares / D + 1e-06)[:, None]
    squashed = jnp.tanh(smoothed / limits)
    return (squashed, (limits * squashed).astype(jnp.bfloat16))


def swiglu_parts(gate_pre):
    sigmoid_gate = jax.nn.sigmoid(gate_pre)
    silu_gate = gate_pre * sigmoid_gate
    return (sigmoid_gate, silu_gate)


def swiglu_grads(hidden_grad, gate_pre, up_pre):
    sigmoid_gate, silu_gate = swiglu_parts(gate_pre)
    gate_dir = (
        hidden_grad * up_pre * sigmoid_gate * (1.0 + gate_pre * (1.0 - sigmoid_gate))
    ).astype(jnp.bfloat16)
    up_dir = (hidden_grad * silu_gate).astype(jnp.bfloat16)
    return jnp.concatenate([gate_dir, up_dir], axis=1)


def per_device(
    tokens, scales, gate_weight, up_weight, down_weight, gate_mask, up_mask, down_mask, cotangent
):
    hidden_width = gate_weight.shape[1]
    gate_keep = expand(gate_mask)
    up_keep = expand(up_mask)
    down_keep = expand(down_mask)
    gate_kept = (scales[:, None] * gate_weight.astype(jnp.float32) * gate_keep).astype(jnp.bfloat16)
    up_kept = (scales[:, None] * up_weight.astype(jnp.float32) * up_keep).astype(jnp.bfloat16)
    down_kept = down_weight * down_keep.astype(jnp.bfloat16)
    both_kept = jnp.concatenate([gate_kept, up_kept], axis=1)
    smoothed = tokens.astype(jnp.float32) / scales
    squares = lax.psum(jnp.sum(smoothed * smoothed, axis=1), "row")
    squashed, quantized = clip_tokens(smoothed, squares)
    quantized_all = lax.all_gather(quantized, "col", axis=0, tiled=True)
    picked = quantized_all
    gate_up = lax.psum(
        jnp.dot(picked, both_kept, preferred_element_type=jnp.float32).astype(jnp.bfloat16), "row"
    ).astype(jnp.float32)
    gate_pre = gate_up[:, :hidden_width]
    up_pre = gate_up[:, hidden_width:]
    sigmoid_gate, silu_gate = swiglu_parts(gate_pre)
    hidden_all = (silu_gate * up_pre).astype(jnp.bfloat16)
    picked = hidden_all
    output = lax.psum_scatter(
        jnp.dot(picked, down_kept, preferred_element_type=jnp.float32).astype(jnp.bfloat16),
        "col",
        scatter_dimension=0,
        tiled=True,
    )
    cotangent_all = lax.all_gather(cotangent, "col", axis=0, tiled=True)
    down_grad = (contract_first(hidden_all, cotangent_all) * down_keep).astype(jnp.bfloat16)
    picked = cotangent_all
    hidden_grad = lax.psum(contract_last(picked, down_kept).astype(jnp.bfloat16), "row").astype(
        jnp.float32
    )
    both_dirs_all = swiglu_grads(hidden_grad, gate_pre, up_pre)
    picked = both_dirs_all
    quant_grad = lax.psum_scatter(
        contract_last(picked, both_kept).astype(jnp.bfloat16),
        "col",
        scatter_dimension=0,
        tiled=True,
    ).astype(jnp.float32)
    input_grad = (quant_grad * (1.0 - squashed * squashed) / scales).astype(jnp.bfloat16)
    weight_product = contract_first(quantized_all, both_dirs_all)
    gate_grad = (scales[:, None] * weight_product[:, :hidden_width] * gate_keep).astype(
        jnp.bfloat16
    )
    up_grad = (scales[:, None] * weight_product[:, hidden_width:] * up_keep).astype(jnp.bfloat16)
    return (output, input_grad, gate_grad, up_grad, down_grad)


def solution(mesh):
    placed = (
        P("col", "row"),
        P("row"),
        P("row", "col"),
        P("row", "col"),
        P("col", "row"),
        P("row", "col"),
        P("row", "col"),
        P("col", "row"),
        P("col", "row"),
    )
    return jax.shard_map(
        per_device,
        mesh=mesh,
        in_specs=placed,
        out_specs=(
            P("col", "row"),
            P("col", "row"),
            P("row", "col"),
            P("row", "col"),
            P("col", "row"),
        ),
        check_vma=False,
    )
```

profile of v0, /device:TPU:1, one launch (start us, length us, event | category | flops | bytes accessed | tf_op | source)
XLA Modules:
  0.0 709.3 jit_solution(10551113524191224439)
XLA Ops:
  7.2 0.0 all-reduce.3.cloned.1.call-start
  7.2 0.9 fusion.15
  8.1 30.6 %psum.21 = f32[16]{0:T(128)S(1)} all-reduce(f32[16]{0:T(128)S(1)} %fusion.15), channel_id=1, replica_groups=mesh['row'=16,'col'=32] {'row'}, use_global_device_ids=true, to_apply=%region_1.0 | all-reduce | flops 16 | bytes 128 | tf_op jit(solution)/shard_map/psum | solution.py:62
  38.7 0.7 convert_element_type.102
  39.4 0.7 convert_element_type.107
  40.1 0.7 convert_element_type.114
  40.8 0.8 multiply_convert_fusion.1
  41.6 38.7 %all_gather.6 = bf16[512,512]{1,0:T(8,128)(2,1)S(1)} all-gather(bf16[16,512]{1,0:T(8,128)(2,1)S(1)} %multiply_convert_fusion.1), channel_id=1, replica_groups=mesh['row'=16,'col'=32] {'col'}, dimensions={0}, use_global_device_ids=true | all-gather | bytes 540672 | tf_op jit(solution)/shard_map/all_gather | solution.py:64
  80.3 36.5 %all_gather.7 = bf16[512,512]{1,0:T(8,128)(2,1)S(1)} all-gather(bf16[16,512]{1,0:T(8,128)(2,1)} %param.17), channel_id=1, replica_groups=mesh['row'=16,'col'=32] {'col'}, dimensions={0}, use_global_device_ids=true | all-gather | bytes 540672 | tf_op jit(solution)/shard_map/all_gather | solution.py:80
  116.9 0.6 broadcast_in_dim.30
  117.5 1.3 fusion.1
  118.8 0.6 broadcast_in_dim.26
  119.4 0.6 broadcast_in_dim.28
  120.1 0.3 fusion.8
  120.4 0.8 copy-done.9
  121.2 0.2 copy-done.11
  121.3 1.7 convolution_convert_fusion
  123.1 0.0 reduce-scatter.5.cloned.1.call-start
  123.1 138.4 %all-reduce.3.cloned.1.call-done = (bf16[512,1024]{1,0:T(8,128)(2,1)}, bf16[512,512]{1,0:T(8,128)(2,1)}) async-done(((bf16[512,1024]{1,0:T(8,128)(2,1)}, bf16[512,512]{1,0:T(8,128)(2,1)}), (bf16[512,1024]{1,0:T(8,128)(2,1)}, bf16[512,512]{1,0:T(8,128)(2,1)})) %all-reduce.3.cloned.1.call-update) | async-done | bytes 1572880 | tf_op jit(solution)/shard_map/psum | solution.py:66
  261.5 1.5 convert_element_type.112
  263.1 1.4 fusion.4
  264.5 0.8 copy-done.3
  265.3 0.2 copy-done.5
  265.5 1.6 convolution_convert_fusion.3
  267.1 0.0 reduce-scatter.3.cloned.1.call-start
  267.2 2.5 convolution_convert_fusion.2
  269.7 2.6 fusion
  272.3 0.7 fusion.11
  273.0 1.2 fusion.7
  274.3 206.1 %reduce-scatter.5.cloned.1.call-done = bf16[16,512]{1,0:T(8,128)(2,1)} async-done(((bf16[512,512]{1,0:T(8,128)(2,1)}), bf16[16,512]{1,0:T(8,128)(2,1)}) %reduce-scatter.5.cloned.1.call-update) | async-done | bytes 16400 | tf_op jit(solution)/shard_map/reduce_scatter | solution.py:88
  480.4 1.4 divide_convert_fusion
  481.8 220.9 %reduce-scatter.3.cloned.1.call-done = bf16[16,512]{1,0:T(8,128)(2,1)} async-done(((bf16[512,512]{1,0:T(8,128)(2,1)}), bf16[16,512]{1,0:T(8,128)(2,1)}) %reduce-scatter.3.cloned.1.call-update) | async-done | bytes 16400 | tf_op jit(solution)/shard_map/reduce_scatter | solution.py:74
  (37 shorter events, 0.2 us)
Async XLA Ops:
  7.2 110.3 %copy-start.16 = (bf16[512,512]{1,0:T(8,128)(2,1)S(1)}, bf16[512,512]{1,0:T(8,128)(2,1)}, u32[]{:S(2)}) copy-start(bf16[512,512]{1,0:T(8,128)(2,1)} %param.13) | copy-start | bytes 1572868
  7.2 254.3 %all-reduce.3.cloned.1.call-start = ((), (), s32[]{:S(2)}) async-start(), calls=%async_computation.4 | async-start | bytes 3145728 | tf_op jit(solution)/shard_map/psum | solution.py:66
  80.3 40.0 %copy-start = (bf16[512,512]{1,0:T(8,128)(2,1)}, bf16[512,512]{1,0:T(8,128)(2,1)S(1)}, u32[]{:S(2)}) copy-start(bf16[512,512]{1,0:T(8,128)(2,1)S(1)} %all_gather.6) | copy-start | bytes 1572868
  116.8 2.0 copy-start.2
  118.8 1.3 copy-start.7
  118.8 1.3 copy-start.8
  118.8 1.3 copy-start.15
  120.4 0.8 copy-start.9
  120.4 1.0 copy-start.11
  123.1 357.3 %reduce-scatter.5.cloned.1.call-start = ((), (), s32[]{:S(2)}) async-start(), calls=%async_computation.3 | async-start | bytes 540672 | tf_op jit(solution)/shard_map/reduce_scatter | solution.py:88
  261.5 1.5 copy-start.13
  263.1 2.4 copy-start.10
  263.1 2.4 copy-start.12
  264.5 0.8 copy-start.3
  264.5 1.0 copy-start.5
  267.1 435.6 %reduce-scatter.3.cloned.1.call-start = ((), (), s32[]{:S(2)}) async-start(), calls=%async_computation.2 | async-start | bytes 540672 | tf_op jit(solution)/shard_map/reduce_scatter | solution.py:74
  269.7 2.6 copy-start.1
  269.7 2.6 copy-start.4
  269.7 2.6 copy-start.6
  273.0 207.4 %copy-start.14 = (bf16[16,512]{1,0:T(8,128)(2,1)S(1)}, bf16[16,512]{1,0:T(8,128)(2,1)}, u32[]{:S(2)}) copy-start(bf16[16,512]{1,0:T(8,128)(2,1)} %param.9) | copy-start | bytes 49156
Sparse Core Ops, SparseCore 0:
  123.2 138.3 all-reduce.2
  267.2 213.1 reduce-scatter.4
  485.4 217.3 reduce-scatter.2
where the time goes:
time: 714 us; the launch traced here: 709 us
  waiting for transfers between devices  566 us (79%)
  blocking collectives  106 us (15%)
  between operations  13.9 us (2%)
  matrix products  10.3 us (1%)
  other arithmetic  9.67 us (1%)
    reduce_scatter x1, waiting for transfers between devices, per_device(): lax.psum_scatter(jnp.dot(picked, down_kept, preferred_element_type=jnp.fl...  221 us
    reduce_scatter x1, waiting for transfers between devices, per_device(): lax.psum_scatter(contract_last(picked, both_kept).astype(jnp.bfloat16), '...  206 us
    psum x1, waiting for transfers between devices, per_device(): lax.psum(jnp.dot(picked, both_kept, preferred_element_type=jnp.float32).a...  138 us
    all_gather x1, blocking collectives, per_device(): quantized_all = lax.all_gather(quantized, 'col', axis=0, tiled=True)  38.7 us
    all_gather x1, blocking collectives, per_device(): cotangent_all = lax.all_gather(cotangent, 'col', axis=0, tiled=True)  36.5 us
    psum x1, blocking collectives, per_device(): squares = lax.psum(jnp.sum(smoothed * smoothed, axis=1), 'row')  30.6 us
  transfers between devices with their start and end apart: 3, of which 3 were waited for; matrix products, arithmetic and copies ran while one was open for 1% of the time, Pallas kernels for 0%

commit v1 on v0

v1 whole, which is shorter than its diff:
```python
import jax
import jax.numpy as jnp
from jax import lax
from jax.sharding import Mesh, PartitionSpec as P

D = 8192
TILE = 128
ROW = ("z", "core")
COL = ("x", "y")
N_Z, N_CORE, N_X, N_Y = 8, 2, 4, 8
N_ROW = N_Z * N_CORE
N_COL = N_X * N_Y


clip_ratio = 1.5


def expand(mask):
    return jnp.repeat(jnp.repeat(mask, TILE, axis=0), TILE, axis=1).astype(jnp.float32)


def matmul(left, right):
    return jnp.dot(left, right, preferred_element_type=jnp.float32)


def contract_last(left, right):
    return lax.dot_general(
        left, right, (((1,), (1,)), ((), ())), preferred_element_type=jnp.float32
    )


def contract_first(left, right):
    return lax.dot_general(
        left, right, (((0,), (0,)), ((), ())), preferred_element_type=jnp.float32
    )


def to_everyone(block, axis, size):
    copies = jnp.broadcast_to(block[None], (size,) + block.shape)
    return lax.all_to_all(copies, axis, 0, 0, tiled=True)


def exchange_sum(total, axis, size):
    rows = total.shape[0] // size
    parts = lax.all_to_all(
        total.reshape(size, rows, total.shape[1]), axis, 0, 0, tiled=True
    )
    return jnp.sum(parts.astype(jnp.float32), axis=0)


def swap_cores(block):
    return lax.ppermute(block, "core", [(0, 1), (1, 0)])


def half_of(block, which):
    rows = block.shape[0] // N_CORE
    return lax.dynamic_slice_in_dim(block, which * rows, rows, 0)


def join_halves(own, other, core):
    return jnp.where(
        core == 0,
        jnp.concatenate([own, other], axis=0),
        jnp.concatenate([other, own], axis=0),
    )


def per_device(
    tokens, scales, gate_weight, up_weight, down_weight, gate_mask, up_mask, down_mask, cotangent
):
    hidden_width = gate_weight.shape[1]
    width = tokens.shape[1]
    core = lax.axis_index("core")
    gate_keep = expand(gate_mask)
    up_keep = expand(up_mask)
    down_keep = expand(down_mask)
    gate_kept = (scales[:, None] * gate_weight.astype(jnp.float32) * gate_keep).astype(jnp.bfloat16)
    up_kept = (scales[:, None] * up_weight.astype(jnp.float32) * up_keep).astype(jnp.bfloat16)
    down_kept = down_weight * down_keep.astype(jnp.bfloat16)
    both_kept = jnp.concatenate([gate_kept, up_kept], axis=1)

    smoothed = tokens.astype(jnp.float32) / scales
    squares = to_everyone(jnp.sum(smoothed * smoothed, axis=1)[None], ROW, N_ROW)
    squares = jnp.sum(squares.reshape(N_ROW, -1), axis=0)
    limits = clip_ratio * jnp.sqrt(squares / D + 1e-06)[:, None]
    squashed = jnp.tanh(smoothed / limits)
    quantized = (limits * squashed).astype(jnp.bfloat16)

    both_in = jnp.concatenate([quantized, cotangent], axis=1)
    both_in = to_everyone(both_in, COL, N_COL).reshape(-1, 2 * width)

    def partial_sums(rows):
        gate_up = matmul(rows[:, :width], both_kept)
        hidden_grad = contract_last(rows[:, width:], down_kept)
        return jnp.concatenate([gate_up, hidden_grad], axis=1)

    theirs = swap_cores(partial_sums(half_of(both_in, 1 - core)).astype(jnp.bfloat16))
    own = partial_sums(half_of(both_in, core))
    pair_sum = (own + theirs.astype(jnp.float32)).astype(jnp.bfloat16)
    pre = exchange_sum(pair_sum, "z", N_Z)

    gate_pre = pre[:, :hidden_width]
    up_pre = pre[:, hidden_width : 2 * hidden_width]
    hidden_grad = pre[:, 2 * hidden_width :]
    sigmoid_gate = jax.nn.sigmoid(gate_pre)
    silu_gate = gate_pre * sigmoid_gate
    hidden = (silu_gate * up_pre).astype(jnp.bfloat16)
    gate_dir = (
        hidden_grad * up_pre * sigmoid_gate * (1.0 + gate_pre * (1.0 - sigmoid_gate))
    ).astype(jnp.bfloat16)
    up_dir = (hidden_grad * silu_gate).astype(jnp.bfloat16)
    mid = jnp.concatenate([gate_dir, up_dir, hidden], axis=1)

    own_mid = to_everyone(mid, "z", N_Z).reshape(-1, 3 * hidden_width)
    other_mid = swap_cores(own_mid)

    def back_sums(rows):
        output = matmul(rows[:, 2 * hidden_width :], down_kept)
        quant_grad = contract_last(rows[:, : 2 * hidden_width], both_kept)
        return jnp.concatenate([output, quant_grad], axis=1).astype(jnp.bfloat16)

    back = join_halves(back_sums(own_mid), back_sums(other_mid), core)
    back = exchange_sum(back, "x", N_X).astype(jnp.bfloat16)
    back = exchange_sum(back, "y", N_Y)
    output = back[:, :width].astype(jnp.bfloat16)
    input_grad = (back[:, width:] * (1.0 - squashed * squashed) / scales).astype(jnp.bfloat16)

    own_in = half_of(both_in, core)
    other_in = half_of(both_in, 1 - core)
    weight_product = contract_first(
        own_in[:, :width], own_mid[:, : 2 * hidden_width]
    ) + contract_first(other_in[:, :width], other_mid[:, : 2 * hidden_width])
    down_product = contract_first(own_mid[:, 2 * hidden_width :], own_in[:, width:]) + (
        contract_first(other_mid[:, 2 * hidden_width :], other_in[:, width:])
    )
    gate_grad = (scales[:, None] * weight_product[:, :hidden_width] * gate_keep).astype(
        jnp.bfloat16
    )
    up_grad = (scales[:, None] * weight_product[:, hidden_width:] * up_keep).astype(jnp.bfloat16)
    down_grad = (down_product * down_keep).astype(jnp.bfloat16)
    return (output, input_grad, gate_grad, up_grad, down_grad)


def solution(mesh):
    fine = Mesh(mesh.devices.reshape(N_Z, N_CORE, N_X, N_Y), ROW + COL)
    placed = (
        P(COL, ROW),
        P(ROW),
        P(ROW, COL),
        P(ROW, COL),
        P(COL, ROW),
        P(ROW, COL),
        P(ROW, COL),
        P(COL, ROW),
        P(COL, ROW),
    )
    return jax.shard_map(
        per_device,
        mesh=fine,
        in_specs=placed,
        out_specs=(
            P(COL, ROW),
            P(COL, ROW),
            P(ROW, COL),
            P(ROW, COL),
            P(COL, ROW),
        ),
        check_vma=False,
    )
```

time: 714 us -> 171 us (0.24)
  waiting for transfers between devices: 566 us -> 35 us
  blocking collectives: 106 us -> 70.6 us
  starting transfers between devices: 0.12 us -> 27 us
  between operations: 13.9 us -> 1.03 us
  matrix products: 10.3 us -> 19.9 us
    reduce_scatter x2 -> x0, waiting for transfers between devices: 427 us -> none  [the longest x1 221 us: per_device(): lax.psum_scatter(jnp.dot(picked, down_kept, preferred_element_type=jnp.fl...]
    psum x1 -> x0, waiting for transfers between devices: 138 us -> none  [per_device(): lax.psum(jnp.dot(picked, both_kept, preferred_element_type=jnp.float32).a...]
    all_gather x2 -> x0, blocking collectives: 75.2 us -> none  [the longest x1 38.7 us: per_device(): quantized_all = lax.all_gather(quantized, 'col', axis=0, tiled=True)]
    all_to_all x0 -> x3, blocking collectives: none -> 70.6 us  [the longest x2 44.6 us: to_everyone(): return lax.all_to_all(copies, axis, 0, 0, tiled=True)]
    all_to_all x0 -> x3, waiting for transfers between devices: none -> 35 us  [the longest x1 20.4 us: to_everyone(): return lax.all_to_all(copies, axis, 0, 0, tiled=True)]
    psum x1 -> x0, blocking collectives: 30.6 us -> none  [per_device(): squares = lax.psum(jnp.sum(smoothed * smoothed, axis=1), 'row')]
    all_to_all x0 -> x3, starting transfers between devices: none -> 17.7 us  [the longest x1 9.93 us: to_everyone(): return lax.all_to_all(copies, axis, 0, 0, tiled=True)]
    ppermute x0 -> x2, starting transfers between devices: none -> 9.3 us  [swap_cores(): return lax.ppermute(block, 'core', [(0, 1), (1, 0)])]
  transfers between devices with their start and end apart: 3 -> 5, of which waited for: 3 -> 3; matrix products, arithmetic and copies ran while one was open for 1% -> 11% of each run, Pallas kernels for 0% -> 0%
where the time goes in v1:
time: 171 us; the launch traced here: 169 us
  blocking collectives  70.6 us (41%)
  waiting for transfers between devices  35 us (20%)
  starting transfers between devices  27 us (16%)
  matrix products  19.9 us (12%)
  other arithmetic  10.8 us (6%)
  local copies, waits for them, and re-layouts  4.69 us (3%)
    all_to_all x2, blocking collectives, to_everyone(): return lax.all_to_all(copies, axis, 0, 0, tiled=True)  44.6 us
    all_to_all x1, blocking collectives, exchange_sum(): lax.all_to_all(total.reshape(size, rows, total.shape[1]), axis, 0, 0, til...  26 us
    all_to_all x1, waiting for transfers between devices, to_everyone(): return lax.all_to_all(copies, axis, 0, 0, tiled=True)  20.4 us
    all_to_all x2, waiting for transfers between devices, exchange_sum(): lax.all_to_all(total.reshape(size, rows, total.shape[1]), axis, 0, 0, til...  14.6 us
    all_to_all x1, starting transfers between devices, to_everyone(): return lax.all_to_all(copies, axis, 0, 0, tiled=True)  9.93 us
    ppermute x2, starting transfers between devices, swap_cores(): return lax.ppermute(block, 'core', [(0, 1), (1, 0)])  9.3 us
    dot_general x4, matrix products, contract_first(): lax.dot_general(left, right, (((0,), (0,)), ((), ())), preferred_element_...  9.23 us
    all_to_all x2, starting transfers between devices, exchange_sum(): lax.all_to_all(total.reshape(size, rows, total.shape[1]), axis, 0, 0, til...  7.82 us
  transfers between devices with their start and end apart: 5, of which 3 were waited for; matrix products, arithmetic and copies ran while one was open for 11% of the time, Pallas kernels for 0%

profile of v1, /device:TPU:1, one launch (start us, length us, event | category | flops | bytes accessed | tf_op | source)
XLA Modules:
  0.0 169.1 jit_solution(5942886409433230621)
XLA Ops:
  0.7 0.9 fusion.33
  1.5 18.6 %all_to_all.30 = f32[16,1,16]{2,1,0:T(1,128)S(1)} all-to-all(f32[16,1,16]{2,1,0:T(1,128)S(1)} %broadcast_in_dim.18), channel_id=1, replica_groups=mesh['z'=8,'core'=2,'x'=4,'y'=8] {'z','core'}, dimensions={0} | all-to-all | bytes 2048 | tf_op jit(solution)/shard_map/all_to_all | solution.py:40
  20.2 0.8 multiply_convert_fusion.3
  21.0 0.7 pad_maximum_fusion.3
  21.7 1.1 broadcast_in_dim.19
  22.8 9.9 %all-to-all-start.1 = ((bf16[32,16,1024]{2,1,0:T(8,128)(2,1)}), bf16[32,16,1024]{2,1,0:T(8,128)(2,1)}, u32[]{:S(2)}, u32[]{:S(2)}) async-start(bf16[32,16,1024]{2,1,0:T(8,128)(2,1)} %broadcast_in_dim.19), calls=%async_computation.1 | async-start | bytes 2097152 | tf_op jit(solution)/shard_map/all_to_all | solution.py:40
  34.9 1.0 copy-done
  35.9 1.1 fusion.5
  37.0 20.4 %all-to-all-done.1 = bf16[32,16,1024]{2,1,0:T(8,128)(2,1)} async-done(((bf16[32,16,1024]{2,1,0:T(8,128)(2,1)}), bf16[32,16,1024]{2,1,0:T(8,128)(2,1)}, u32[]{:S(2)}, u32[]{:S(2)}) %all-to-all-start.1) | async-done | bytes 1048608 | tf_op jit(solution)/shard_map/all_to_all | solution.py:40
  57.4 1.3 convolution_convert_fusion.5
  58.7 1.6 convolution_convert_fusion
  60.3 6.9 %collective-permute-start = (bf16[256,1536]{1,0:T(8,128)(2,1)S(1)}, bf16[256,1536]{1,0:T(8,128)(2,1)}, u32[]{:S(2)}, u32[]{:S(2)}) collective-permute-start(bf16[256,1536]{1,0:T(8,128)(2,1)S(1)} %pad_maximum_fusion.1), channel_id=1, source_target_pairs={{0,32},{32,0},{1,33},{33,1},{2,34},{34,2},{3,35},{35,3},{4,36},{36... | collective-permute-start | bytes 2359304 | tf_op jit(solution)/shard_map/ppermute | solution.py:52
  67.2 1.7 %fusion.21 = f32[256,1024]{1,0:T(8,128)S(1)} fusion(bf16[512,1024]{1,0:T(8,128)(2,1)} %bitcast.1, s32[]{:T(128)S(6)} %select_n.21, bf16[512,512]{1,0:T(8,128)(2,1)} %get-tuple-element.11, bf16[512,512]{1,0:T(8,128)(2,1)} %copy-done.6), kind=kOutput, calls=%fused_computation.42 | convolution fusion | flops 270532608 | bytes 2359300 | tf_op jit(solution)/shard_map/dot_general | solution.py:23
  68.9 1.3 fusion.26
  70.2 1.4 fusion
  71.6 26.0 %all_to_all.31 = bf16[8,32,1536]{2,1,0:T(8,128)(2,1)S(1)} all-to-all(bf16[8,32,1536]{2,1,0:T(8,128)(2,1)S(1)} %bitcast.47), channel_id=1, replica_groups=mesh['z'=8,'core'=2,'x'=4,'y'=8] {'z'}, dimensions={0} | all-to-all | bytes 1572864 | tf_op jit(solution)/shard_map/all_to_all | solution.py:45
  97.9 25.9 %all_to_all.32 = bf16[8,32,1536]{2,1,0:T(8,128)(2,1)S(1)} all-to-all(bf16[8,32,1536]{2,1,0:T(8,128)(2,1)S(1)} %broadcast_in_dim.50), channel_id=1, replica_groups=mesh['z'=8,'core'=2,'x'=4,'y'=8] {'z'}, dimensions={0} | all-to-all | bytes 1572864 | tf_op jit(solution)/shard_map/all_to_all | solution.py:40
  123.8 2.4 %collective-permute-start.1 = (bf16[256,1536]{1,0:T(8,128)(2,1)S(1)}, bf16[256,1536]{1,0:T(8,128)(2,1)}, u32[]{:S(2)}, u32[]{:S(2)}) collective-permute-start(bf16[256,1536]{1,0:T(8,128)(2,1)S(1)} %bitcast.41), channel_id=1, source_target_pairs={{0,32},{32,0},{1,33},{33,1},{2,34},{34,2},{3,35},{35,3},{4,36},{36... | collective-permute-start | bytes 2359304 | tf_op jit(solution)/shard_map/ppermute | solution.py:52
  126.3 1.8 %convolution_convert_fusion.3 = bf16[256,512]{1,0:T(8,128)(2,1)S(1)} fusion(bf16[256,1536]{1,0:T(8,128)(2,1)S(1)} %bitcast.42, bf16[512,512]{1,0:T(8,128)(2,1)} %get-tuple-element.11, bf16[512,512]{1,0:T(8,128)(2,1)} %copy-done.6), kind=kOutput, calls=%fused_computation.10 | convolution fusion | flops 270663680 | bytes 1835008 | tf_op jit(solution)/shard_map/dot_general | solution.py:27
  128.4 1.5 convolution_convert_fusion.1
  129.9 1.2 convolution_convert_fusion.2
  131.2 1.5 maximum_select_fusion
  132.6 4.3 %all-to-all-start.4 = ((bf16[4,128,1024]{2,1,0:T(8,128)(2,1)}), bf16[4,128,1024]{2,1,0:T(8,128)(2,1)}, u32[]{:S(2)}, u32[]{:S(2)}) async-start(bf16[4,128,1024]{2,1,0:T(8,128)(2,1)} %bitcast.46), calls=%async_computation.4 | async-start | bytes 2097152 | tf_op jit(solution)/shard_map/all_to_all | solution.py:45
  136.9 2.2 %fusion.15 = f32[512,512]{1,0:T(8,128)} fusion(bf16[256,1536]{1,0:T(8,128)(2,1)S(1)} %bitcast.44, bf16[512,1024]{1,0:T(8,128)(2,1)} %bitcast.1, s32[]{:T(128)S(6)} %select_n.21, s32[]{:T(128)S(6)} %add.38), kind=kOutput, calls=%fused_computation.36 | convolution fusion | flops 134217728 | bytes 1572872 | tf_op jit(solution)/shard_map/dot_general | solution.py:33
  139.1 1.4 fusion.10
  140.5 2.9 %convolution_add_fusion = f32[512,1024]{1,0:T(8,128)} fusion(f32[512,1024]{1,0:T(8,128)S(1)} %fusion.10, bf16[256,1536]{1,0:T(8,128)(2,1)} %collective-permute-done.1, bf16[512,1024]{1,0:T(8,128)(2,1)} %bitcast.1, s32[]{:T(128)S(6)} %select_n.22), kind=kOutput, calls=%fused_computation | convolution fusion | flops 268959744 | bytes 4980740 | tf_op jit(solution)/shard_map/dot_general | solution.py:33
  143.5 8.4 %all-to-all-done.4 = bf16[4,128,1024]{2,1,0:T(8,128)(2,1)} async-done(((bf16[4,128,1024]{2,1,0:T(8,128)(2,1)}), bf16[4,128,1024]{2,1,0:T(8,128)(2,1)}, u32[]{:S(2)}, u32[]{:S(2)}) %all-to-all-start.4) | async-done | bytes 1048608 | tf_op jit(solution)/shard_map/all_to_all | solution.py:45
  151.9 2.2 %reduce_sum.51 = bf16[128,1024]{1,0:T(8,128)(2,1)} reduce(bf16[4,128,1024]{2,1,0:T(8,128)(2,1)} %all-to-all-done.4, bf16[]{:T(256)} %constant.27.clone.1), dimensions={0}, to_apply=%region_3.4 | reduce | flops 393216 | bytes 1310722 | tf_op jit(solution)/shard_map/reduce_sum | solution.py:48
  154.1 3.6 %all-to-all-start.5 = ((bf16[8,16,1024]{2,1,0:T(8,128)(2,1)}), bf16[8,16,1024]{2,1,0:T(8,128)(2,1)S(1)}, u32[]{:S(2)}, u32[]{:S(2)}) async-start(bf16[8,16,1024]{2,1,0:T(8,128)(2,1)} %bitcast.8), calls=%async_computation.5 | async-start | bytes 524288 | tf_op jit(solution)/shard_map/all_to_all | solution.py:45
  157.7 2.7 %fusion.2 = bf16[512,512]{1,0:T(8,128)(2,1)} fusion(f32[512,512]{1,0:T(8,128)} %fusion.15, f32[64,8,4,128]{3,2,1,0:T(4,128)S(1)} %bitcast.38, bf16[256,1536]{1,0:T(8,128)(2,1)} %collective-permute-done.1, bf16[512,1024]{1,0:T(8,128)(2,1)} %bitcast.1, s32[]{:T(128)S(6)} %select_n.22, s32[]{:T(128)S(6)} %add.38), kind=kOutput, calls=%fused_computation.7 | convolution fusion | flops 135004160 | bytes 3145736 | tf_op jit(solution)/shard_map/dot_general | solution.py:33
  160.3 1.2 fusion.4
  161.6 6.2 %all-to-all-done.5 = bf16[8,16,1024]{2,1,0:T(8,128)(2,1)S(1)} async-done(((bf16[8,16,1024]{2,1,0:T(8,128)(2,1)}), bf16[8,16,1024]{2,1,0:T(8,128)(2,1)S(1)}, u32[]{:S(2)}, u32[]{:S(2)}) %all-to-all-start.5) | async-done | bytes 262176 | tf_op jit(solution)/shard_map/all_to_all | solution.py:45
  (51 shorter events, 4.0 us)
Async XLA Ops:
  0.6 32.2 %copy-start.11 = (s32[4,4]{1,0:T(4,128)S(1)}, s32[4,4]{1,0:T(4,128)}, u32[]{:S(2)}) copy-start(s32[4,4]{1,0:T(4,128)} %param.14) | copy-start | bytes 196
  0.6 32.2 %copy-start.12 = (s32[4,4]{1,0:T(4,128)S(1)}, s32[4,4]{1,0:T(4,128)}, u32[]{:S(2)}) copy-start(s32[4,4]{1,0:T(4,128)} %param.15) | copy-start | bytes 196
  0.7 32.2 %copy-start.13 = (s32[4,4]{1,0:T(4,128)S(1)}, s32[4,4]{1,0:T(4,128)}, u32[]{:S(2)}) copy-start(s32[4,4]{1,0:T(4,128)} %param.16) | copy-start | bytes 196
  22.8 10.6 %copy-start.3 = (bf16[512,512]{1,0:T(8,128)(2,1)S(1)}, bf16[512,512]{1,0:T(8,128)(2,1)}, u32[]{:S(2)}) copy-start(bf16[512,512]{1,0:T(8,128)(2,1)} %param.13) | copy-start | bytes 1572868
  22.8 34.5 %all-to-all-start.1 = ((bf16[32,16,1024]{2,1,0:T(8,128)(2,1)}), bf16[32,16,1024]{2,1,0:T(8,128)(2,1)}, u32[]{:S(2)}, u32[]{:S(2)}) async-start(bf16[32,16,1024]{2,1,0:T(8,128)(2,1)} %broadcast_in_dim.19), calls=%async_computation.1 | async-start | bytes 2097152 | tf_op jit(solution)/shard_map/all_to_all | solution.py:40
  33.6 2.3 %copy-start.4 = (bf16[512,512]{1,0:T(8,128)(2,1)S(1)}, bf16[512,512]{1,0:T(8,128)(2,1)}, u32[]{:S(2)}) copy-start(bf16[512,512]{1,0:T(8,128)(2,1)} %param.11) | copy-start | bytes 1572868
  33.6 2.3 %copy-start.5 = (bf16[512,512]{1,0:T(8,128)(2,1)S(1)}, bf16[512,512]{1,0:T(8,128)(2,1)}, u32[]{:S(2)}) copy-start(bf16[512,512]{1,0:T(8,128)(2,1)} %param.12) | copy-start | bytes 1572868
  33.6 2.3 %copy-start.10 = (f32[512]{0:T(512)S(1)}, f32[512]{0:T(512)}, u32[]{:S(2)}) copy-start(f32[512]{0:T(512)} %param.10) | copy-start | bytes 6148
  34.9 1.0 copy-start
  37.0 21.7 %copy-start.6 = (bf16[512,512]{1,0:T(8,128)(2,1)}, bf16[512,512]{1,0:T(8,128)(2,1)S(1)}, u32[]{:S(2)}) copy-start(bf16[512,512]{1,0:T(8,128)(2,1)S(1)} %get-tuple-element.10) | copy-start | bytes 1572868
  60.3 9.9 %collective-permute-start = (bf16[256,1536]{1,0:T(8,128)(2,1)S(1)}, bf16[256,1536]{1,0:T(8,128)(2,1)}, u32[]{:S(2)}, u32[]{:S(2)}) collective-permute-start(bf16[256,1536]{1,0:T(8,128)(2,1)S(1)} %pad_maximum_fusion.1), channel_id=1, source_target_pairs={{0,32},{32,0},{1,33},{33,1},{2,34},{34,2},{3,35},{35,3},{4,36},{36... | collective-permute-start | bytes 2359304 | tf_op jit(solution)/shard_map/ppermute | solution.py:52
  123.8 4.5 %collective-permute-start.1 = (bf16[256,1536]{1,0:T(8,128)(2,1)S(1)}, bf16[256,1536]{1,0:T(8,128)(2,1)}, u32[]{:S(2)}, u32[]{:S(2)}) collective-permute-start(bf16[256,1536]{1,0:T(8,128)(2,1)S(1)} %bitcast.41), channel_id=1, source_target_pairs={{0,32},{32,0},{1,33},{33,1},{2,34},{34,2},{3,35},{35,3},{4,36},{36... | collective-permute-start | bytes 2359304 | tf_op jit(solution)/shard_map/ppermute | solution.py:52
  126.3 2.1 %copy-start.7 = (bf16[512,512]{1,0:T(8,128)(2,1)S(1)}, bf16[512,512]{1,0:T(8,128)(2,1)}, u32[]{:S(2)}) copy-start(bf16[512,512]{1,0:T(8,128)(2,1)} %copy-done.6) | copy-start | bytes 1572868
  126.3 2.1 %copy-start.8 = (bf16[512,512]{1,0:T(8,128)(2,1)S(1)}, bf16[512,512]{1,0:T(8,128)(2,1)}, u32[]{:S(2)}) copy-start(bf16[512,512]{1,0:T(8,128)(2,1)} %get-tuple-element.11) | copy-start | bytes 1572868
  132.6 19.3 %all-to-all-start.4 = ((bf16[4,128,1024]{2,1,0:T(8,128)(2,1)}), bf16[4,128,1024]{2,1,0:T(8,128)(2,1)}, u32[]{:S(2)}, u32[]{:S(2)}) async-start(bf16[4,128,1024]{2,1,0:T(8,128)(2,1)} %bitcast.46), calls=%async_computation.4 | async-start | bytes 2097152 | tf_op jit(solution)/shard_map/all_to_all | solution.py:45
  154.1 6.2 %copy-start.1 = (f32[512,4,128]{2,1,0:T(4,128)S(1)}, f32[512,4,128]{2,1,0:T(4,128)}, u32[]{:S(2)}) copy-start(f32[512,4,128]{2,1,0:T(4,128)} %copy-done) | copy-start | bytes 3145732
  154.1 13.6 %all-to-all-start.5 = ((bf16[8,16,1024]{2,1,0:T(8,128)(2,1)}), bf16[8,16,1024]{2,1,0:T(8,128)(2,1)S(1)}, u32[]{:S(2)}, u32[]{:S(2)}) async-start(bf16[8,16,1024]{2,1,0:T(8,128)(2,1)} %bitcast.8), calls=%async_computation.5 | async-start | bytes 524288 | tf_op jit(solution)/shard_map/all_to_all | solution.py:45
  157.6 2.7 %copy-start.2 = (f32[512,1024]{1,0:T(8,128)S(1)}, f32[512,1024]{1,0:T(8,128)}, u32[]{:S(2)}) copy-start(f32[512,1024]{1,0:T(8,128)} %convolution_add_fusion) | copy-start | bytes 6291460
  160.3 7.4 %copy-start.9 = (bf16[16,512]{1,0:T(8,128)(2,1)S(1)}, bf16[16,512]{1,0:T(8,128)(2,1)}, u32[]{:S(2)}) copy-start(bf16[16,512]{1,0:T(8,128)(2,1)} %param.9) | copy-start | bytes 49156

commit v2 on v1

v2 whole, which is shorter than its diff:
```python
import jax
import jax.numpy as jnp
from jax import lax
from jax.experimental import pallas as pl
from jax.experimental.pallas import tpu as pltpu
from jax.sharding import Mesh, PartitionSpec as P

D = 8192
TILE = 128
ROW = ("z", "core")
COL = ("x", "y")
N_Z, N_CORE, N_X, N_Y = 8, 2, 4, 8
N_ROW = N_Z * N_CORE
N_COL = N_X * N_Y


clip_ratio = 1.5


def expand(mask):
    return jnp.repeat(jnp.repeat(mask, TILE, axis=0), TILE, axis=1).astype(jnp.float32)


def matmul(left, right):
    return jnp.dot(left, right, preferred_element_type=jnp.float32)


def contract_last(left, right):
    return lax.dot_general(
        left, right, (((1,), (1,)), ((), ())), preferred_element_type=jnp.float32
    )


def contract_first(left, right):
    return lax.dot_general(
        left, right, (((0,), (0,)), ((), ())), preferred_element_type=jnp.float32
    )


def swap_cores(block):
    return lax.ppermute(block, "core", [(0, 1), (1, 0)])


def exchange(parts, axis):
    return lax.all_to_all(parts, axis, 0, 0, tiled=True)


def add_parts(parts):
    total = parts[0].astype(jnp.float32)
    for i in range(1, parts.shape[0]):
        total = total + parts[i].astype(jnp.float32)
    return total


def local_kernel(body, outs, args, scalars=0, flops=0):
    moved = sum(a.size * a.dtype.itemsize for a in list(args) + list(outs))
    many = len(outs) > 1
    return pl.pallas_call(
        body,
        out_shape=outs if many else outs[0],
        in_specs=[pl.BlockSpec(memory_space=pltpu.SMEM)] * scalars
        + [pl.BlockSpec(memory_space=pltpu.VMEM)] * (len(args) - scalars),
        out_specs=[pl.BlockSpec(memory_space=pltpu.VMEM)] * len(outs)
        if many
        else pl.BlockSpec(memory_space=pltpu.VMEM),
        compiler_params=pltpu.CompilerParams(vmem_limit_bytes=24 << 20),
        cost_estimate=pl.CostEstimate(flops=flops, transcendentals=0, bytes_accessed=moved),
    )(*args)


def shape(dims, dtype):
    return jax.ShapeDtypeStruct(dims, dtype)


def squares_kernel(tokens, scales, copies):
    smoothed = tokens[...].astype(jnp.float32) / scales[...]
    squares = smoothed * smoothed
    lanes = copies.shape[2]
    total = squares[:, :lanes]
    for start in range(lanes, squares.shape[1], lanes):
        total = total + squares[:, start : start + lanes]
    for i in range(copies.shape[0]):
        copies[i] = total


def quantize_kernel(squares, tokens, scales, cotangent, copies, slope):
    width = tokens.shape[1]
    mean_square = jnp.sum(add_parts(squares), axis=1, keepdims=True) / D
    limits = clip_ratio * jnp.sqrt(mean_square + 1e-06)
    squashed = jnp.tanh(tokens[...].astype(jnp.float32) / scales[...] / limits)
    quantized = (limits * squashed).astype(jnp.bfloat16)
    slope[...] = (1.0 - squashed * squashed) / scales[...]
    for i in range(copies.shape[0]):
        copies[i, :, :width] = quantized
        copies[i, :, width:] = cotangent[...]


def forward_kernel(half, both_in, both_kept, down_kept, sums):
    rows = sums.shape[0]
    width = both_kept.shape[0]
    split = both_kept.shape[1]
    picked = pl.ds(pl.multiple_of(half[0] * rows, rows), rows)
    sums[:, :split] = matmul(both_in[picked, :width], both_kept[...]).astype(sums.dtype)
    sums[:, split:] = contract_last(both_in[picked, width:], down_kept[...]).astype(sums.dtype)


def pair_kernel(own, theirs, sums):
    sums[...] = (own[...] + theirs[...].astype(jnp.float32)).astype(sums.dtype)


def swiglu_kernel(parts, copies):
    pre = add_parts(parts)
    width = pre.shape[1] // 3
    gate_pre = pre[:, :width]
    up_pre = pre[:, width : 2 * width]
    hidden_grad = pre[:, 2 * width :]
    sigmoid_gate = 1.0 / (1.0 + jnp.exp(-gate_pre))
    silu_gate = gate_pre * sigmoid_gate
    gate_dir = hidden_grad * up_pre * sigmoid_gate * (1.0 + gate_pre * (1.0 - sigmoid_gate))
    up_dir = hidden_grad * silu_gate
    hidden = silu_gate * up_pre
    for k, value in enumerate((gate_dir, up_dir, hidden)):
        rounded = value.astype(copies.dtype)
        for i in range(copies.shape[0]):
            copies[i, :, k * width : (k + 1) * width] = rounded


def back_sums(mid, both_kept, down_kept, store):
    split = both_kept.shape[1]
    store(0, matmul(mid[:, split:], down_kept[...]))
    store(1, contract_last(mid[:, :split], both_kept[...]))


def own_back_kernel(mid, both_kept, down_kept, back):
    width = back.shape[1] // 2

    def store(k, value):
        back[:, k * width : (k + 1) * width] = value.astype(back.dtype)

    back_sums(mid, both_kept, down_kept, store)


def other_back_kernel(core, mid, own, both_kept, down_kept, back):
    rows = own.shape[0]
    width = back.shape[1] // 2
    own_rows = pl.ds(pl.multiple_of(core[0] * rows, rows), rows)
    other_rows = pl.ds(pl.multiple_of((1 - core[0]) * rows, rows), rows)
    back[own_rows, :] = own[...]

    def store(k, value):
        back[other_rows, k * width : (k + 1) * width] = value.astype(back.dtype)

    back_sums(mid, both_kept, down_kept, store)


def add_kernel(parts, total):
    total[...] = add_parts(parts).astype(total.dtype)


def finish_kernel(parts, slope, output, input_grad):
    total = add_parts(parts)
    width = output.shape[1]
    output[...] = total[:, :width].astype(output.dtype)
    input_grad[...] = (total[:, width:] * slope[...]).astype(input_grad.dtype)


def per_device(
    tokens, scales, gate_weight, up_weight, down_weight, gate_mask, up_mask, down_mask, cotangent
):
    hidden_width = gate_weight.shape[1]
    own_tokens, width = tokens.shape
    all_tokens = own_tokens * N_COL
    half_tokens = all_tokens // N_CORE
    mid_tokens = half_tokens // N_Z
    bf16, f32 = jnp.bfloat16, jnp.float32
    core = lax.axis_index("core").astype(jnp.int32).reshape(1)
    gate_keep = expand(gate_mask)
    up_keep = expand(up_mask)
    down_keep = expand(down_mask)
    gate_kept = (scales[:, None] * gate_weight.astype(jnp.float32) * gate_keep).astype(jnp.bfloat16)
    up_kept = (scales[:, None] * up_weight.astype(jnp.float32) * up_keep).astype(jnp.bfloat16)
    down_kept = down_weight * down_keep.astype(jnp.bfloat16)
    both_kept = jnp.concatenate([gate_kept, up_kept], axis=1)
    scale_row = scales[None, :]

    squares = local_kernel(
        squares_kernel, [shape((N_ROW, own_tokens, TILE), f32)], [tokens, scale_row]
    )
    squares = exchange(squares, ROW)
    copies, slope = local_kernel(
        quantize_kernel,
        [shape((N_Y, own_tokens, 2 * width), bf16), shape((own_tokens, width), f32)],
        [squares, tokens, scale_row, cotangent],
    )
    both_in = exchange(copies, "y").reshape(1, N_Y * own_tokens, 2 * width)
    both_in = exchange(jnp.broadcast_to(both_in, (N_X,) + both_in.shape[1:]), "x")
    both_in = both_in.reshape(all_tokens, 2 * width)

    flops = 6 * half_tokens * width * hidden_width
    theirs = local_kernel(
        forward_kernel,
        [shape((half_tokens, 3 * hidden_width), bf16)],
        [1 - core, both_in, both_kept, down_kept],
        1,
        flops,
    )
    theirs = swap_cores(theirs)
    own = local_kernel(
        forward_kernel,
        [shape((half_tokens, 3 * hidden_width), f32)],
        [core, both_in, both_kept, down_kept],
        1,
        flops,
    )
    pair_sum = local_kernel(
        pair_kernel, [shape((half_tokens, 3 * hidden_width), bf16)], [own, theirs]
    )
    parts = exchange(pair_sum.reshape(N_Z, mid_tokens, -1), "z")
    mid = local_kernel(swiglu_kernel, [shape(parts.shape, bf16)], [parts])
    own_mid = exchange(mid, "z").reshape(half_tokens, -1)
    other_mid = swap_cores(own_mid)
    own_back = local_kernel(
        own_back_kernel,
        [shape((half_tokens, 2 * width), bf16)],
        [own_mid, both_kept, down_kept],
        0,
        flops,
    )
    back = local_kernel(
        other_back_kernel,
        [shape((all_tokens, 2 * width), bf16)],
        [core, other_mid, own_back, both_kept, down_kept],
        1,
        flops,
    )
    back = exchange(back.reshape(N_X, all_tokens // N_X, -1), "x")
    back = local_kernel(add_kernel, [shape(back.shape[1:], bf16)], [back])
    back = exchange(back.reshape(N_Y, own_tokens, -1), "y")
    output, input_grad = local_kernel(
        finish_kernel, [shape((own_tokens, width), bf16)] * 2, [back, slope]
    )

    own_in = lax.dynamic_slice_in_dim(both_in, core[0] * half_tokens, half_tokens, 0)
    other_in = lax.dynamic_slice_in_dim(both_in, (1 - core[0]) * half_tokens, half_tokens, 0)
    weight_product = contract_first(
        own_in[:, :width], own_mid[:, : 2 * hidden_width]
    ) + contract_first(other_in[:, :width], other_mid[:, : 2 * hidden_width])
    down_product = contract_first(own_mid[:, 2 * hidden_width :], own_in[:, width:]) + (
        contract_first(other_mid[:, 2 * hidden_width :], other_in[:, width:])
    )
    gate_grad = (scales[:, None] * weight_product[:, :hidden_width] * gate_keep).astype(
        jnp.bfloat16
    )
    up_grad = (scales[:, None] * weight_product[:, hidden_width:] * up_keep).astype(jnp.bfloat16)
    down_grad = (down_product * down_keep).astype(jnp.bfloat16)
    return (output, input_grad, gate_grad, up_grad, down_grad)


def solution(mesh):
    fine = Mesh(mesh.devices.reshape(N_Z, N_CORE, N_X, N_Y), ROW + COL)
    placed = (
        P(COL, ROW),
        P(ROW),
        P(ROW, COL),
        P(ROW, COL),
        P(COL, ROW),
        P(ROW, COL),
        P(ROW, COL),
        P(COL, ROW),
        P(COL, ROW),
    )
    return jax.shard_map(
        per_device,
        mesh=fine,
        in_specs=placed,
        out_specs=(
            P(COL, ROW),
            P(COL, ROW),
            P(ROW, COL),
            P(ROW, COL),
            P(COL, ROW),
        ),
        check_vma=False,
    )
```

time: 171 us -> 164 us (0.959)
  blocking collectives: 70.6 us -> 91.7 us
  matrix products: 19.9 us -> 7.4 us
  starting transfers between devices: 27 us -> 17.1 us
  other arithmetic: 10.8 us -> 3.3 us
  waiting for transfers between devices: 35 us -> 27.6 us
  Pallas kernels: 0 us -> 5.39 us
  local copies, waits for them, and re-layouts: 4.69 us -> 9.12 us
    all_to_all x3 -> x4, blocking collectives: 70.6 us -> 91.7 us  [exchange(): return lax.all_to_all(parts, axis, 0, 0, tiled=True)]
    dot_general x8 -> x0, matrix products: 10.7 us -> none  [the longest x4 5.83 us: contract_last(): lax.dot_general(left, right, (((1,), (1,)), ((), ())), preferred_element_...]
    all_to_all x3, waiting for transfers between devices: 35 us -> 24.9 us  [exchange(): return lax.all_to_all(parts, axis, 0, 0, tiled=True)]
    all_to_all x3, starting transfers between devices: 17.7 us -> 11.1 us  [exchange(): return lax.all_to_all(parts, axis, 0, 0, tiled=True)]
    pallas_call x0 -> x10, Pallas kernels: none -> 5.39 us  [local_kernel(): pl.pallas_call(body, out_shape=outs if many else outs[0], in_specs=[pl.Bl...]
    unnamed x28 -> x36, local copies, waits for them, and re-layouts: 1.05 us -> 6.14 us
    ppermute x2, starting transfers between devices: 9.3 us -> 5.98 us  [swap_cores(): return lax.ppermute(block, 'core', [(0, 1), (1, 0)])]
    reduce_sum x5 -> x0, other arithmetic: 3.21 us -> none  [the longest x3 2.34 us: exchange_sum(): return jnp.sum(parts.astype(jnp.float32), axis=0)]
  transfers between devices with their start and end apart: 5 -> 5, of which waited for: 3 -> 5; matrix products, arithmetic and copies ran while one was open for 11% -> 8% of each run, Pallas kernels for 0% -> 1%
where the time goes in v2:
time: 164 us; the launch traced here: 163 us
  blocking collectives  91.7 us (56%)
  waiting for transfers between devices  27.6 us (17%)
  starting transfers between devices  17.1 us (10%)
  local copies, waits for them, and re-layouts  9.12 us (6%)
  matrix products  7.4 us (5%)
  Pallas kernels  5.39 us (3%)
  other arithmetic  3.3 us (2%)
    all_to_all x4, blocking collectives, exchange(): return lax.all_to_all(parts, axis, 0, 0, tiled=True)  91.7 us
    all_to_all x3, waiting for transfers between devices, exchange(): return lax.all_to_all(parts, axis, 0, 0, tiled=True)  24.9 us
    all_to_all x3, starting transfers between devices, exchange(): return lax.all_to_all(parts, axis, 0, 0, tiled=True)  11.1 us
    dot_general x4, matrix products, contract_first(): lax.dot_general(left, right, (((0,), (0,)), ((), ())), preferred_element_...  7.4 us
    unnamed x36, local copies, waits for them, and re-layouts  6.14 us
    ppermute x2, starting transfers between devices, swap_cores(): return lax.ppermute(block, 'core', [(0, 1), (1, 0)])  5.98 us
    pallas_call x10, Pallas kernels, local_kernel(): pl.pallas_call(body, out_shape=outs if many else outs[0], in_specs=[pl.Bl...  5.39 us
  transfers between devices with their start and end apart: 5, of which 5 were waited for; matrix products, arithmetic and copies ran while one was open for 8% of the time, Pallas kernels for 1%

profile of v2, /device:TPU:1, one launch (start us, length us, event | category | flops | bytes accessed | tf_op | source)
XLA Modules:
  0.0 162.5 jit_solution(1818630206515316759)
XLA Ops:
  0.6 0.7 copy-done.1
  1.4 0.7 copy-done.3
  2.1 20.8 %all_to_all.35.squares = f32[16,16,128]{2,1,0:T(8,128)S(1)} all-to-all(f32[16,16,128]{2,1,0:T(8,128)S(1)} %shard_map.128), channel_id=1, replica_groups=mesh['z'=8,'core'=2,'x'=4,'y'=8] {'z','core'}, dimensions={0} | all-to-all | bytes 262144 | tf_op jit(solution)/shard_map/all_to_all | solution.py:45
  22.9 0.7 copy-done.2
  23.6 0.7 copy-done.4
  24.3 0.7 copy-done.6
  25.1 19.0 %all_to_all.36 = bf16[8,16,1024]{2,1,0:T(8,128)(2,1)S(1)} all-to-all(bf16[8,16,1024]{2,1,0:T(8,128)(2,1)S(1)} %get-tuple-element.9), channel_id=1, replica_groups=mesh['z'=8,'core'=2,'x'=4,'y'=8] {'y'}, dimensions={0} | all-to-all | bytes 524288 | tf_op jit(solution)/shard_map/all_to_all | solution.py:45
  44.1 1.1 broadcast_in_dim.34
  45.2 4.0 %all-to-all-start.2 = ((bf16[4,128,1024]{2,1,0:T(8,128)(2,1)}), bf16[4,128,1024]{2,1,0:T(8,128)(2,1)S(1)}, u32[]{:S(2)}, u32[]{:S(2)}) async-start(bf16[4,128,1024]{2,1,0:T(8,128)(2,1)} %broadcast_in_dim.34), calls=%async_computation.2 | async-start | bytes 2097152 | tf_op jit(solution)/shard_map/all_to_all | solution.py:45
  49.4 0.6 broadcast_in_dim.36
  51.0 0.6 copy-done.9
  51.8 0.6 broadcast_in_dim.40
  52.4 1.0 copy-done.11
  53.5 10.2 %all-to-all-done.2 = bf16[4,128,1024]{2,1,0:T(8,128)(2,1)S(1)} async-done(((bf16[4,128,1024]{2,1,0:T(8,128)(2,1)}), bf16[4,128,1024]{2,1,0:T(8,128)(2,1)S(1)}, u32[]{:S(2)}, u32[]{:S(2)}) %all-to-all-start.2) | async-done | bytes 1048608 | tf_op jit(solution)/shard_map/all_to_all | solution.py:45
  64.3 3.5 %collective-permute-start = (bf16[256,1536]{1,0:T(8,128)(2,1)S(1)}, bf16[256,1536]{1,0:T(8,128)(2,1)S(1)}, u32[]{:S(2)}, u32[]{:S(2)}) collective-permute-start(bf16[256,1536]{1,0:T(8,128)(2,1)S(1)} %shard_map.131), channel_id=1, source_target_pairs={{0,32},{32,0},{1,33},{33,1},{2,34},{34,2},{3,35},{35,3},{4,36},{36... | collective-permute-start | bytes 2359304 | tf_op jit(solution)/shard_map/ppermute | solution.py:41
  68.4 1.3 collective-permute-done.theirs
  69.8 26.0 %all_to_all.37.parts = bf16[8,32,1536]{2,1,0:T(8,128)(2,1)S(1)} all-to-all(bf16[8,32,1536]{2,1,0:T(8,128)(2,1)S(1)} %bitcast.44), channel_id=1, replica_groups=mesh['z'=8,'core'=2,'x'=4,'y'=8] {'z'}, dimensions={0} | all-to-all | bytes 1572864 | tf_op jit(solution)/shard_map/all_to_all | solution.py:45
  96.0 25.9 %all_to_all.38 = bf16[8,32,1536]{2,1,0:T(8,128)(2,1)S(1)} all-to-all(bf16[8,32,1536]{2,1,0:T(8,128)(2,1)S(1)} %shard_map.133), channel_id=1, replica_groups=mesh['z'=8,'core'=2,'x'=4,'y'=8] {'z'}, dimensions={0} | all-to-all | bytes 1572864 | tf_op jit(solution)/shard_map/all_to_all | solution.py:45
  121.9 2.5 %collective-permute-start.1 = (bf16[256,1536]{1,0:T(8,128)(2,1)S(1)}, bf16[256,1536]{1,0:T(8,128)(2,1)}, u32[]{:S(2)}, u32[]{:S(2)}) collective-permute-start(bf16[256,1536]{1,0:T(8,128)(2,1)S(1)} %bitcast.39), channel_id=1, source_target_pairs={{0,32},{32,0},{1,33},{33,1},{2,34},{34,2},{3,35},{35,3},{4,36},{36... | collective-permute-start | bytes 2359304 | tf_op jit(solution)/shard_map/ppermute | solution.py:41
  125.0 1.4 collective-permute-done.1.mid
  126.4 1.7 %shard_map.135 = bf16[512,1024]{1,0:T(8,128)(2,1)S(1)} custom-call(s32[1]{0:T(128)} %bitcast.half.core, bf16[256,1536]{1,0:T(8,128)(2,1)} %collective-permute-done.1.mid, bf16[256,1024]{1,0:T(8,128)(2,1)S(1)} %shard_map.134.own, bf16[512,1024]{1,0:T(8,128)(2,1)S(1)} %pad_maximum_fusion.both_kept, bf16[512,512]{1,0:T(8,128)(2,1)S(1)} %fusion.6.down_kept), custom_call_target="tpu_custom_call" | custom-call | flops 402653184 | bytes 3932164 | tf_op jit(solution)/shard_map/pallas_call | solution.py:58
  128.2 0.9 copy-done
  129.1 3.5 %all-to-all-start.5 = ((bf16[4,128,1024]{2,1,0:T(8,128)(2,1)}), bf16[4,128,1024]{2,1,0:T(8,128)(2,1)S(1)}, u32[]{:S(2)}, u32[]{:S(2)}) async-start(bf16[4,128,1024]{2,1,0:T(8,128)(2,1)} %bitcast.43), calls=%async_computation.5 | async-start | bytes 2097152 | tf_op jit(solution)/shard_map/all_to_all | solution.py:45
  132.6 1.3 fusion.12
  134.4 2.9 %convolution_add_fusion = f32[512,1024]{1,0:T(8,128)} fusion(f32[512,1024]{1,0:T(8,128)S(1)} %fusion.8, bf16[256,1536]{1,0:T(8,128)(2,1)} %collective-permute-done.1.mid, bf16[512,1024]{1,0:T(8,128)(2,1)S(1)} %bitcast.37, s32[]{:T(128)S(6)} %select_n.7), kind=kOutput, calls=%fused_computation | convolution fusion | flops 268959744 | bytes 4980740 | tf_op jit(solution)/shard_map/dot_general | solution.py:35
  137.3 10.1 %all-to-all-done.5.parts = bf16[4,128,1024]{2,1,0:T(8,128)(2,1)S(1)} async-done(((bf16[4,128,1024]{2,1,0:T(8,128)(2,1)}), bf16[4,128,1024]{2,1,0:T(8,128)(2,1)S(1)}, u32[]{:S(2)}, u32[]{:S(2)}) %all-to-all-start.5) | async-done | bytes 1048608 | tf_op jit(solution)/shard_map/all_to_all | solution.py:45
  147.4 0.8 shard_map.136
  148.3 3.5 %all-to-all-start.6 = ((bf16[8,16,1024]{2,1,0:T(8,128)(2,1)}), bf16[8,16,1024]{2,1,0:T(8,128)(2,1)S(1)}, u32[]{:S(2)}, u32[]{:S(2)}) async-start(bf16[8,16,1024]{2,1,0:T(8,128)(2,1)} %bitcast.10), calls=%async_computation.6 | async-start | bytes 524288 | tf_op jit(solution)/shard_map/all_to_all | solution.py:45
  151.8 2.8 %fusion.1 = bf16[512,512]{1,0:T(8,128)(2,1)} fusion(f32[512,512]{1,0:T(8,128)} %fusion.12, f32[64,8,4,128]{3,2,1,0:T(4,128)} %bitcast.52, bf16[512,1024]{1,0:T(8,128)(2,1)S(1)} %bitcast.38, s32[]{:T(128)S(6)} %select_n.7, s32[]{:T(128)S(6)} %add.16, bf16[256,1536]{1,0:T(8,128)(2,1)} %collective-permute-done.1.mid), kind=kOutput, calls=%fused_computation.3 | convolution fusion | flops 135004160 | bytes 3145736 | tf_op jit(solution)/shard_map/dot_general | solution.py:35
  154.6 2.8 %fusion.3 = (bf16[512,512]{1,0:T(8,128)(2,1)}, bf16[512,512]{1,0:T(8,128)(2,1)}) fusion(f32[512,1024]{1,0:T(8,128)} %convolution_add_fusion, f32[64,8,4,128]{3,2,1,0:T(4,128)S(1)} %bitcast.50, f32[512]{0:T(512)S(1)} %copy-done.5, f32[64,8,4,128]{3,2,1,0:T(4,128)S(1)} %bitcast.48), kind=kLoop, calls=%fused_computation.8 | loop fusion | flops 1572864 | bytes 5244928 | tf_op jit(solution)/shard_map/convert_element_type | solution.py:254
  157.4 4.5 %all-to-all-done.6.parts = bf16[8,16,1024]{2,1,0:T(8,128)(2,1)S(1)} async-done(((bf16[8,16,1024]{2,1,0:T(8,128)(2,1)}), bf16[8,16,1024]{2,1,0:T(8,128)(2,1)S(1)}, u32[]{:S(2)}, u32[]{:S(2)}) %all-to-all-start.6) | async-done | bytes 262176 | tf_op jit(solution)/shard_map/all_to_all | solution.py:45
  161.9 0.6 shard_map.137
  (46 shorter events, 3.9 us)
Async XLA Ops:
  0.6 0.7 copy-start.1
  1.4 0.7 copy-start.3
  22.9 0.7 copy-start.2
  23.6 0.7 copy-start.4
  24.3 0.7 copy-start.6
  25.0 24.3 %copy-start.15 = (s32[4,4]{1,0:T(4,128)S(1)}, s32[4,4]{1,0:T(4,128)}, u32[]{:S(2)}) copy-start(s32[4,4]{1,0:T(4,128)} %param.14) | copy-start | bytes 196
  25.0 24.3 %copy-start.16 = (s32[4,4]{1,0:T(4,128)S(1)}, s32[4,4]{1,0:T(4,128)}, u32[]{:S(2)}) copy-start(s32[4,4]{1,0:T(4,128)} %param.15) | copy-start | bytes 196
  25.0 24.3 %copy-start.17 = (s32[4,4]{1,0:T(4,128)S(1)}, s32[4,4]{1,0:T(4,128)}, u32[]{:S(2)}) copy-start(s32[4,4]{1,0:T(4,128)} %param.16) | copy-start | bytes 196
  45.2 18.5 %all-to-all-start.2 = ((bf16[4,128,1024]{2,1,0:T(8,128)(2,1)}), bf16[4,128,1024]{2,1,0:T(8,128)(2,1)S(1)}, u32[]{:S(2)}, u32[]{:S(2)}) async-start(bf16[4,128,1024]{2,1,0:T(8,128)(2,1)} %broadcast_in_dim.34), calls=%async_computation.2 | async-start | bytes 2097152 | tf_op jit(solution)/shard_map/all_to_all | solution.py:45
  49.3 1.4 copy-start.5
  49.3 1.4 copy-start.13
  49.3 1.4 copy-start.14
  50.0 1.0 copy-start.7
  50.6 1.0 copy-start.9
  51.6 1.8 %copy-start.12 = (bf16[512,512]{1,0:T(8,128)(2,1)S(1)}, bf16[512,512]{1,0:T(8,128)(2,1)}, u32[]{:S(2)}) copy-start(bf16[512,512]{1,0:T(8,128)(2,1)} %param.13) | copy-start | bytes 1572868
  52.4 1.0 copy-start.11
  64.3 5.4 %collective-permute-start = (bf16[256,1536]{1,0:T(8,128)(2,1)S(1)}, bf16[256,1536]{1,0:T(8,128)(2,1)S(1)}, u32[]{:S(2)}, u32[]{:S(2)}) collective-permute-start(bf16[256,1536]{1,0:T(8,128)(2,1)S(1)} %shard_map.131), channel_id=1, source_target_pairs={{0,32},{32,0},{1,33},{33,1},{2,34},{34,2},{3,35},{35,3},{4,36},{36... | collective-permute-start | bytes 2359304 | tf_op jit(solution)/shard_map/ppermute | solution.py:41
  121.9 4.5 %collective-permute-start.1 = (bf16[256,1536]{1,0:T(8,128)(2,1)S(1)}, bf16[256,1536]{1,0:T(8,128)(2,1)}, u32[]{:S(2)}, u32[]{:S(2)}) collective-permute-start(bf16[256,1536]{1,0:T(8,128)(2,1)S(1)} %bitcast.39), channel_id=1, source_target_pairs={{0,32},{32,0},{1,33},{33,1},{2,34},{34,2},{3,35},{35,3},{4,36},{36... | collective-permute-start | bytes 2359304 | tf_op jit(solution)/shard_map/ppermute | solution.py:41
  128.2 1.0 copy-start
  129.1 18.3 %all-to-all-start.5 = ((bf16[4,128,1024]{2,1,0:T(8,128)(2,1)}), bf16[4,128,1024]{2,1,0:T(8,128)(2,1)S(1)}, u32[]{:S(2)}, u32[]{:S(2)}) async-start(bf16[4,128,1024]{2,1,0:T(8,128)(2,1)} %bitcast.43), calls=%async_computation.5 | async-start | bytes 2097152 | tf_op jit(solution)/shard_map/all_to_all | solution.py:45
  148.3 6.3 %copy-start.8 = (f32[512,4,128]{2,1,0:T(4,128)S(1)}, f32[512,4,128]{2,1,0:T(4,128)}, u32[]{:S(2)}) copy-start(f32[512,4,128]{2,1,0:T(4,128)} %copy-done.7) | copy-start | bytes 3145732
  148.3 6.3 %copy-start.10 = (f32[512,4,128]{2,1,0:T(4,128)S(1)}, f32[512,4,128]{2,1,0:T(4,128)}, u32[]{:S(2)}) copy-start(f32[512,4,128]{2,1,0:T(4,128)} %copy-done.9) | copy-start | bytes 3145732
  148.3 13.6 %all-to-all-start.6 = ((bf16[8,16,1024]{2,1,0:T(8,128)(2,1)}), bf16[8,16,1024]{2,1,0:T(8,128)(2,1)S(1)}, u32[]{:S(2)}, u32[]{:S(2)}) async-start(bf16[8,16,1024]{2,1,0:T(8,128)(2,1)} %bitcast.10), calls=%async_computation.6 | async-start | bytes 524288 | tf_op jit(solution)/shard_map/all_to_all | solution.py:45

commit v3 on v2

v3 whole, which is shorter than its diff:
```python
import functools

import jax
import jax.numpy as jnp
from jax import lax
from jax.experimental import pallas as pl
from jax.experimental.pallas import tpu as pltpu
from jax.sharding import Mesh, PartitionSpec as P

D = 8192
TILE = 128
ROW = ("z", "core")
COL = ("x", "y")
N_Z, N_CORE, N_X, N_Y = 8, 2, 4, 8
N_ROW = N_Z * N_CORE
N_COL = N_X * N_Y


clip_ratio = 1.5


def matmul(left, right):
    return jnp.dot(left, right, preferred_element_type=jnp.float32)


def contract_last(left, right):
    return lax.dot_general(
        left, right, (((1,), (1,)), ((), ())), preferred_element_type=jnp.float32
    )


def contract_first(left, right):
    return lax.dot_general(
        left, right, (((0,), (0,)), ((), ())), preferred_element_type=jnp.float32
    )


def swap_cores(block):
    return lax.ppermute(block, "core", [(0, 1), (1, 0)])


def exchange(parts, axis):
    return lax.all_to_all(parts, axis, 0, 0, tiled=True)


def add_parts(parts):
    total = parts[0].astype(jnp.float32)
    for i in range(1, parts.shape[0]):
        total = total + parts[i].astype(jnp.float32)
    return total


def local_kernel(body, outs, args, scalars=0, flops=0, apart=(), stored=(), scratch=(), room=32):
    moved = sum(a.size * a.dtype.itemsize for a in list(args) + list(outs))
    spaces = [pltpu.SMEM if i < scalars else pltpu.VMEM for i in range(len(args))]
    for i in apart:
        spaces[i] = pl.ANY
    for i in stored:
        spaces[i] = pltpu.HBM
    specs = [pl.BlockSpec(memory_space=pltpu.VMEM)] * len(outs)
    return pl.pallas_call(
        body,
        out_shape=outs if len(outs) > 1 else outs[0],
        in_specs=[pl.BlockSpec(memory_space=space) for space in spaces],
        out_specs=specs if len(outs) > 1 else specs[0],
        scratch_shapes=list(scratch),
        compiler_params=pltpu.CompilerParams(vmem_limit_bytes=room << 20),
        cost_estimate=pl.CostEstimate(flops=flops, transcendentals=0, bytes_accessed=moved),
    )(*args)


def shape(dims, dtype):
    return jax.ShapeDtypeStruct(dims, dtype)


def squares_kernel(
    core, tokens, scales, cotangent, copies, smoothed, scales_here, cotangent_here, tokens_here, arrived
):
    del core
    moves = [
        pltpu.make_async_copy(tokens, tokens_here, arrived.at[0]),
        pltpu.make_async_copy(scales, scales_here, arrived.at[1]),
        pltpu.make_async_copy(cotangent, cotangent_here, arrived.at[2]),
    ]
    for move in moves:
        move.start()
    for move in moves:
        move.wait()
    value = tokens_here[...].astype(jnp.float32) / scales_here[...]
    smoothed[...] = value
    squares = value * value
    lanes = copies.shape[2]
    total = squares[:, :lanes]
    for start in range(lanes, squares.shape[1], lanes):
        total = total + squares[:, start : start + lanes]
    for i in range(copies.shape[0]):
        copies[i] = total


def prepare_kernel(
    gate_mask, up_mask, down_mask, scales, gate, up, down, both_kept, down_kept
):
    width = gate.shape[1]
    for i in range(gate.shape[0] // TILE):
        rows = slice(i * TILE, (i + 1) * TILE)
        scale = scales[rows, :]
        for j in range(width // TILE):
            columns = slice(j * TILE, (j + 1) * TILE)
            shifted = slice(width + j * TILE, width + (j + 1) * TILE)
            gate_keep = gate_mask[i, j].astype(jnp.float32)
            up_keep = up_mask[i, j].astype(jnp.float32)
            down_keep = down_mask[i, j].astype(jnp.float32)
            both_kept[rows, columns] = (
                scale * gate[rows, columns].astype(jnp.float32) * gate_keep
            ).astype(both_kept.dtype)
            both_kept[rows, shifted] = (
                scale * up[rows, columns].astype(jnp.float32) * up_keep
            ).astype(both_kept.dtype)
            down_kept[rows, columns] = (
                down[rows, columns].astype(jnp.float32) * down_keep
            ).astype(down_kept.dtype)


def quantize_kernel(squares, smoothed, scales, cotangent, both_kept, down_kept, copies, slope):
    del both_kept, down_kept
    width = smoothed.shape[1]
    mean_square = jnp.sum(add_parts(squares), axis=1, keepdims=True) / D
    limits = clip_ratio * jnp.sqrt(mean_square + 1e-06)
    squashed = jnp.tanh(smoothed[...] / limits)
    quantized = (limits * squashed).astype(jnp.bfloat16)
    slope[...] = (1.0 - squashed * squashed) / scales[...]
    for i in range(copies.shape[0]):
        copies[i, :, :width] = quantized
        copies[i, :, width:] = cotangent[...]


def forward_kernel(other, core, both_in, both_kept, down_kept, sums):
    rows = sums.shape[0]
    width = both_kept.shape[0]
    split = both_kept.shape[1]
    half = 1 - core[0] if other else core[0]
    picked = pl.ds(pl.multiple_of(half * rows, rows), rows)
    sums[:, :split] = matmul(both_in[picked, :width], both_kept[...]).astype(sums.dtype)
    sums[:, split:] = contract_last(both_in[picked, width:], down_kept[...]).astype(sums.dtype)


def pair_kernel(own, theirs, sums):
    sums[...] = (own[...] + theirs[...].astype(jnp.float32)).astype(sums.dtype)


def swiglu_kernel(parts, copies):
    pre = add_parts(parts)
    width = pre.shape[1] // 3
    gate_pre = pre[:, :width]
    up_pre = pre[:, width : 2 * width]
    hidden_grad = pre[:, 2 * width :]
    sigmoid_gate = 1.0 / (1.0 + jnp.exp(-gate_pre))
    silu_gate = gate_pre * sigmoid_gate
    gate_dir = hidden_grad * up_pre * sigmoid_gate * (1.0 + gate_pre * (1.0 - sigmoid_gate))
    up_dir = hidden_grad * silu_gate
    hidden = silu_gate * up_pre
    for k, value in enumerate((gate_dir, up_dir, hidden)):
        rounded = value.astype(copies.dtype)
        for i in range(copies.shape[0]):
            copies[i, :, k * width : (k + 1) * width] = rounded


def back_sums(mid, both_kept, down_kept, store):
    split = both_kept.shape[1]
    store(0, matmul(mid[:, split:], down_kept[...]))
    store(1, contract_last(mid[:, :split], both_kept[...]))


def own_back_kernel(mid, both_kept, down_kept, back):
    width = back.shape[1] // 2

    def store(k, value):
        back[:, k * width : (k + 1) * width] = value.astype(back.dtype)

    back_sums(mid, both_kept, down_kept, store)


def other_back_kernel(
    core,
    gate_mask,
    up_mask,
    down_mask,
    both_in,
    own_mid,
    other_mid,
    own,
    both_kept,
    down_kept,
    scales,
    back,
    gate_grad,
    up_grad,
    down_grad,
):
    rows = own.shape[0]
    width = back.shape[1] // 2
    split = both_kept.shape[1]
    own_rows = pl.ds(pl.multiple_of(core[0] * rows, rows), rows)
    other_rows = pl.ds(pl.multiple_of((1 - core[0]) * rows, rows), rows)
    back[own_rows, :] = own[...]

    def store(k, value):
        back[other_rows, k * width : (k + 1) * width] = value.astype(back.dtype)

    back_sums(other_mid, both_kept, down_kept, store)

    for i in range(width // TILE):
        block = slice(i * TILE, (i + 1) * TILE)
        product = contract_first(both_in[own_rows, block], own_mid[:, :split])
        product = product + contract_first(both_in[other_rows, block], other_mid[:, :split])
        for j in range(split // TILE):
            mask, grad = (gate_mask, gate_grad) if j < split // TILE // 2 else (up_mask, up_grad)
            column = j % (split // TILE // 2)
            tile = product[:, j * TILE : (j + 1) * TILE]
            keep = mask[i, column].astype(jnp.float32)
            grad[block, column * TILE : (column + 1) * TILE] = (
                scales[block, :] * tile * keep
            ).astype(grad.dtype)
    for i in range((other_mid.shape[1] - split) // TILE):
        units = slice(split + i * TILE, split + (i + 1) * TILE)
        product = contract_first(own_mid[:, units], both_in[own_rows, width:])
        product = product + contract_first(other_mid[:, units], both_in[other_rows, width:])
        for j in range(width // TILE):
            columns = slice(j * TILE, (j + 1) * TILE)
            keep = down_mask[i, j].astype(jnp.float32)
            down_grad[i * TILE : (i + 1) * TILE, columns] = (product[:, columns] * keep).astype(
                down_grad.dtype
            )


def finish_kernel(parts, slope, output, input_grad):
    total = add_parts(parts)
    width = output.shape[1]
    output[...] = total[:, :width].astype(output.dtype)
    input_grad[...] = (total[:, width:] * slope[...]).astype(input_grad.dtype)


def per_device(
    tokens, scales, gate_weight, up_weight, down_weight, gate_mask, up_mask, down_mask, cotangent
):
    hidden_width = gate_weight.shape[1]
    own_tokens, width = tokens.shape
    all_tokens = own_tokens * N_COL
    half_tokens = all_tokens // N_CORE
    mid_tokens = half_tokens // N_Z
    bf16, f32 = jnp.bfloat16, jnp.float32
    core = lax.axis_index("core").astype(jnp.int32).reshape(1)
    masks = [gate_mask, up_mask, down_mask]
    scale_lanes = jnp.broadcast_to(scales[:, None], (width, TILE))

    squares, smoothed, scales_here, cotangent_here = local_kernel(
        squares_kernel,
        [
            shape((N_ROW, own_tokens, TILE), f32),
            shape((own_tokens, width), f32),
            shape((1, width), f32),
            shape((own_tokens, width), bf16),
        ],
        [core, tokens, scales[None, :], cotangent],
        1,
        stored=(1, 2, 3),
        room=60,
        scratch=[pltpu.VMEM((own_tokens, width), bf16), pltpu.SemaphoreType.DMA((3,))],
    )
    squares = exchange(squares, ROW)
    both_kept, down_kept = local_kernel(
        prepare_kernel,
        [shape((width, 2 * hidden_width), bf16), shape((hidden_width, width), bf16)],
        masks + [scale_lanes, gate_weight, up_weight, down_weight],
        3,
    )
    copies, slope = local_kernel(
        quantize_kernel,
        [shape((N_COL, own_tokens, 2 * width), bf16), shape((own_tokens, width), f32)],
        [squares, smoothed, scales_here, cotangent_here, both_kept, down_kept],
        apart=(4, 5),
    )
    both_in = exchange(copies, COL).reshape(all_tokens, 2 * width)

    flops = 6 * half_tokens * width * hidden_width
    theirs = local_kernel(
        functools.partial(forward_kernel, True),
        [shape((half_tokens, 3 * hidden_width), bf16)],
        [core, both_in, both_kept, down_kept],
        1,
        flops,
    )
    theirs = swap_cores(theirs)
    own = local_kernel(
        functools.partial(forward_kernel, False),
        [shape((half_tokens, 3 * hidden_width), f32)],
        [core, both_in, both_kept, down_kept],
        1,
        flops,
    )
    pair_sum = local_kernel(
        pair_kernel, [shape((half_tokens, 3 * hidden_width), bf16)], [own, theirs]
    )
    parts = exchange(pair_sum.reshape(N_Z, mid_tokens, -1), "z")
    mid = local_kernel(swiglu_kernel, [shape(parts.shape, bf16)], [parts])
    own_mid = exchange(mid, "z").reshape(half_tokens, -1)
    other_mid = swap_cores(own_mid)
    own_back = local_kernel(
        own_back_kernel,
        [shape((half_tokens, 2 * width), bf16)],
        [own_mid, both_kept, down_kept],
        0,
        flops,
    )
    back, gate_grad, up_grad, down_grad = local_kernel(
        other_back_kernel,
        [
            shape((all_tokens, 2 * width), bf16),
            shape(gate_weight.shape, bf16),
            shape(up_weight.shape, bf16),
            shape(down_weight.shape, bf16),
        ],
        [core]
        + masks
        + [both_in, own_mid, other_mid, own_back, both_kept, down_kept, scale_lanes],
        4,
        4 * flops,
    )
    back = exchange(back.reshape(N_COL, own_tokens, -1), COL)
    output, input_grad = local_kernel(
        finish_kernel, [shape((own_tokens, width), bf16)] * 2, [back, slope]
    )
    return (output, input_grad, gate_grad, up_grad, down_grad)


def solution(mesh):
    fine = Mesh(mesh.devices.reshape(N_Z, N_CORE, N_X, N_Y), ROW + COL)
    placed = (
        P(COL, ROW),
        P(ROW),
        P(ROW, COL),
        P(ROW, COL),
        P(COL, ROW),
        P(ROW, COL),
        P(ROW, COL),
        P(COL, ROW),
        P(COL, ROW),
    )
    return jax.shard_map(
        per_device,
        mesh=fine,
        in_specs=placed,
        out_specs=(
            P(COL, ROW),
            P(COL, ROW),
            P(ROW, COL),
            P(ROW, COL),
            P(COL, ROW),
        ),
        check_vma=False,
    )
```

time: 164 us -> 161 us (0.982)
  the two profiles are of different devices: /device:TPU:1 before, /device:TPU:8 now
where the time goes in v3:
time: 161 us
  blocking collectives  126 us (78%)
  starting transfers between devices  14.5 us (9%)
  Pallas kernels  8.46 us (5%)
  local copies, waits for them, and re-layouts  6 us (4%)
  waiting for transfers between devices  5.03 us (3%)
    all_to_all x4, blocking collectives, exchange(): return lax.all_to_all(parts, axis, 0, 0, tiled=True)  126 us
    all_to_all x1, starting transfers between devices, exchange(): return lax.all_to_all(parts, axis, 0, 0, tiled=True)  10.6 us
    pallas_call x10, Pallas kernels, local_kernel(): pl.pallas_call(body, out_shape=outs if len(outs) > 1 else outs[0], in_spe...  8.46 us
    unnamed x24, local copies, waits for them, and re-layouts  5.19 us
    ppermute x2, starting transfers between devices, swap_cores(): return lax.ppermute(block, 'core', [(0, 1), (1, 0)])  3.96 us
    ppermute x2, waiting for transfers between devices, swap_cores(): return lax.ppermute(block, 'core', [(0, 1), (1, 0)])  3.35 us
  transfers between devices with their start and end apart: 3, of which 3 were waited for; matrix products, arithmetic and copies ran while one was open for 1% of the time, Pallas kernels for 1%

profile of v3, /device:TPU:8, one launch (start us, length us, event | category | flops | bytes accessed | tf_op | source)
XLA Modules:
  0.0 160.8 jit_solution(3878612339529902725)
XLA Ops:
  0.6 1.5 shard_map.128
  2.1 0.0 copy-start.3
  2.1 0.0 copy-start.4
  2.1 0.0 copy-start.5
  2.1 10.6 %all-to-all-start = ((f32[16,16,128]{2,1,0:T(8,128)}), f32[16,16,128]{2,1,0:T(8,128)S(1)}, u32[]{:S(2)}, u32[]{:S(2)}) async-start(f32[16,16,128]{2,1,0:T(8,128)} %get-tuple-element.19), calls=%async_computation | async-start | bytes 262144 | tf_op jit(solution)/shard_map/all_to_all | solution.py:43
  12.7 0.8 broadcast_in_dim.10.scales
  13.5 0.0 copy-start
  13.5 1.0 copy-done
  14.6 1.0 copy-done.1
  15.6 1.0 copy-done.2
  16.7 0.7 copy-done.6
  17.3 0.7 copy-done.8
  18.0 0.7 copy-done.10
  18.7 1.1 shard_map.129
  19.8 1.7 %all-to-all-done.squares = f32[16,16,128]{2,1,0:T(8,128)S(1)} async-done(((f32[16,16,128]{2,1,0:T(8,128)}), f32[16,16,128]{2,1,0:T(8,128)S(1)}, u32[]{:S(2)}, u32[]{:S(2)}) %all-to-all-start) | async-done | bytes 131104 | tf_op jit(solution)/shard_map/all_to_all | solution.py:43
  21.5 0.0 copy-done.3
  21.5 0.2 shard_map.130
  21.6 39.0 %all_to_all.25 = bf16[32,16,1024]{2,1,0:T(8,128)(2,1)S(1)} all-to-all(bf16[32,16,1024]{2,1,0:T(8,128)(2,1)S(1)} %get-tuple-element.25), channel_id=1, replica_groups=mesh['z'=8,'core'=2,'x'=4,'y'=8] {'x','y'}, dimensions={0} | all-to-all | bytes 2097152 | tf_op jit(solution)/shard_map/all_to_all | solution.py:43
  60.7 0.6 shard_map.132
  61.3 1.9 %collective-permute-start = (bf16[256,1536]{1,0:T(8,128)(2,1)S(1)}, bf16[256,1536]{1,0:T(8,128)(2,1)S(1)}, u32[]{:S(2)}, u32[]{:S(2)}) collective-permute-start(bf16[256,1536]{1,0:T(8,128)(2,1)S(1)} %shard_map.132), channel_id=1, source_target_pairs={{0,32},{32,0},{1,33},{33,1},{2,34},{34,2},{3,35},{35,3},{4,36},{36... | collective-permute-start | bytes 2359304 | tf_op jit(solution)/shard_map/ppermute | solution.py:39
  63.2 0.6 shard_map.131.own
  63.8 1.7 %collective-permute-done.theirs = bf16[256,1536]{1,0:T(8,128)(2,1)S(1)} collective-permute-done((bf16[256,1536]{1,0:T(8,128)(2,1)S(1)}, bf16[256,1536]{1,0:T(8,128)(2,1)S(1)}, u32[]{:S(2)}, u32[]{:S(2)}) %collective-permute-start) | collective-permute-done | bytes 786464 | tf_op jit(solution)/shard_map/ppermute | solution.py:39
  65.4 0.1 shard_map.133
  65.6 28.4 %all_to_all.26.parts = bf16[8,32,1536]{2,1,0:T(8,128)(2,1)S(1)} all-to-all(bf16[8,32,1536]{2,1,0:T(8,128)(2,1)S(1)} %bitcast.12), channel_id=1, replica_groups=mesh['z'=8,'core'=2,'x'=4,'y'=8] {'z'}, dimensions={0} | all-to-all | bytes 1572864 | tf_op jit(solution)/shard_map/all_to_all | solution.py:43
  94.0 0.2 shard_map.134
  94.1 24.7 %all_to_all.27 = bf16[8,32,1536]{2,1,0:T(8,128)(2,1)S(1)} all-to-all(bf16[8,32,1536]{2,1,0:T(8,128)(2,1)S(1)} %shard_map.134), channel_id=1, replica_groups=mesh['z'=8,'core'=2,'x'=4,'y'=8] {'z'}, dimensions={0} | all-to-all | bytes 1572864 | tf_op jit(solution)/shard_map/all_to_all | solution.py:43
  118.9 2.0 %collective-permute-start.1 = (bf16[256,1536]{1,0:T(8,128)(2,1)S(1)}, bf16[256,1536]{1,0:T(8,128)(2,1)S(1)}, u32[]{:S(2)}, u32[]{:S(2)}) collective-permute-start(bf16[256,1536]{1,0:T(8,128)(2,1)S(1)} %bitcast.9), channel_id=1, source_target_pairs={{0,32},{32,0},{1,33},{33,1},{2,34},{34,2},{3,35},{35,3},{4,36},{36... | collective-permute-start | bytes 2359304 | tf_op jit(solution)/shard_map/ppermute | solution.py:39
  120.9 0.6 shard_map.135.own
  121.5 1.7 %collective-permute-done.1.other_mid = bf16[256,1536]{1,0:T(8,128)(2,1)S(1)} collective-permute-done((bf16[256,1536]{1,0:T(8,128)(2,1)S(1)}, bf16[256,1536]{1,0:T(8,128)(2,1)S(1)}, u32[]{:S(2)}, u32[]{:S(2)}) %collective-permute-start.1) | collective-permute-done | bytes 786464 | tf_op jit(solution)/shard_map/ppermute | solution.py:39
  123.2 3.0 %shard_map.136 = (bf16[512,1024]{1,0:T(8,128)(2,1)S(1)}, bf16[512,512]{1,0:T(8,128)(2,1)}, bf16[512,512]{1,0:T(8,128)(2,1)}, bf16[512,512]{1,0:T(8,128)(2,1)}) custom-call(s32[1]{0:T(128)} %bitcast.core, s32[4,4]{1,0:T(4,128)S(1)} %copy-done.7, s32[4,4]{1,0:T(4,128)S(1)} %copy-done.9, s32[4,4]{1,0:T(4,128)S(1)} %copy-done.11, bf16[512,1024]{1,0:T(8,128)(2,1)S(1)} %bitcast.8, ...), custom_call_target="tpu_custom_call" | custom-call | flops 1610612736 | bytes 7602372 | tf_op jit(solution)/shard_map/pallas_call | solution.py:61
  126.2 33.8 %all_to_all.28.parts = bf16[32,16,1024]{2,1,0:T(8,128)(2,1)S(1)} all-to-all(bf16[32,16,1024]{2,1,0:T(8,128)(2,1)S(1)} %bitcast.13), channel_id=1, replica_groups=mesh['z'=8,'core'=2,'x'=4,'y'=8] {'x','y'}, dimensions={0} | all-to-all | bytes 2097152 | tf_op jit(solution)/shard_map/all_to_all | solution.py:43
  160.0 0.8 shard_map.137
  (13 shorter events, 0.0 us)
Async XLA Ops:
  2.1 19.4 %copy-start.3 = (f32[16,512]{1,0:T(8,128)S(1)}, f32[16,512]{1,0:T(8,128)}, u32[]{:S(2)}) copy-start(f32[16,512]{1,0:T(8,128)} %get-tuple-element.20.smoothed) | copy-start | bytes 98308
  2.1 19.3 %copy-start.4 = (bf16[16,512]{1,0:T(8,128)(2,1)S(1)}, bf16[16,512]{1,0:T(8,128)(2,1)}, u32[]{:S(2)}) copy-start(bf16[16,512]{1,0:T(8,128)(2,1)} %get-tuple-element.22.cotangent) | copy-start | bytes 49156
  2.1 19.3 %copy-start.5 = (f32[1,512]{1,0:T(1,128)S(1)}, f32[1,512]{1,0:T(1,128)}, u32[]{:S(2)}) copy-start(f32[1,512]{1,0:T(1,128)} %get-tuple-element.21.scales) | copy-start | bytes 6148
  2.1 19.3 %all-to-all-start = ((f32[16,16,128]{2,1,0:T(8,128)}), f32[16,16,128]{2,1,0:T(8,128)S(1)}, u32[]{:S(2)}, u32[]{:S(2)}) async-start(f32[16,16,128]{2,1,0:T(8,128)} %get-tuple-element.19), calls=%async_computation | async-start | bytes 262144 | tf_op jit(solution)/shard_map/all_to_all | solution.py:43
  13.5 1.0 copy-start
  14.6 1.0 copy-start.1
  15.6 1.0 copy-start.2
  16.7 0.7 copy-start.6
  17.3 0.7 copy-start.8
  18.0 0.7 copy-start.10
  61.3 4.2 %collective-permute-start = (bf16[256,1536]{1,0:T(8,128)(2,1)S(1)}, bf16[256,1536]{1,0:T(8,128)(2,1)S(1)}, u32[]{:S(2)}, u32[]{:S(2)}) collective-permute-start(bf16[256,1536]{1,0:T(8,128)(2,1)S(1)} %shard_map.132), channel_id=1, source_target_pairs={{0,32},{32,0},{1,33},{33,1},{2,34},{34,2},{3,35},{35,3},{4,36},{36... | collective-permute-start | bytes 2359304 | tf_op jit(solution)/shard_map/ppermute | solution.py:39
  118.9 4.3 %copy-start.7 = (s32[4,4]{1,0:T(4,128)S(1)}, s32[4,4]{1,0:T(4,128)}, u32[]{:S(2)}) copy-start(s32[4,4]{1,0:T(4,128)} %gate_mask.3) | copy-start | bytes 196
  118.9 4.3 %copy-start.9 = (s32[4,4]{1,0:T(4,128)S(1)}, s32[4,4]{1,0:T(4,128)}, u32[]{:S(2)}) copy-start(s32[4,4]{1,0:T(4,128)} %up_mask.3) | copy-start | bytes 196
  118.9 4.3 %copy-start.11 = (s32[4,4]{1,0:T(4,128)S(1)}, s32[4,4]{1,0:T(4,128)}, u32[]{:S(2)}) copy-start(s32[4,4]{1,0:T(4,128)} %down_mask.3) | copy-start | bytes 196
  118.9 4.3 %collective-permute-start.1 = (bf16[256,1536]{1,0:T(8,128)(2,1)S(1)}, bf16[256,1536]{1,0:T(8,128)(2,1)S(1)}, u32[]{:S(2)}, u32[]{:S(2)}) collective-permute-start(bf16[256,1536]{1,0:T(8,128)(2,1)S(1)} %bitcast.9), channel_id=1, source_target_pairs={{0,32},{32,0},{1,33},{33,1},{2,34},{34,2},{3,35},{35,3},{4,36},{36... | collective-permute-start | bytes 2359304 | tf_op jit(solution)/shard_map/ppermute | solution.py:39

commit v4 on v3

--- a/solution.py
+++ b/solution.py
@@ -98,31 +98,61 @@
 
 
 def prepare_kernel(
-    gate_mask, up_mask, down_mask, scales, gate, up, down, both_kept, down_kept
+    gate_mask,
+    up_mask,
+    down_mask,
+    scales,
+    gate,
+    up,
+    down,
+    both_kept,
+    down_kept,
+    ready,
+    gate_keeps,
+    up_keeps,
+    down_keeps,
+    gate_here,
+    up_here,
+    down_here,
+    arrived,
 ):
+    sources = (gate_mask, up_mask, down_mask, gate, up, down)
+    places = (gate_keeps, up_keeps, down_keeps, gate_here, up_here, down_here)
+    moves = [
+        pltpu.make_async_copy(source, place, arrived.at[k])
+        for k, (source, place) in enumerate(zip(sources, places))
+    ]
+    for move in moves:
+        move.start()
+    for move in moves[:4]:
+        move.wait()
     width = gate.shape[1]
-    for i in range(gate.shape[0] // TILE):
-        rows = slice(i * TILE, (i + 1) * TILE)
-        scale = scales[rows, :]
-        for j in range(width // TILE):
-            columns = slice(j * TILE, (j + 1) * TILE)
-            shifted = slice(width + j * TILE, width + (j + 1) * TILE)
-            gate_keep = gate_mask[i, j].astype(jnp.float32)
-            up_keep = up_mask[i, j].astype(jnp.float32)
-            down_keep = down_mask[i, j].astype(jnp.float32)
-            both_kept[rows, columns] = (
-                scale * gate[rows, columns].astype(jnp.float32) * gate_keep
-            ).astype(both_kept.dtype)
-            both_kept[rows, shifted] = (
-                scale * up[rows, columns].astype(jnp.float32) * up_keep
-            ).astype(both_kept.dtype)
-            down_kept[rows, columns] = (
-                down[rows, columns].astype(jnp.float32) * down_keep
-            ).astype(down_kept.dtype)
-
-
-def quantize_kernel(squares, smoothed, scales, cotangent, both_kept, down_kept, copies, slope):
-    del both_kept, down_kept
+    count = gate.shape[0] // TILE
+    tiles = [
+        (i, j, slice(i * TILE, (i + 1) * TILE), slice(j * TILE, (j + 1) * TILE))
+        for i in range(count)
+        for j in range(width // TILE)
+    ]
+    for i, j, rows, columns in tiles:
+        keep = gate_keeps[i, j].astype(jnp.float32)
+        kept = scales[rows, :] * gate_here[rows, columns].astype(jnp.float32) * keep
+        both_kept[rows, columns] = kept.astype(both_kept.dtype)
+    moves[4].wait()
+    for i, j, rows, columns in tiles:
+        keep = up_keeps[i, j].astype(jnp.float32)
+        kept = scales[rows, :] * up_here[rows, columns].astype(jnp.float32) * keep
+        shifted = slice(width + columns.start, width + columns.stop)
+        both_kept[rows, shifted] = kept.astype(both_kept.dtype)
+    moves[5].wait()
+    for i, j, rows, columns in tiles:
+        keep = down_keeps[i, j].astype(jnp.float32)
+        kept = down_here[rows, columns].astype(jnp.float32) * keep
+        down_kept[rows, columns] = kept.astype(down_kept.dtype)
+    ready[...] = scales[: ready.shape[0], :]
+
+
+def quantize_kernel(squares, smoothed, scales, cotangent, ready, copies, slope):
+    del ready
     width = smoothed.shape[1]
     mean_square = jnp.sum(add_parts(squares), axis=1, keepdims=True) / D
     limits = clip_ratio * jnp.sqrt(mean_square + 1e-06)
@@ -132,6 +162,11 @@
     for i in range(copies.shape[0]):
         copies[i, :, :width] = quantized
         copies[i, :, width:] = cotangent[...]
+
+
+def copy_kernel(block, copies):
+    for i in range(copies.shape[0]):
+        copies[i] = block[0]
 
 
 def forward_kernel(other, core, both_in, both_kept, down_kept, sums):
@@ -233,6 +268,10 @@
             )
 
 
+def add_kernel(parts, total):
+    total[...] = add_parts(parts).astype(total.dtype)
+
+
 def finish_kernel(parts, slope, output, input_grad):
     total = add_parts(parts)
     width = output.shape[1]
@@ -268,19 +307,29 @@
         scratch=[pltpu.VMEM((own_tokens, width), bf16), pltpu.SemaphoreType.DMA((3,))],
     )
     squares = exchange(squares, ROW)
-    both_kept, down_kept = local_kernel(
+    both_kept, down_kept, ready = local_kernel(
         prepare_kernel,
-        [shape((width, 2 * hidden_width), bf16), shape((hidden_width, width), bf16)],
+        [
+            shape((width, 2 * hidden_width), bf16),
+            shape((hidden_width, width), bf16),
+            shape((8, TILE), f32),
+        ],
         masks + [scale_lanes, gate_weight, up_weight, down_weight],
-        3,
+        stored=(0, 1, 2, 4, 5, 6),
+        room=60,
+        scratch=[pltpu.SMEM(mask.shape, mask.dtype) for mask in masks]
+        + [pltpu.VMEM(w.shape, w.dtype) for w in (gate_weight, up_weight, down_weight)]
+        + [pltpu.SemaphoreType.DMA((6,))],
     )
     copies, slope = local_kernel(
         quantize_kernel,
-        [shape((N_COL, own_tokens, 2 * width), bf16), shape((own_tokens, width), f32)],
-        [squares, smoothed, scales_here, cotangent_here, both_kept, down_kept],
-        apart=(4, 5),
-    )
-    both_in = exchange(copies, COL).reshape(all_tokens, 2 * width)
+        [shape((N_Y, own_tokens, 2 * width), bf16), shape((own_tokens, width), f32)],
+        [squares, smoothed, scales_here, cotangent_here, ready],
+        apart=(4,),
+    )
+    gathered = exchange(copies, "y").reshape(1, N_Y * own_tokens, 2 * width)
+    copies = local_kernel(copy_kernel, [shape((N_X,) + gathered.shape[1:], bf16)], [gathered])
+    both_in = exchange(copies, "x").reshape(all_tokens, 2 * width)
 
     flops = 6 * half_tokens * width * hidden_width
     theirs = local_kernel(
@@ -326,7 +375,9 @@
         4,
         4 * flops,
     )
-    back = exchange(back.reshape(N_COL, own_tokens, -1), COL)
+    back = exchange(back.reshape(N_X, all_tokens // N_X, -1), "x")
+    back = local_kernel(add_kernel, [shape(back.shape[1:], bf16)], [back])
+    back = exchange(back.reshape(N_Y, own_tokens, -1), "y")
     output, input_grad = local_kernel(
         finish_kernel, [shape((own_tokens, width), bf16)] * 2, [back, slope]
     )

time: 161 us -> 159 us (0.988)
  the two profiles are of different devices: /device:TPU:8 before, /device:TPU:1 now
where the time goes in v4:
time: 159 us; the launch traced here: 158 us
  blocking collectives  119 us (75%)
  starting transfers between devices  18.3 us (12%)
  Pallas kernels  11 us (7%)
  waiting for transfers between devices  6.73 us (4%)
  local copies, waits for them, and re-layouts  2.24 us (1%)
    all_to_all x6, blocking collectives, exchange(): return lax.all_to_all(parts, axis, 0, 0, tiled=True)  119 us
    all_to_all x1, starting transfers between devices, exchange(): return lax.all_to_all(parts, axis, 0, 0, tiled=True)  11.8 us
    pallas_call x12, Pallas kernels, local_kernel(): pl.pallas_call(body, out_shape=outs if len(outs) > 1 else outs[0], in_spe...  11 us
    ppermute x2, starting transfers between devices, swap_cores(): return lax.ppermute(block, 'core', [(0, 1), (1, 0)])  6.42 us
    all_to_all x1, waiting for transfers between devices, exchange(): return lax.all_to_all(parts, axis, 0, 0, tiled=True)  4.11 us
  transfers between devices with their start and end apart: 3, of which 3 were waited for; matrix products, arithmetic and copies ran while one was open for 1% of the time, Pallas kernels for 3%

profile of v4, /device:TPU:1, one launch (start us, length us, event | category | flops | bytes accessed | tf_op | source)
XLA Modules:
  0.0 157.8 jit_solution(15186348874611447438)
XLA Ops:
  0.6 1.5 shard_map.128
  2.1 0.0 copy-start.3
  2.1 0.0 copy-start.4
  2.1 11.8 %all-to-all-start = ((f32[16,16,128]{2,1,0:T(8,128)}), f32[16,16,128]{2,1,0:T(8,128)S(1)}, u32[]{:S(2)}, u32[]{:S(2)}) async-start(f32[16,16,128]{2,1,0:T(8,128)} %get-tuple-element.20), calls=%async_computation | async-start | bytes 262144 | tf_op jit(solution)/shard_map/all_to_all | solution.py:43
  14.0 1.5 broadcast_in_dim.10.scales
  15.5 3.5 %shard_map.129 = (bf16[512,1024]{1,0:T(8,128)(2,1)}, bf16[512,512]{1,0:T(8,128)(2,1)}, f32[8,128]{1,0:T(8,128)}) custom-call(s32[4,4]{1,0:T(4,128)} %gate_mask.3, s32[4,4]{1,0:T(4,128)} %up_mask.3, s32[4,4]{1,0:T(4,128)} %down_mask.3, f32[512,128]{1,0:T(8,128)} %broadcast_in_dim.10.scales, bf16[512,512]{1,0:T(8,128)(2,1)} %gate.1, bf16[512,512]{1,0:T(8,128)(2,1)} %up.1, ...), custom_call_target="tpu_custom_call" | custom-call | bytes 3412160 | tf_op jit(solution)/shard_map/pallas_call | solution.py:61
  19.0 4.1 %all-to-all-done.squares = f32[16,16,128]{2,1,0:T(8,128)S(1)} async-done(((f32[16,16,128]{2,1,0:T(8,128)}), f32[16,16,128]{2,1,0:T(8,128)S(1)}, u32[]{:S(2)}, u32[]{:S(2)}) %all-to-all-start) | async-done | bytes 131104 | tf_op jit(solution)/shard_map/all_to_all | solution.py:43
  23.2 0.0 copy-done.4
  23.2 0.0 copy-start.5
  23.2 0.7 copy-done.5
  23.9 0.1 shard_map.130
  24.0 19.0 %all_to_all.35 = bf16[8,16,1024]{2,1,0:T(8,128)(2,1)S(1)} all-to-all(bf16[8,16,1024]{2,1,0:T(8,128)(2,1)S(1)} %get-tuple-element.25), channel_id=1, replica_groups=mesh['z'=8,'core'=2,'x'=4,'y'=8] {'y'}, dimensions={0} | all-to-all | bytes 524288 | tf_op jit(solution)/shard_map/all_to_all | solution.py:43
  43.0 0.1 shard_map.131
  43.1 18.1 %all_to_all.36 = bf16[4,128,1024]{2,1,0:T(8,128)(2,1)S(1)} all-to-all(bf16[4,128,1024]{2,1,0:T(8,128)(2,1)S(1)} %shard_map.131), channel_id=1, replica_groups=mesh['z'=8,'core'=2,'x'=4,'y'=8] {'x'}, dimensions={0} | all-to-all | bytes 2097152 | tf_op jit(solution)/shard_map/all_to_all | solution.py:43
  61.2 0.6 shard_map.133
  61.8 3.8 %collective-permute-start = (bf16[256,1536]{1,0:T(8,128)(2,1)S(1)}, bf16[256,1536]{1,0:T(8,128)(2,1)S(1)}, u32[]{:S(2)}, u32[]{:S(2)}) collective-permute-start(bf16[256,1536]{1,0:T(8,128)(2,1)S(1)} %shard_map.133), channel_id=1, source_target_pairs={{0,32},{32,0},{1,33},{33,1},{2,34},{34,2},{3,35},{35,3},{4,36},{36... | collective-permute-start | bytes 2359304 | tf_op jit(solution)/shard_map/ppermute | solution.py:39
  65.6 0.6 shard_map.132.own
  66.2 1.3 collective-permute-done.theirs
  67.5 0.1 shard_map.134
  67.6 26.0 %all_to_all.37.parts = bf16[8,32,1536]{2,1,0:T(8,128)(2,1)S(1)} all-to-all(bf16[8,32,1536]{2,1,0:T(8,128)(2,1)S(1)} %bitcast.14), channel_id=1, replica_groups=mesh['z'=8,'core'=2,'x'=4,'y'=8] {'z'}, dimensions={0} | all-to-all | bytes 1572864 | tf_op jit(solution)/shard_map/all_to_all | solution.py:43
  93.6 0.2 shard_map.135
  93.8 25.9 %all_to_all.38 = bf16[8,32,1536]{2,1,0:T(8,128)(2,1)S(1)} all-to-all(bf16[8,32,1536]{2,1,0:T(8,128)(2,1)S(1)} %shard_map.135), channel_id=1, replica_groups=mesh['z'=8,'core'=2,'x'=4,'y'=8] {'z'}, dimensions={0} | all-to-all | bytes 1572864 | tf_op jit(solution)/shard_map/all_to_all | solution.py:43
  119.7 2.6 %collective-permute-start.1 = (bf16[256,1536]{1,0:T(8,128)(2,1)S(1)}, bf16[256,1536]{1,0:T(8,128)(2,1)S(1)}, u32[]{:S(2)}, u32[]{:S(2)}) collective-permute-start(bf16[256,1536]{1,0:T(8,128)(2,1)S(1)} %bitcast.11), channel_id=1, source_target_pairs={{0,32},{32,0},{1,33},{33,1},{2,34},{34,2},{3,35},{35,3},{4,36},{36... | collective-permute-start | bytes 2359304 | tf_op jit(solution)/shard_map/ppermute | solution.py:39
  122.3 0.6 shard_map.136.own
  122.9 1.3 collective-permute-done.1.other_mid
  124.2 0.0 copy-done.2
  124.2 0.0 copy-done.8
  124.2 3.0 %shard_map.137 = (bf16[512,1024]{1,0:T(8,128)(2,1)S(1)}, bf16[512,512]{1,0:T(8,128)(2,1)}, bf16[512,512]{1,0:T(8,128)(2,1)}, bf16[512,512]{1,0:T(8,128)(2,1)}) custom-call(s32[1]{0:T(128)} %bitcast.core, s32[4,4]{1,0:T(4,128)S(1)} %copy-done.7, s32[4,4]{1,0:T(4,128)S(1)} %copy-done.8, s32[4,4]{1,0:T(4,128)S(1)} %copy-done.9, bf16[512,1024]{1,0:T(8,128)(2,1)S(1)} %bitcast.10, ...), custom_call_target="tpu_custom_call" | custom-call | flops 1610612736 | bytes 7602372 | tf_op jit(solution)/shard_map/pallas_call | solution.py:61
  127.2 17.3 %all_to_all.39.parts = bf16[4,128,1024]{2,1,0:T(8,128)(2,1)S(1)} all-to-all(bf16[4,128,1024]{2,1,0:T(8,128)(2,1)S(1)} %bitcast.17), channel_id=1, replica_groups=mesh['z'=8,'core'=2,'x'=4,'y'=8] {'x'}, dimensions={0} | all-to-all | bytes 2097152 | tf_op jit(solution)/shard_map/all_to_all | solution.py:43
  144.5 0.1 shard_map.138
  144.6 12.5 %all_to_all.40.parts = bf16[8,16,1024]{2,1,0:T(8,128)(2,1)S(1)} all-to-all(bf16[8,16,1024]{2,1,0:T(8,128)(2,1)S(1)} %bitcast.16), channel_id=1, replica_groups=mesh['z'=8,'core'=2,'x'=4,'y'=8] {'y'}, dimensions={0} | all-to-all | bytes 524288 | tf_op jit(solution)/shard_map/all_to_all | solution.py:43
  157.1 0.6 shard_map.139
  (13 shorter events, 0.0 us)
Async XLA Ops:
  2.1 21.0 %copy-start.3 = (f32[16,512]{1,0:T(8,128)S(1)}, f32[16,512]{1,0:T(8,128)}, u32[]{:S(2)}) copy-start(f32[16,512]{1,0:T(8,128)} %get-tuple-element.21.smoothed) | copy-start | bytes 98308
  2.1 21.0 %copy-start.4 = (bf16[16,512]{1,0:T(8,128)(2,1)S(1)}, bf16[16,512]{1,0:T(8,128)(2,1)}, u32[]{:S(2)}) copy-start(bf16[16,512]{1,0:T(8,128)(2,1)} %get-tuple-element.23.cotangent) | copy-start | bytes 49156
  2.1 21.0 %copy-start.6 = (f32[1,512]{1,0:T(1,128)S(1)}, f32[1,512]{1,0:T(1,128)}, u32[]{:S(2)}) copy-start(f32[1,512]{1,0:T(1,128)} %get-tuple-element.22.scales) | copy-start | bytes 6148
  2.1 21.0 %all-to-all-start = ((f32[16,16,128]{2,1,0:T(8,128)}), f32[16,16,128]{2,1,0:T(8,128)S(1)}, u32[]{:S(2)}, u32[]{:S(2)}) async-start(f32[16,16,128]{2,1,0:T(8,128)} %get-tuple-element.20), calls=%async_computation | async-start | bytes 262144 | tf_op jit(solution)/shard_map/all_to_all | solution.py:43
  23.2 0.7 copy-start.5
  43.0 18.2 %copy-start = (bf16[512,1024]{1,0:T(8,128)(2,1)S(1)}, bf16[512,1024]{1,0:T(8,128)(2,1)}, u32[]{:S(2)}) copy-start(bf16[512,1024]{1,0:T(8,128)(2,1)} %get-tuple-element.26.both_kept) | copy-start | bytes 3145732
  43.0 18.2 %copy-start.1 = (bf16[512,512]{1,0:T(8,128)(2,1)S(1)}, bf16[512,512]{1,0:T(8,128)(2,1)}, u32[]{:S(2)}) copy-start(bf16[512,512]{1,0:T(8,128)(2,1)} %get-tuple-element.27.down_kept) | copy-start | bytes 1572868
  61.8 5.7 %collective-permute-start = (bf16[256,1536]{1,0:T(8,128)(2,1)S(1)}, bf16[256,1536]{1,0:T(8,128)(2,1)S(1)}, u32[]{:S(2)}, u32[]{:S(2)}) collective-permute-start(bf16[256,1536]{1,0:T(8,128)(2,1)S(1)} %shard_map.133), channel_id=1, source_target_pairs={{0,32},{32,0},{1,33},{33,1},{2,34},{34,2},{3,35},{35,3},{4,36},{36... | collective-permute-start | bytes 2359304 | tf_op jit(solution)/shard_map/ppermute | solution.py:39
  119.7 4.5 %copy-start.2 = (f32[512,128]{1,0:T(8,128)S(1)}, f32[512,128]{1,0:T(8,128)}, u32[]{:S(2)}) copy-start(f32[512,128]{1,0:T(8,128)} %broadcast_in_dim.10.scales) | copy-start | bytes 786436
  119.7 4.5 %copy-start.7 = (s32[4,4]{1,0:T(4,128)S(1)}, s32[4,4]{1,0:T(4,128)}, u32[]{:S(2)}) copy-start(s32[4,4]{1,0:T(4,128)} %gate_mask.3) | copy-start | bytes 196
  119.7 4.5 %copy-start.8 = (s32[4,4]{1,0:T(4,128)S(1)}, s32[4,4]{1,0:T(4,128)}, u32[]{:S(2)}) copy-start(s32[4,4]{1,0:T(4,128)} %up_mask.3) | copy-start | bytes 196
  119.7 4.5 %copy-start.9 = (s32[4,4]{1,0:T(4,128)S(1)}, s32[4,4]{1,0:T(4,128)}, u32[]{:S(2)}) copy-start(s32[4,4]{1,0:T(4,128)} %down_mask.3) | copy-start | bytes 196
  119.7 4.5 %collective-permute-start.1 = (bf16[256,1536]{1,0:T(8,128)(2,1)S(1)}, bf16[256,1536]{1,0:T(8,128)(2,1)S(1)}, u32[]{:S(2)}, u32[]{:S(2)}) collective-permute-start(bf16[256,1536]{1,0:T(8,128)(2,1)S(1)} %bitcast.11), channel_id=1, source_target_pairs={{0,32},{32,0},{1,33},{33,1},{2,34},{34,2},{3,35},{35,3},{4,36},{36... | collective-permute-start | bytes 2359304 | tf_op jit(solution)/shard_map/ppermute | solution.py:39

commit v5 on v4

--- a/solution.py
+++ b/solution.py
@@ -14,6 +14,9 @@
 N_Z, N_CORE, N_X, N_Y = 8, 2, 4, 8
 N_ROW = N_Z * N_CORE
 N_COL = N_X * N_Y
+PLANE = ("core",) + COL
+N_NEAR = 4
+N_FAR = N_COL // N_NEAR
 
 
 clip_ratio = 1.5
@@ -41,6 +44,38 @@
 
 def exchange(parts, axis):
     return lax.all_to_all(parts, axis, 0, 0, tiled=True)
+
+
+def plane_place(core, x, y):
+    return (core * N_X + x % N_X) * N_Y + y % N_Y
+
+
+def near_groups():
+    groups = []
+    for core in range(N_CORE):
+        for x in range(core, N_X + core, 2):
+            for y in range(core, N_Y + core, 2):
+                block = [(x + i, y + j) for i in range(2) for j in range(2)]
+                block.sort(key=lambda at: (at[0] % 2, at[1] % 2))
+                groups.append([plane_place(core, *at) for at in block])
+    return groups
+
+
+def far_groups():
+    return [
+        [
+            plane_place(core, x, y)
+            for x in range(x_parity, N_X, 2)
+            for y in range(y_parity, N_Y, 2)
+        ]
+        for core in range(N_CORE)
+        for x_parity in range(2)
+        for y_parity in range(2)
+    ]
+
+
+def exchange_in(parts, groups):
+    return lax.all_to_all(parts, PLANE, 0, 0, axis_index_groups=groups, tiled=True)
 
 
 def add_parts(parts):
@@ -107,7 +142,6 @@
     down,
     both_kept,
     down_kept,
-    ready,
     gate_keeps,
     up_keeps,
     down_keeps,
@@ -148,11 +182,9 @@
         keep = down_keeps[i, j].astype(jnp.float32)
         kept = down_here[rows, columns].astype(jnp.float32) * keep
         down_kept[rows, columns] = kept.astype(down_kept.dtype)
-    ready[...] = scales[: ready.shape[0], :]
-
-
-def quantize_kernel(squares, smoothed, scales, cotangent, ready, copies, slope):
-    del ready
+
+
+def quantize_kernel(squares, smoothed, scales, cotangent, copies, slope):
     width = smoothed.shape[1]
     mean_square = jnp.sum(add_parts(squares), axis=1, keepdims=True) / D
     limits = clip_ratio * jnp.sqrt(mean_square + 1e-06)
@@ -307,12 +339,11 @@
         scratch=[pltpu.VMEM((own_tokens, width), bf16), pltpu.SemaphoreType.DMA((3,))],
     )
     squares = exchange(squares, ROW)
-    both_kept, down_kept, ready = local_kernel(
+    both_kept, down_kept = local_kernel(
         prepare_kernel,
         [
             shape((width, 2 * hidden_width), bf16),
             shape((hidden_width, width), bf16),
-            shape((8, TILE), f32),
         ],
         masks + [scale_lanes, gate_weight, up_weight, down_weight],
         stored=(0, 1, 2, 4, 5, 6),
@@ -321,15 +352,15 @@
         + [pltpu.VMEM(w.shape, w.dtype) for w in (gate_weight, up_weight, down_weight)]
         + [pltpu.SemaphoreType.DMA((6,))],
     )
+    squares, both_kept, down_kept = lax.optimization_barrier((squares, both_kept, down_kept))
     copies, slope = local_kernel(
         quantize_kernel,
-        [shape((N_Y, own_tokens, 2 * width), bf16), shape((own_tokens, width), f32)],
-        [squares, smoothed, scales_here, cotangent_here, ready],
-        apart=(4,),
-    )
-    gathered = exchange(copies, "y").reshape(1, N_Y * own_tokens, 2 * width)
-    copies = local_kernel(copy_kernel, [shape((N_X,) + gathered.shape[1:], bf16)], [gathered])
-    both_in = exchange(copies, "x").reshape(all_tokens, 2 * width)
+        [shape((N_FAR, own_tokens, 2 * width), bf16), shape((own_tokens, width), f32)],
+        [squares, smoothed, scales_here, cotangent_here],
+    )
+    gathered = exchange_in(copies, far_groups()).reshape(1, N_FAR * own_tokens, 2 * width)
+    copies = local_kernel(copy_kernel, [shape((N_NEAR,) + gathered.shape[1:], bf16)], [gathered])
+    both_in = exchange_in(copies, near_groups()).reshape(all_tokens, 2 * width)
 
     flops = 6 * half_tokens * width * hidden_width
     theirs = local_kernel(
@@ -375,9 +406,9 @@
         4,
         4 * flops,
     )
-    back = exchange(back.reshape(N_X, all_tokens // N_X, -1), "x")
+    back = exchange_in(back.reshape(N_NEAR, all_tokens // N_NEAR, -1), near_groups())
     back = local_kernel(add_kernel, [shape(back.shape[1:], bf16)], [back])
-    back = exchange(back.reshape(N_Y, own_tokens, -1), "y")
+    back = exchange_in(back.reshape(N_FAR, own_tokens, -1), far_groups())
     output, input_grad = local_kernel(
         finish_kernel, [shape((own_tokens, width), bf16)] * 2, [back, slope]
     )

time: 159 us -> 155 us (0.975)
  starting transfers between devices: 18.3 us -> 16.5 us
    all_to_all x6 -> x2, blocking collectives: 119 us -> 51.9 us  [exchange(): return lax.all_to_all(parts, axis, 0, 0, tiled=True)]
    all_to_all x0 -> x4, blocking collectives: none -> 65.6 us  [exchange_in(): lax.all_to_all(parts, PLANE, 0, 0, axis_index_groups=groups, tiled=True)]
    ppermute x2, starting transfers between devices: 6.42 us -> 4.52 us  [swap_cores(): return lax.ppermute(block, 'core', [(0, 1), (1, 0)])]
where the time goes in v5:
time: 155 us; the launch traced here: 154 us
  blocking collectives  118 us (76%)
  starting transfers between devices  16.5 us (11%)
  Pallas kernels  11 us (7%)
  waiting for transfers between devices  7.1 us (5%)
  local copies, waits for them, and re-layouts  1.56 us (1%)
    all_to_all x4, blocking collectives, exchange_in(): lax.all_to_all(parts, PLANE, 0, 0, axis_index_groups=groups, tiled=True)  65.6 us
    all_to_all x2, blocking collectives, exchange(): return lax.all_to_all(parts, axis, 0, 0, tiled=True)  51.9 us
    all_to_all x1, starting transfers between devices, exchange(): return lax.all_to_all(parts, axis, 0, 0, tiled=True)  12 us
    pallas_call x12, Pallas kernels, local_kernel(): pl.pallas_call(body, out_shape=outs if len(outs) > 1 else outs[0], in_spe...  11 us
    ppermute x2, starting transfers between devices, swap_cores(): return lax.ppermute(block, 'core', [(0, 1), (1, 0)])  4.52 us
    all_to_all x1, waiting for transfers between devices, exchange(): return lax.all_to_all(parts, axis, 0, 0, tiled=True)  4.11 us
  transfers between devices with their start and end apart: 3, of which 3 were waited for; matrix products, arithmetic and copies ran while one was open for 1% of the time, Pallas kernels for 3%

profile of v5, /device:TPU:1, one launch (start us, length us, event | category | flops | bytes accessed | tf_op | source)
XLA Modules:
  0.0 154.4 jit_solution(6481498996841677729)
XLA Ops:
  0.6 1.5 shard_map.128
  2.1 0.0 copy-start.3
  2.1 0.0 copy-start.4
  2.1 0.0 copy-start.5
  2.1 12.0 %all-to-all-start = ((f32[16,16,128]{2,1,0:T(8,128)}), f32[16,16,128]{2,1,0:T(8,128)S(1)}, u32[]{:S(2)}, u32[]{:S(2)}) async-start(f32[16,16,128]{2,1,0:T(8,128)} %get-tuple-element.22), calls=%async_computation | async-start | bytes 262144 | tf_op jit(solution)/shard_map/all_to_all | solution.py:46
  14.1 1.5 broadcast_in_dim.10.scales
  15.6 3.5 %shard_map.129 = (bf16[512,1024]{1,0:T(8,128)(2,1)}, bf16[512,512]{1,0:T(8,128)(2,1)}) custom-call(s32[4,4]{1,0:T(4,128)} %gate_mask.3, s32[4,4]{1,0:T(4,128)} %up_mask.3, s32[4,4]{1,0:T(4,128)} %down_mask.3, f32[512,128]{1,0:T(8,128)} %broadcast_in_dim.10.scales, bf16[512,512]{1,0:T(8,128)(2,1)} %gate.1, bf16[512,512]{1,0:T(8,128)(2,1)} %up.1, ...), custom_call_target="tpu_custom_call" | custom-call | bytes 3408064 | tf_op jit(solution)/shard_map/pallas_call | solution.py:96
  19.2 4.1 %all-to-all-done.squares = f32[16,16,128]{2,1,0:T(8,128)S(1)} async-done(((f32[16,16,128]{2,1,0:T(8,128)}), f32[16,16,128]{2,1,0:T(8,128)S(1)}, u32[]{:S(2)}, u32[]{:S(2)}) %all-to-all-start) | async-done | bytes 131104 | tf_op jit(solution)/shard_map/all_to_all | solution.py:46
  23.3 0.0 copy-done.3
  23.3 0.0 copy-done.4
  23.3 0.0 copy-done.5
  23.3 0.1 shard_map.130
  23.4 21.7 %all_to_all.35 = bf16[8,16,1024]{2,1,0:T(8,128)(2,1)S(1)} all-to-all(bf16[8,16,1024]{2,1,0:T(8,128)(2,1)S(1)} %get-tuple-element.29), channel_id=1, replica_groups={{0,2,4,6,16,18,20,22},{1,3,5,7,17,19,21,23},{8,10,12,14,24,26,28,30},{9..., dimensions={0} | all-to-all | bytes 524288 | tf_op jit(solution)/shard_map/all_to_all | solution.py:78
  45.1 0.1 shard_map.131
  45.2 13.8 %all_to_all.36 = bf16[4,128,1024]{2,1,0:T(8,128)(2,1)S(1)} all-to-all(bf16[4,128,1024]{2,1,0:T(8,128)(2,1)S(1)} %shard_map.131), channel_id=1, replica_groups={{0,1,8,9},{2,3,10,11},{4,5,12,13},{6,7,14,15},{16,17,24,25},{18,19,26,2..., dimensions={0} | all-to-all | bytes 2097152 | tf_op jit(solution)/shard_map/all_to_all | solution.py:78
  59.0 0.6 shard_map.133
  59.6 1.9 %collective-permute-start = (bf16[256,1536]{1,0:T(8,128)(2,1)S(1)}, bf16[256,1536]{1,0:T(8,128)(2,1)S(1)}, u32[]{:S(2)}, u32[]{:S(2)}) collective-permute-start(bf16[256,1536]{1,0:T(8,128)(2,1)S(1)} %shard_map.133), channel_id=1, source_target_pairs={{0,32},{32,0},{1,33},{33,1},{2,34},{34,2},{3,35},{35,3},{4,36},{36... | collective-permute-start | bytes 2359304 | tf_op jit(solution)/shard_map/ppermute | solution.py:42
  61.5 0.6 shard_map.132.own
  62.1 1.7 %collective-permute-done.theirs = bf16[256,1536]{1,0:T(8,128)(2,1)S(1)} collective-permute-done((bf16[256,1536]{1,0:T(8,128)(2,1)S(1)}, bf16[256,1536]{1,0:T(8,128)(2,1)S(1)}, u32[]{:S(2)}, u32[]{:S(2)}) %collective-permute-start) | collective-permute-done | bytes 786464 | tf_op jit(solution)/shard_map/ppermute | solution.py:42
  63.7 0.1 shard_map.134
  63.9 26.0 %all_to_all.37.parts = bf16[8,32,1536]{2,1,0:T(8,128)(2,1)S(1)} all-to-all(bf16[8,32,1536]{2,1,0:T(8,128)(2,1)S(1)} %bitcast.14), channel_id=1, replica_groups=mesh['z'=8,'core'=2,'x'=4,'y'=8] {'z'}, dimensions={0} | all-to-all | bytes 1572864 | tf_op jit(solution)/shard_map/all_to_all | solution.py:46
  89.9 0.2 shard_map.135
  90.1 25.9 %all_to_all.38 = bf16[8,32,1536]{2,1,0:T(8,128)(2,1)S(1)} all-to-all(bf16[8,32,1536]{2,1,0:T(8,128)(2,1)S(1)} %shard_map.135), channel_id=1, replica_groups=mesh['z'=8,'core'=2,'x'=4,'y'=8] {'z'}, dimensions={0} | all-to-all | bytes 1572864 | tf_op jit(solution)/shard_map/all_to_all | solution.py:46
  116.0 2.6 %collective-permute-start.1 = (bf16[256,1536]{1,0:T(8,128)(2,1)S(1)}, bf16[256,1536]{1,0:T(8,128)(2,1)S(1)}, u32[]{:S(2)}, u32[]{:S(2)}) collective-permute-start(bf16[256,1536]{1,0:T(8,128)(2,1)S(1)} %bitcast.11), channel_id=1, source_target_pairs={{0,32},{32,0},{1,33},{33,1},{2,34},{34,2},{3,35},{35,3},{4,36},{36... | collective-permute-start | bytes 2359304 | tf_op jit(solution)/shard_map/ppermute | solution.py:42
  118.6 0.6 shard_map.136.own
  119.2 1.3 collective-permute-done.1.other_mid
  120.5 0.0 copy-done.7
  120.5 3.0 %shard_map.137 = (bf16[512,1024]{1,0:T(8,128)(2,1)S(1)}, bf16[512,512]{1,0:T(8,128)(2,1)}, bf16[512,512]{1,0:T(8,128)(2,1)}, bf16[512,512]{1,0:T(8,128)(2,1)}) custom-call(s32[1]{0:T(128)} %bitcast.core, s32[4,4]{1,0:T(4,128)S(1)} %copy-done.6, s32[4,4]{1,0:T(4,128)S(1)} %copy-done.7, s32[4,4]{1,0:T(4,128)S(1)} %copy-done.8, bf16[512,1024]{1,0:T(8,128)(2,1)S(1)} %bitcast.10, ...), custom_call_target="tpu_custom_call" | custom-call | flops 1610612736 | bytes 7602372 | tf_op jit(solution)/shard_map/pallas_call | solution.py:96
  123.5 13.6 %all_to_all.39.parts = bf16[4,128,1024]{2,1,0:T(8,128)(2,1)S(1)} all-to-all(bf16[4,128,1024]{2,1,0:T(8,128)(2,1)S(1)} %bitcast.17), channel_id=1, replica_groups={{0,1,8,9},{2,3,10,11},{4,5,12,13},{6,7,14,15},{16,17,24,25},{18,19,26,2..., dimensions={0} | all-to-all | bytes 2097152 | tf_op jit(solution)/shard_map/all_to_all | solution.py:78
  137.1 0.1 shard_map.138
  137.3 16.5 %all_to_all.40.parts = bf16[8,16,1024]{2,1,0:T(8,128)(2,1)S(1)} all-to-all(bf16[8,16,1024]{2,1,0:T(8,128)(2,1)S(1)} %bitcast.16), channel_id=1, replica_groups={{0,2,4,6,16,18,20,22},{1,3,5,7,17,19,21,23},{8,10,12,14,24,26,28,30},{9..., dimensions={0} | all-to-all | bytes 524288 | tf_op jit(solution)/shard_map/all_to_all | solution.py:78
  153.8 0.6 shard_map.139
  (11 shorter events, 0.0 us)
Async XLA Ops:
  2.1 21.2 %copy-start.3 = (f32[16,512]{1,0:T(8,128)S(1)}, f32[16,512]{1,0:T(8,128)}, u32[]{:S(2)}) copy-start(f32[16,512]{1,0:T(8,128)} %get-tuple-element.26.smoothed) | copy-start | bytes 98308
  2.1 21.2 %copy-start.4 = (bf16[16,512]{1,0:T(8,128)(2,1)S(1)}, bf16[16,512]{1,0:T(8,128)(2,1)}, u32[]{:S(2)}) copy-start(bf16[16,512]{1,0:T(8,128)(2,1)} %get-tuple-element.28.cotangent) | copy-start | bytes 49156
  2.1 21.2 %copy-start.5 = (f32[1,512]{1,0:T(1,128)S(1)}, f32[1,512]{1,0:T(1,128)}, u32[]{:S(2)}) copy-start(f32[1,512]{1,0:T(1,128)} %get-tuple-element.27.scales) | copy-start | bytes 6148
  2.1 21.1 %all-to-all-start = ((f32[16,16,128]{2,1,0:T(8,128)}), f32[16,16,128]{2,1,0:T(8,128)S(1)}, u32[]{:S(2)}, u32[]{:S(2)}) async-start(f32[16,16,128]{2,1,0:T(8,128)} %get-tuple-element.22), calls=%async_computation | async-start | bytes 262144 | tf_op jit(solution)/shard_map/all_to_all | solution.py:46
  45.1 13.8 %copy-start = (bf16[512,1024]{1,0:T(8,128)(2,1)S(1)}, bf16[512,1024]{1,0:T(8,128)(2,1)}, u32[]{:S(2)}) copy-start(bf16[512,1024]{1,0:T(8,128)(2,1)} %get-tuple-element.30.both_kept) | copy-start | bytes 3145732
  45.1 13.8 %copy-start.1 = (bf16[512,512]{1,0:T(8,128)(2,1)S(1)}, bf16[512,512]{1,0:T(8,128)(2,1)}, u32[]{:S(2)}) copy-start(bf16[512,512]{1,0:T(8,128)(2,1)} %get-tuple-element.31.down_kept) | copy-start | bytes 1572868
  59.6 4.2 %collective-permute-start = (bf16[256,1536]{1,0:T(8,128)(2,1)S(1)}, bf16[256,1536]{1,0:T(8,128)(2,1)S(1)}, u32[]{:S(2)}, u32[]{:S(2)}) collective-permute-start(bf16[256,1536]{1,0:T(8,128)(2,1)S(1)} %shard_map.133), channel_id=1, source_target_pairs={{0,32},{32,0},{1,33},{33,1},{2,34},{34,2},{3,35},{35,3},{4,36},{36... | collective-permute-start | bytes 2359304 | tf_op jit(solution)/shard_map/ppermute | solution.py:42
  116.0 4.5 %copy-start.2 = (f32[512,128]{1,0:T(8,128)S(1)}, f32[512,128]{1,0:T(8,128)}, u32[]{:S(2)}) copy-start(f32[512,128]{1,0:T(8,128)} %broadcast_in_dim.10.scales) | copy-start | bytes 786436
  116.0 4.5 %copy-start.6 = (s32[4,4]{1,0:T(4,128)S(1)}, s32[4,4]{1,0:T(4,128)}, u32[]{:S(2)}) copy-start(s32[4,4]{1,0:T(4,128)} %gate_mask.3) | copy-start | bytes 196
  116.0 4.5 %copy-start.7 = (s32[4,4]{1,0:T(4,128)S(1)}, s32[4,4]{1,0:T(4,128)}, u32[]{:S(2)}) copy-start(s32[4,4]{1,0:T(4,128)} %up_mask.3) | copy-start | bytes 196
  116.0 4.5 %copy-start.8 = (s32[4,4]{1,0:T(4,128)S(1)}, s32[4,4]{1,0:T(4,128)}, u32[]{:S(2)}) copy-start(s32[4,4]{1,0:T(4,128)} %down_mask.3) | copy-start | bytes 196
  116.0 4.5 %collective-permute-start.1 = (bf16[256,1536]{1,0:T(8,128)(2,1)S(1)}, bf16[256,1536]{1,0:T(8,128)(2,1)S(1)}, u32[]{:S(2)}, u32[]{:S(2)}) collective-permute-start(bf16[256,1536]{1,0:T(8,128)(2,1)S(1)} %bitcast.11), channel_id=1, source_target_pairs={{0,32},{32,0},{1,33},{33,1},{2,34},{34,2},{3,35},{35,3},{4,36},{36... | collective-permute-start | bytes 2359304 | tf_op jit(solution)/shard_map/ppermute | solution.py:42

commit v6 on v5

v6 whole, which is shorter than its diff:
```python
import functools

import jax
import jax.numpy as jnp
from jax import lax
from jax.experimental import pallas as pl
from jax.experimental.pallas import tpu as pltpu
from jax.sharding import Mesh, PartitionSpec as P

D = 8192
TILE = 128
ROW = ("z", "core")
COL = ("x", "y")
N_Z, N_CORE, N_X, N_Y = 8, 2, 4, 8
N_ROW = N_Z * N_CORE
N_COL = N_X * N_Y
PLANE = ("core",) + COL
N_NEAR = 4
N_FAR = N_COL // N_NEAR


clip_ratio = 1.5


def matmul(left, right):
    return jnp.dot(left, right, preferred_element_type=jnp.float32)


def contract_last(left, right):
    return lax.dot_general(
        left, right, (((1,), (1,)), ((), ())), preferred_element_type=jnp.float32
    )


def contract_first(left, right):
    return lax.dot_general(
        left, right, (((0,), (0,)), ((), ())), preferred_element_type=jnp.float32
    )


def swap_cores(block):
    return lax.ppermute(block, "core", [(0, 1), (1, 0)])


def exchange(parts, axis):
    return lax.all_to_all(parts, axis, 0, 0, tiled=True)


def plane_place(core, x, y):
    return (core * N_X + x % N_X) * N_Y + y % N_Y


def near_groups():
    groups = []
    for core in range(N_CORE):
        for x in range(core, N_X + core, 2):
            for y in range(core, N_Y + core, 2):
                block = [(x + i, y + j) for i in range(2) for j in range(2)]
                block.sort(key=lambda at: (at[0] % 2, at[1] % 2))
                groups.append([plane_place(core, *at) for at in block])
    return groups


def far_groups():
    return [
        [
            plane_place(core, x, y)
            for core in range(N_CORE)
            for x in range(x_parity, N_X, 2)
            for y in range(y_parity, N_Y, 2)
        ]
        for x_parity in range(2)
        for y_parity in range(2)
    ]


def exchange_in(parts, groups):
    return lax.all_to_all(parts, PLANE, 0, 0, axis_index_groups=groups, tiled=True)


def add_parts(parts):
    total = parts[0].astype(jnp.float32)
    for i in range(1, parts.shape[0]):
        total = total + parts[i].astype(jnp.float32)
    return total


def local_kernel(body, outs, args, scalars=0, flops=0, apart=(), stored=(), scratch=(), room=32):
    moved = sum(a.size * a.dtype.itemsize for a in list(args) + list(outs))
    spaces = [pltpu.SMEM if i < scalars else pltpu.VMEM for i in range(len(args))]
    for i in apart:
        spaces[i] = pl.ANY
    for i in stored:
        spaces[i] = pltpu.HBM
    specs = [pl.BlockSpec(memory_space=pltpu.VMEM)] * len(outs)
    return pl.pallas_call(
        body,
        out_shape=outs if len(outs) > 1 else outs[0],
        in_specs=[pl.BlockSpec(memory_space=space) for space in spaces],
        out_specs=specs if len(outs) > 1 else specs[0],
        scratch_shapes=list(scratch),
        compiler_params=pltpu.CompilerParams(vmem_limit_bytes=room << 20),
        cost_estimate=pl.CostEstimate(flops=flops, transcendentals=0, bytes_accessed=moved),
    )(*args)


def shape(dims, dtype):
    return jax.ShapeDtypeStruct(dims, dtype)


def squares_kernel(
    core, tokens, scales, cotangent, copies, smoothed, scales_here, cotangent_here, tokens_here, arrived
):
    del core
    moves = [
        pltpu.make_async_copy(tokens, tokens_here, arrived.at[0]),
        pltpu.make_async_copy(scales, scales_here, arrived.at[1]),
        pltpu.make_async_copy(cotangent, cotangent_here, arrived.at[2]),
    ]
    for move in moves:
        move.start()
    for move in moves:
        move.wait()
    value = tokens_here[...].astype(jnp.float32) / scales_here[...]
    smoothed[...] = value
    squares = value * value
    lanes = copies.shape[2]
    total = squares[:, :lanes]
    for start in range(lanes, squares.shape[1], lanes):
        total = total + squares[:, start : start + lanes]
    for i in range(copies.shape[0]):
        copies[i] = total


def prepare_kernel(
    gate_mask,
    up_mask,
    down_mask,
    scales,
    gate,
    up,
    down,
    weights,
    scale_lanes,
    gate_keeps,
    up_keeps,
    down_keeps,
    scales_here,
    gate_here,
    up_here,
    down_here,
    arrived,
):
    sources = (gate_mask, up_mask, down_mask, scales, gate, up, down)
    places = (gate_keeps, up_keeps, down_keeps, scales_here, gate_here, up_here, down_here)
    moves = [
        pltpu.make_async_copy(source, place, arrived.at[k])
        for k, (source, place) in enumerate(zip(sources, places))
    ]
    for move in moves:
        move.start()
    for move in moves[:5]:
        move.wait()
    width = gate.shape[1]
    count = gate.shape[0] // TILE
    for i in range(count):
        block = slice(i * TILE, (i + 1) * TILE)
        scale_lanes[block, :] = jnp.broadcast_to(scales_here[:, block], (TILE, TILE)).T
    tiles = [
        (i, j, slice(i * TILE, (i + 1) * TILE), slice(j * TILE, (j + 1) * TILE))
        for i in range(count)
        for j in range(width // TILE)
    ]
    for i, j, rows, columns in tiles:
        keep = gate_keeps[i, j].astype(jnp.float32)
        kept = scale_lanes[rows, :] * gate_here[rows, columns].astype(jnp.float32) * keep
        weights[rows, columns] = kept.astype(weights.dtype)
    moves[5].wait()
    for i, j, rows, columns in tiles:
        keep = up_keeps[i, j].astype(jnp.float32)
        kept = scale_lanes[rows, :] * up_here[rows, columns].astype(jnp.float32) * keep
        shifted = slice(width + columns.start, width + columns.stop)
        weights[rows, shifted] = kept.astype(weights.dtype)
    moves[6].wait()
    for i, j, rows, columns in tiles:
        keep = down_keeps[i, j].astype(jnp.float32)
        kept = down_here[rows, columns].astype(jnp.float32) * keep
        shifted = slice(2 * width + columns.start, 2 * width + columns.stop)
        weights[rows, shifted] = kept.astype(weights.dtype)


def quantize_kernel(squares, smoothed, scales, cotangent, copies, slope):
    rows, width = copies.shape[1], smoothed.shape[1]
    mean_square = jnp.sum(add_parts(squares), axis=1, keepdims=True) / D
    limits = clip_ratio * jnp.sqrt(mean_square + 1e-06)
    squashed = jnp.tanh(smoothed[...] / limits)
    quantized = limits * squashed
    slope[...] = (1.0 - squashed * squashed) / scales[...]
    gradient = cotangent[...].astype(jnp.float32)
    for core in range(N_CORE):
        own = slice(core * rows, (core + 1) * rows)
        quantized_half = quantized[own].astype(copies.dtype)
        gradient_half = gradient[own].astype(copies.dtype)
        for i in range(N_FAR):
            copies[core * N_FAR + i, :, :width] = quantized_half
            copies[core * N_FAR + i, :, width:] = gradient_half


def copy_kernel(blocks, copies):
    width = blocks.shape[2]
    for i in range(copies.shape[0]):
        for core in range(blocks.shape[0]):
            copies[i, :, core * width : (core + 1) * width] = blocks[core]


def lanes_of(core, start, width, count=1):
    return pl.ds(pl.multiple_of(core * 2 * width + start, TILE), count * width)


def forward_kernel(core, both_in, own_weights, other_weights, sums):
    width = own_weights.shape[0]
    split = sums.shape[1] - width
    gate_up = None
    for place, weights in ((core[0], own_weights), (1 - core[0], other_weights)):
        quantized = both_in[:, lanes_of(place, 0, width)]
        gradient = both_in[:, lanes_of(place, width, width)]
        first = matmul(quantized, weights[:, :split])
        second = contract_last(gradient, weights[:, split:])
        if gate_up is None:
            gate_up, hidden_grad = first, second
        else:
            gate_up, hidden_grad = gate_up + first, hidden_grad + second
    sums[:, :split] = gate_up.astype(sums.dtype)
    sums[:, split:] = hidden_grad.astype(sums.dtype)


def swiglu_kernel(parts, copies):
    pre = add_parts(parts)
    width = pre.shape[1] // 3
    gate_pre = pre[:, :width]
    up_pre = pre[:, width : 2 * width]
    hidden_grad = pre[:, 2 * width :]
    sigmoid_gate = 1.0 / (1.0 + jnp.exp(-gate_pre))
    silu_gate = gate_pre * sigmoid_gate
    gate_dir = hidden_grad * up_pre * sigmoid_gate * (1.0 + gate_pre * (1.0 - sigmoid_gate))
    up_dir = hidden_grad * silu_gate
    hidden = silu_gate * up_pre
    for k, value in enumerate((gate_dir, up_dir, hidden)):
        rounded = value.astype(copies.dtype)
        for i in range(copies.shape[0]):
            copies[i, :, k * width : (k + 1) * width] = rounded


def back_kernel(core, both_in, mid, own_weights, other_weights, back, parcel):
    width = own_weights.shape[0]
    split = mid.shape[1] - width
    parcel[:, : 2 * width] = both_in[:, lanes_of(1 - core[0], 0, width, 2)]
    parcel[:, 2 * width :] = mid[...]
    for place, weights in ((core[0], own_weights), (1 - core[0], other_weights)):
        output = matmul(mid[:, split:], weights[:, split:])
        back[:, lanes_of(place, 0, width)] = output.astype(back.dtype)
        quant_grad = contract_last(mid[:, :split], weights[:, :split])
        back[:, lanes_of(place, width, width)] = quant_grad.astype(back.dtype)


def weight_grads_kernel(
    core,
    gate_mask,
    up_mask,
    down_mask,
    both_in,
    mid,
    parcel,
    scales,
    gate_grad,
    up_grad,
    down_grad,
):
    width = gate_grad.shape[0]
    split = mid.shape[1] - width
    own_quantized = both_in[:, lanes_of(core[0], 0, width)]
    own_gradient = both_in[:, lanes_of(core[0], width, width)]
    start = 2 * width
    for i in range(width // TILE):
        block = slice(i * TILE, (i + 1) * TILE)
        product = contract_first(own_quantized[:, block], mid[:, :split])
        product = product + contract_first(parcel[:, block], parcel[:, start : start + split])
        for j in range(split // TILE):
            mask, grad = (gate_mask, gate_grad) if j < split // TILE // 2 else (up_mask, up_grad)
            column = j % (split // TILE // 2)
            tile = product[:, j * TILE : (j + 1) * TILE]
            keep = mask[i, column].astype(jnp.float32)
            grad[block, column * TILE : (column + 1) * TILE] = (
                scales[block, :] * tile * keep
            ).astype(grad.dtype)
    for i in range(down_grad.shape[0] // TILE):
        units = slice(split + i * TILE, split + (i + 1) * TILE)
        others = slice(start + units.start, start + units.stop)
        product = contract_first(mid[:, units], own_gradient)
        product = product + contract_first(parcel[:, others], parcel[:, width:start])
        for j in range(width // TILE):
            columns = slice(j * TILE, (j + 1) * TILE)
            keep = down_mask[i, j].astype(jnp.float32)
            down_grad[i * TILE : (i + 1) * TILE, columns] = (product[:, columns] * keep).astype(
                down_grad.dtype
            )


def add_kernel(parts, totals):
    total = add_parts(parts).astype(totals.dtype)
    width = totals.shape[2]
    for core in range(totals.shape[0]):
        totals[core] = total[:, core * width : (core + 1) * width]


def finish_kernel(parts, slope, output, input_grad):
    total = jnp.concatenate([add_parts(parts[:N_FAR]), add_parts(parts[N_FAR:])], axis=0)
    width = output.shape[1]
    output[...] = total[:, :width].astype(output.dtype)
    input_grad[...] = (total[:, width:] * slope[...]).astype(input_grad.dtype)


def per_device(
    tokens, scales, gate_weight, up_weight, down_weight, gate_mask, up_mask, down_mask, cotangent
):
    hidden_width = gate_weight.shape[1]
    own_tokens, width = tokens.shape
    all_tokens = own_tokens * N_COL
    half_tokens = all_tokens // N_CORE
    mid_tokens = half_tokens // N_Z
    bf16, f32 = jnp.bfloat16, jnp.float32
    core = lax.axis_index("core").astype(jnp.int32).reshape(1)
    masks = [gate_mask, up_mask, down_mask]

    squares, smoothed, scales_here, cotangent_here = local_kernel(
        squares_kernel,
        [
            shape((N_ROW, own_tokens, TILE), f32),
            shape((own_tokens, width), f32),
            shape((1, width), f32),
            shape((own_tokens, width), bf16),
        ],
        [core, tokens, scales[None, :], cotangent],
        1,
        stored=(1, 2, 3),
        room=60,
        scratch=[pltpu.VMEM((own_tokens, width), bf16), pltpu.SemaphoreType.DMA((3,))],
    )
    squares = exchange(squares, ROW)
    weights = (gate_weight, up_weight, down_weight)
    own_weights, scale_lanes = local_kernel(
        prepare_kernel,
        [shape((width, 3 * hidden_width), bf16), shape((width, TILE), f32)],
        masks + [scales_here] + list(weights),
        stored=range(7),
        room=60,
        scratch=[pltpu.SMEM(mask.shape, mask.dtype) for mask in masks]
        + [pltpu.VMEM((1, width), f32)]
        + [pltpu.VMEM(w.shape, w.dtype) for w in weights]
        + [pltpu.SemaphoreType.DMA((7,))],
    )
    squares, own_weights = lax.optimization_barrier((squares, own_weights))
    other_weights = swap_cores(own_weights)
    copies, slope = local_kernel(
        quantize_kernel,
        [
            shape((N_CORE * N_FAR, own_tokens // N_CORE, 2 * width), bf16),
            shape((own_tokens, width), f32),
        ],
        [squares, smoothed, scales_here, cotangent_here],
    )
    gathered = exchange_in(copies, far_groups())
    gathered, other_weights = lax.optimization_barrier((gathered, other_weights))
    gathered = gathered.reshape(N_CORE, half_tokens // N_NEAR, 2 * width)
    copies = local_kernel(
        copy_kernel, [shape((N_NEAR, half_tokens // N_NEAR, 4 * width), bf16)], [gathered]
    )
    both_in = exchange_in(copies, near_groups()).reshape(half_tokens, 4 * width)

    flops = 12 * half_tokens * width * hidden_width
    sums = local_kernel(
        forward_kernel,
        [shape((half_tokens, 3 * hidden_width), bf16)],
        [core, both_in, own_weights, other_weights],
        1,
        flops,
    )
    parts = exchange(sums.reshape(N_Z, mid_tokens, -1), "z")
    mid = local_kernel(swiglu_kernel, [shape(parts.shape, bf16)], [parts])
    mid = exchange(mid, "z").reshape(half_tokens, -1)
    back, parcel = local_kernel(
        back_kernel,
        [
            shape((half_tokens, 4 * width), bf16),
            shape((half_tokens, 2 * width + 3 * hidden_width), bf16),
        ],
        [core, both_in, mid, own_weights, other_weights],
        1,
        flops,
    )
    back = exchange_in(back.reshape(N_NEAR, half_tokens // N_NEAR, -1), near_groups())
    back, parcel = lax.optimization_barrier((back, parcel))
    parcel = swap_cores(parcel)
    back = local_kernel(
        add_kernel, [shape((N_CORE, half_tokens // N_NEAR, 2 * width), bf16)], [back]
    )
    back = exchange_in(back.reshape(N_CORE * N_FAR, -1, 2 * width), far_groups())
    gate_grad, up_grad, down_grad = local_kernel(
        weight_grads_kernel,
        [shape(w.shape, bf16) for w in weights],
        [core] + masks + [both_in, mid, parcel, scale_lanes],
        4,
        flops,
    )
    output, input_grad = local_kernel(
        finish_kernel, [shape((own_tokens, width), bf16)] * 2, [back, slope]
    )
    return (output, input_grad, gate_grad, up_grad, down_grad)


def solution(mesh):
    fine = Mesh(mesh.devices.reshape(N_Z, N_CORE, N_X, N_Y), ROW + COL)
    placed = (
        P(COL, ROW),
        P(ROW),
        P(ROW, COL),
        P(ROW, COL),
        P(COL, ROW),
        P(ROW, COL),
        P(ROW, COL),
        P(COL, ROW),
        P(COL, ROW),
    )
    return jax.shard_map(
        per_device,
        mesh=fine,
        in_specs=placed,
        out_specs=(
            P(COL, ROW),
            P(COL, ROW),
            P(ROW, COL),
            P(ROW, COL),
            P(COL, ROW),
        ),
        check_vma=False,
    )
```

time: 155 us -> 153 us (0.987)
    ppermute x2, waiting for transfers between devices: 2.99 us -> 0.01 us  [swap_cores(): return lax.ppermute(block, 'core', [(0, 1), (1, 0)])]
    all_to_all x4, blocking collectives: 65.6 us -> 67.9 us  [exchange_in(): lax.all_to_all(parts, PLANE, 0, 0, axis_index_groups=groups, tiled=True)]
    all_to_all x1, waiting for transfers between devices: 4.11 us -> 6.41 us  [exchange(): return lax.all_to_all(parts, axis, 0, 0, tiled=True)]
    pallas_call x12 -> x10, Pallas kernels: 11 us -> 9.78 us  [local_kernel(): pl.pallas_call(body, out_shape=outs if len(outs) > 1 else outs[0], in_spe...]
  transfers between devices with their start and end apart: 3 -> 3, of which waited for: 3 -> 1; matrix products, arithmetic and copies ran while one was open for 1% -> 0% of each run, Pallas kernels for 3% -> 2%
where the time goes in v6:
time: 153 us; the launch traced here: 152 us
  blocking collectives  119 us (78%)
  starting transfers between devices  15.9 us (10%)
  Pallas kernels  9.78 us (6%)
  waiting for transfers between devices  6.42 us (4%)
    all_to_all x4, blocking collectives, exchange_in(): lax.all_to_all(parts, PLANE, 0, 0, axis_index_groups=groups, tiled=True)  67.9 us
    all_to_all x2, blocking collectives, exchange(): return lax.all_to_all(parts, axis, 0, 0, tiled=True)  51 us
    all_to_all x1, starting transfers between devices, exchange(): return lax.all_to_all(parts, axis, 0, 0, tiled=True)  12 us
    pallas_call x10, Pallas kernels, local_kernel(): pl.pallas_call(body, out_shape=outs if len(outs) > 1 else outs[0], in_spe...  9.78 us
    all_to_all x1, waiting for transfers between devices, exchange(): return lax.all_to_all(parts, axis, 0, 0, tiled=True)  6.41 us
    ppermute x2, starting transfers between devices, swap_cores(): return lax.ppermute(block, 'core', [(0, 1), (1, 0)])  3.96 us
  transfers between devices with their start and end apart: 3, of which 1 were waited for; matrix products, arithmetic and copies ran while one was open for 0% of the time, Pallas kernels for 2%

profile of v6, /device:TPU:1, one launch (start us, length us, event | category | flops | bytes accessed | tf_op | source)
XLA Modules:
  0.0 151.9 jit_solution(16477376386794641012)
XLA Ops:
  0.6 1.5 shard_map.128
  2.1 0.0 copy-start.2
  2.1 0.0 copy-start.3
  2.1 0.0 copy-start.7
  2.1 12.0 %all-to-all-start = ((f32[16,16,128]{2,1,0:T(8,128)}), f32[16,16,128]{2,1,0:T(8,128)S(1)}, u32[]{:S(2)}, u32[]{:S(2)}) async-start(f32[16,16,128]{2,1,0:T(8,128)} %get-tuple-element.26), calls=%async_computation | async-start | bytes 262144 | tf_op jit(solution)/shard_map/all_to_all | solution.py:46
  14.1 2.7 %shard_map.129 = (bf16[512,1536]{1,0:T(8,128)(2,1)}, f32[512,128]{1,0:T(8,128)}) custom-call(s32[4,4]{1,0:T(4,128)} %gate_mask.3, s32[4,4]{1,0:T(4,128)} %up_mask.3, s32[4,4]{1,0:T(4,128)} %down_mask.3, f32[1,512]{1,0:T(1,128)} %get-tuple-element.27.scales, bf16[512,512]{1,0:T(8,128)(2,1)} %gate.1, bf16[512,512]{1,0:T(8,128)(2,1)} %up.1, bf16[512,512]{1,0:T(8,128)(2,1)} %down.1), custom_call_target="tpu_custom_call" | custom-call | bytes 3410112 | tf_op jit(solution)/shard_map/pallas_call | solution.py:96
  16.9 6.4 %all-to-all-done.squares = f32[16,16,128]{2,1,0:T(8,128)S(1)} async-done(((f32[16,16,128]{2,1,0:T(8,128)}), f32[16,16,128]{2,1,0:T(8,128)S(1)}, u32[]{:S(2)}, u32[]{:S(2)}) %all-to-all-start) | async-done | bytes 131104 | tf_op jit(solution)/shard_map/all_to_all | solution.py:46
  23.3 1.9 %collective-permute-start = (bf16[512,1536]{1,0:T(8,128)(2,1)}, bf16[512,1536]{1,0:T(8,128)(2,1)S(1)}, u32[]{:S(2)}, u32[]{:S(2)}) collective-permute-start(bf16[512,1536]{1,0:T(8,128)(2,1)} %get-tuple-element.33.own_weights), channel_id=1, source_target_pairs={{0,32},{32,0},{1,33},{33,1},{2,34},{34,2},{3,35},{35,3},{4,36},{36... | collective-permute-start | bytes 4718600 | tf_op jit(solution)/shard_map/ppermute | solution.py:42
  25.2 0.0 copy-done.2
  25.2 0.0 copy-done.3
  25.2 0.0 copy-done.7
  25.2 0.1 shard_map.130
  25.4 23.6 %all_to_all.35 = bf16[16,8,1024]{2,1,0:T(8,128)(2,1)S(1)} all-to-all(bf16[16,8,1024]{2,1,0:T(8,128)(2,1)S(1)} %get-tuple-element.32), channel_id=1, replica_groups={{0,2,4,6,16,18,20,22,32,34,36,38,48,50,52,54},{1,3,5,7,17,19,21,23,33,3..., dimensions={0} | all-to-all | bytes 524288 | tf_op jit(solution)/shard_map/all_to_all | solution.py:78
  48.9 0.0 collective-permute-done.other_weights
  48.9 0.1 shard_map.131
  49.0 13.8 %all_to_all.36 = bf16[4,64,2048]{2,1,0:T(8,128)(2,1)S(1)} all-to-all(bf16[4,64,2048]{2,1,0:T(8,128)(2,1)S(1)} %shard_map.131), channel_id=1, replica_groups={{0,1,8,9},{2,3,10,11},{4,5,12,13},{6,7,14,15},{16,17,24,25},{18,19,26,2..., dimensions={0} | all-to-all | bytes 2097152 | tf_op jit(solution)/shard_map/all_to_all | solution.py:78
  62.8 0.0 copy-done
  62.8 1.0 shard_map.132
  63.8 25.0 %all_to_all.37.parts = bf16[8,32,1536]{2,1,0:T(8,128)(2,1)S(1)} all-to-all(bf16[8,32,1536]{2,1,0:T(8,128)(2,1)S(1)} %bitcast.13), channel_id=1, replica_groups=mesh['z'=8,'core'=2,'x'=4,'y'=8] {'z'}, dimensions={0} | all-to-all | bytes 1572864 | tf_op jit(solution)/shard_map/all_to_all | solution.py:46
  88.8 0.2 shard_map.133
  88.9 26.1 %all_to_all.38 = bf16[8,32,1536]{2,1,0:T(8,128)(2,1)S(1)} all-to-all(bf16[8,32,1536]{2,1,0:T(8,128)(2,1)S(1)} %shard_map.133), channel_id=1, replica_groups=mesh['z'=8,'core'=2,'x'=4,'y'=8] {'z'}, dimensions={0} | all-to-all | bytes 1572864 | tf_op jit(solution)/shard_map/all_to_all | solution.py:46
  115.0 1.0 shard_map.134
  116.0 13.6 %all_to_all.39.parts = bf16[4,64,2048]{2,1,0:T(8,128)(2,1)S(1)} all-to-all(bf16[4,64,2048]{2,1,0:T(8,128)(2,1)S(1)} %bitcast.16), channel_id=1, replica_groups={{0,1,8,9},{2,3,10,11},{4,5,12,13},{6,7,14,15},{16,17,24,25},{18,19,26,2..., dimensions={0} | all-to-all | bytes 2097152 | tf_op jit(solution)/shard_map/all_to_all | solution.py:78
  129.6 2.1 %collective-permute-start.1 = (bf16[256,2560]{1,0:T(8,128)(2,1)S(1)}, bf16[256,2560]{1,0:T(8,128)(2,1)S(1)}, u32[]{:S(2)}, u32[]{:S(2)}) collective-permute-start(bf16[256,2560]{1,0:T(8,128)(2,1)S(1)} %get-tuple-element.42), channel_id=1, source_target_pairs={{0,32},{32,0},{1,33},{33,1},{2,34},{34,2},{3,35},{35,3},{4,36},{36... | collective-permute-start | bytes 3932168 | tf_op jit(solution)/shard_map/ppermute | solution.py:42
  131.7 0.1 shard_map.135
  131.8 17.0 %all_to_all.40.parts = bf16[16,8,1024]{2,1,0:T(8,128)(2,1)S(1)} all-to-all(bf16[16,8,1024]{2,1,0:T(8,128)(2,1)S(1)} %bitcast.15), channel_id=1, replica_groups={{0,2,4,6,16,18,20,22,32,34,36,38,48,50,52,54},{1,3,5,7,17,19,21,23,33,3..., dimensions={0} | all-to-all | bytes 524288 | tf_op jit(solution)/shard_map/all_to_all | solution.py:78
  148.8 0.6 shard_map.136
  149.4 0.0 collective-permute-done.1.parcel
  149.4 0.0 copy-done.1
  149.4 0.0 copy-done.4
  149.4 0.0 copy-done.5
  149.4 2.5 %shard_map.137 = (bf16[512,512]{1,0:T(8,128)(2,1)}, bf16[512,512]{1,0:T(8,128)(2,1)}, bf16[512,512]{1,0:T(8,128)(2,1)}) custom-call(s32[1]{0:T(128)} %bitcast.core, s32[4,4]{1,0:T(4,128)S(1)} %copy-done.4, s32[4,4]{1,0:T(4,128)S(1)} %copy-done.5, s32[4,4]{1,0:T(4,128)S(1)} %copy-done.6, bf16[256,2048]{1,0:T(8,128)(2,1)S(1)} %bitcast.10, ...), custom_call_target="tpu_custom_call" | custom-call | flops 805306368 | bytes 4980932 | tf_op jit(solution)/shard_map/pallas_call | solution.py:96
  (6 shorter events, 0.0 us)
Async XLA Ops:
  2.1 23.1 %copy-start.2 = (f32[16,512]{1,0:T(8,128)S(1)}, f32[16,512]{1,0:T(8,128)}, u32[]{:S(2)}) copy-start(f32[16,512]{1,0:T(8,128)} %get-tuple-element.30.smoothed) | copy-start | bytes 98308
  2.1 23.1 %copy-start.3 = (bf16[16,512]{1,0:T(8,128)(2,1)S(1)}, bf16[16,512]{1,0:T(8,128)(2,1)}, u32[]{:S(2)}) copy-start(bf16[16,512]{1,0:T(8,128)(2,1)} %get-tuple-element.31.cotangent) | copy-start | bytes 49156
  2.1 23.1 %copy-start.7 = (f32[1,512]{1,0:T(1,128)S(1)}, f32[1,512]{1,0:T(1,128)}, u32[]{:S(2)}) copy-start(f32[1,512]{1,0:T(1,128)} %get-tuple-element.27.scales) | copy-start | bytes 6148
  2.1 21.1 %all-to-all-start = ((f32[16,16,128]{2,1,0:T(8,128)}), f32[16,16,128]{2,1,0:T(8,128)S(1)}, u32[]{:S(2)}, u32[]{:S(2)}) async-start(f32[16,16,128]{2,1,0:T(8,128)} %get-tuple-element.26), calls=%async_computation | async-start | bytes 262144 | tf_op jit(solution)/shard_map/all_to_all | solution.py:46
  23.3 25.7 %collective-permute-start = (bf16[512,1536]{1,0:T(8,128)(2,1)}, bf16[512,1536]{1,0:T(8,128)(2,1)S(1)}, u32[]{:S(2)}, u32[]{:S(2)}) collective-permute-start(bf16[512,1536]{1,0:T(8,128)(2,1)} %get-tuple-element.33.own_weights), channel_id=1, source_target_pairs={{0,32},{32,0},{1,33},{33,1},{2,34},{34,2},{3,35},{35,3},{4,36},{36... | collective-permute-start | bytes 4718600 | tf_op jit(solution)/shard_map/ppermute | solution.py:42
  48.9 13.8 %copy-start = (bf16[512,1536]{1,0:T(8,128)(2,1)S(1)}, bf16[512,1536]{1,0:T(8,128)(2,1)}, u32[]{:S(2)}) copy-start(bf16[512,1536]{1,0:T(8,128)(2,1)} %get-tuple-element.33.own_weights) | copy-start | bytes 4718596
  129.6 19.8 %copy-start.1 = (f32[512,128]{1,0:T(8,128)S(1)}, f32[512,128]{1,0:T(8,128)}, u32[]{:S(2)}) copy-start(f32[512,128]{1,0:T(8,128)} %get-tuple-element.43.scales) | copy-start | bytes 786436
  129.6 19.8 %copy-start.4 = (s32[4,4]{1,0:T(4,128)S(1)}, s32[4,4]{1,0:T(4,128)}, u32[]{:S(2)}) copy-start(s32[4,4]{1,0:T(4,128)} %gate_mask.3) | copy-start | bytes 196
  129.6 19.8 %copy-start.5 = (s32[4,4]{1,0:T(4,128)S(1)}, s32[4,4]{1,0:T(4,128)}, u32[]{:S(2)}) copy-start(s32[4,4]{1,0:T(4,128)} %up_mask.3) | copy-start | bytes 196
  129.6 19.8 %copy-start.6 = (s32[4,4]{1,0:T(4,128)S(1)}, s32[4,4]{1,0:T(4,128)}, u32[]{:S(2)}) copy-start(s32[4,4]{1,0:T(4,128)} %down_mask.3) | copy-start | bytes 196
  129.6 19.8 %collective-permute-start.1 = (bf16[256,2560]{1,0:T(8,128)(2,1)S(1)}, bf16[256,2560]{1,0:T(8,128)(2,1)S(1)}, u32[]{:S(2)}, u32[]{:S(2)}) collective-permute-start(bf16[256,2560]{1,0:T(8,128)(2,1)S(1)} %get-tuple-element.42), channel_id=1, source_target_pairs={{0,32},{32,0},{1,33},{33,1},{2,34},{34,2},{3,35},{35,3},{4,36},{36... | collective-permute-start | bytes 3932168 | tf_op jit(solution)/shard_map/ppermute | solution.py:42

commit v7 on v6

--- a/solution.py
+++ b/solution.py
@@ -251,11 +251,15 @@
             copies[i, :, k * width : (k + 1) * width] = rounded
 
 
-def back_kernel(core, both_in, mid, own_weights, other_weights, back, parcel):
+def parcel_kernel(core, both_in, mid, parcel):
+    width = both_in.shape[1] // 4
+    parcel[:, : 2 * width] = both_in[:, lanes_of(1 - core[0], 0, width, 2)]
+    parcel[:, 2 * width :] = mid[...]
+
+
+def back_kernel(core, mid, own_weights, other_weights, back):
     width = own_weights.shape[0]
     split = mid.shape[1] - width
-    parcel[:, : 2 * width] = both_in[:, lanes_of(1 - core[0], 0, width, 2)]
-    parcel[:, 2 * width :] = mid[...]
     for place, weights in ((core[0], own_weights), (1 - core[0], other_weights)):
         output = matmul(mid[:, split:], weights[:, split:])
         back[:, lanes_of(place, 0, width)] = output.astype(back.dtype)
@@ -388,18 +392,20 @@
     parts = exchange(sums.reshape(N_Z, mid_tokens, -1), "z")
     mid = local_kernel(swiglu_kernel, [shape(parts.shape, bf16)], [parts])
     mid = exchange(mid, "z").reshape(half_tokens, -1)
-    back, parcel = local_kernel(
+    back = local_kernel(
         back_kernel,
-        [
-            shape((half_tokens, 4 * width), bf16),
-            shape((half_tokens, 2 * width + 3 * hidden_width), bf16),
-        ],
-        [core, both_in, mid, own_weights, other_weights],
+        [shape((half_tokens, 4 * width), bf16)],
+        [core, mid, own_weights, other_weights],
         1,
         flops,
     )
+    parcel = local_kernel(
+        parcel_kernel,
+        [shape((half_tokens, 2 * width + 3 * hidden_width), bf16)],
+        [core, both_in, mid],
+        1,
+    )
     back = exchange_in(back.reshape(N_NEAR, half_tokens // N_NEAR, -1), near_groups())
-    back, parcel = lax.optimization_barrier((back, parcel))
     parcel = swap_cores(parcel)
     back = local_kernel(
         add_kernel, [shape((N_CORE, half_tokens // N_NEAR, 2 * width), bf16)], [back]

time: 153 us -> 150 us (0.980)
  blocking collectives: 119 us -> 88.4 us
  waiting for transfers between devices: 6.42 us -> 23.4 us
  starting transfers between devices: 15.9 us -> 23.6 us
  Pallas kernels: 9.78 us -> 13.4 us
    all_to_all x4 -> x2, blocking collectives: 67.9 us -> 37.3 us  [exchange_in(): lax.all_to_all(parts, PLANE, 0, 0, axis_index_groups=groups, tiled=True)]
    all_to_all x0 -> x2, waiting for transfers between devices: none -> 17 us  [exchange_in(): lax.all_to_all(parts, PLANE, 0, 0, axis_index_groups=groups, tiled=True)]
    all_to_all x0 -> x2, starting transfers between devices: none -> 7.25 us  [exchange_in(): lax.all_to_all(parts, PLANE, 0, 0, axis_index_groups=groups, tiled=True)]
    pallas_call x10 -> x11, Pallas kernels: 9.78 us -> 13.4 us  [local_kernel(): pl.pallas_call(body, out_shape=outs if len(outs) > 1 else outs[0], in_spe...]
  transfers between devices with their start and end apart: 3 -> 5, of which waited for: 1 -> 3; matrix products, arithmetic and copies ran while one was open for 0% -> 0% of each run, Pallas kernels for 2% -> 5%
where the time goes in v7:
time: 150 us
  blocking collectives  88.4 us (59%)
  starting transfers between devices  23.6 us (16%)
  waiting for transfers between devices  23.4 us (16%)
  Pallas kernels  13.4 us (9%)
    all_to_all x2, blocking collectives, exchange(): return lax.all_to_all(parts, axis, 0, 0, tiled=True)  51 us
    all_to_all x2, blocking collectives, exchange_in(): lax.all_to_all(parts, PLANE, 0, 0, axis_index_groups=groups, tiled=True)  37.3 us
    all_to_all x2, waiting for transfers between devices, exchange_in(): lax.all_to_all(parts, PLANE, 0, 0, axis_index_groups=groups, tiled=True)  17 us
    pallas_call x11, Pallas kernels, local_kernel(): pl.pallas_call(body, out_shape=outs if len(outs) > 1 else outs[0], in_spe...  13.4 us
    all_to_all x1, starting transfers between devices, exchange(): return lax.all_to_all(parts, axis, 0, 0, tiled=True)  12 us
    all_to_all x2, starting transfers between devices, exchange_in(): lax.all_to_all(parts, PLANE, 0, 0, axis_index_groups=groups, tiled=True)  7.25 us
    all_to_all x1, waiting for transfers between devices, exchange(): return lax.all_to_all(parts, axis, 0, 0, tiled=True)  6.41 us
    ppermute x2, starting transfers between devices, swap_cores(): return lax.ppermute(block, 'core', [(0, 1), (1, 0)])  4.37 us
  transfers between devices with their start and end apart: 5, of which 3 were waited for; matrix products, arithmetic and copies ran while one was open for 0% of the time, Pallas kernels for 5%

profile of v7, /device:TPU:1, one launch (start us, length us, event | category | flops | bytes accessed | tf_op | source)
XLA Modules:
  0.0 149.6 jit_solution(793517119001018011)
XLA Ops:
  0.6 1.5 shard_map.128
  2.1 0.0 copy-start.2
  2.1 0.0 copy-start.3
  2.1 0.0 copy-start.7
  2.1 12.0 %all-to-all-start = ((f32[16,16,128]{2,1,0:T(8,128)}), f32[16,16,128]{2,1,0:T(8,128)S(1)}, u32[]{:S(2)}, u32[]{:S(2)}) async-start(f32[16,16,128]{2,1,0:T(8,128)} %get-tuple-element.22), calls=%async_computation | async-start | bytes 262144 | tf_op jit(solution)/shard_map/all_to_all | solution.py:46
  14.1 2.7 %shard_map.129 = (bf16[512,1536]{1,0:T(8,128)(2,1)}, f32[512,128]{1,0:T(8,128)}) custom-call(s32[4,4]{1,0:T(4,128)} %gate_mask.3, s32[4,4]{1,0:T(4,128)} %up_mask.3, s32[4,4]{1,0:T(4,128)} %down_mask.3, f32[1,512]{1,0:T(1,128)} %get-tuple-element.23.scales, bf16[512,512]{1,0:T(8,128)(2,1)} %gate.1, bf16[512,512]{1,0:T(8,128)(2,1)} %up.1, bf16[512,512]{1,0:T(8,128)(2,1)} %down.1), custom_call_target="tpu_custom_call" | custom-call | bytes 3410112 | tf_op jit(solution)/shard_map/pallas_call | solution.py:96
  16.9 6.4 %all-to-all-done.squares = f32[16,16,128]{2,1,0:T(8,128)S(1)} async-done(((f32[16,16,128]{2,1,0:T(8,128)}), f32[16,16,128]{2,1,0:T(8,128)S(1)}, u32[]{:S(2)}, u32[]{:S(2)}) %all-to-all-start) | async-done | bytes 131104 | tf_op jit(solution)/shard_map/all_to_all | solution.py:46
  23.3 1.9 %collective-permute-start = (bf16[512,1536]{1,0:T(8,128)(2,1)}, bf16[512,1536]{1,0:T(8,128)(2,1)S(1)}, u32[]{:S(2)}, u32[]{:S(2)}) collective-permute-start(bf16[512,1536]{1,0:T(8,128)(2,1)} %get-tuple-element.29.own_weights), channel_id=1, source_target_pairs={{0,32},{32,0},{1,33},{33,1},{2,34},{34,2},{3,35},{35,3},{4,36},{36... | collective-permute-start | bytes 4718600 | tf_op jit(solution)/shard_map/ppermute | solution.py:42
  25.2 0.0 copy-done.2
  25.2 0.0 copy-done.3
  25.2 0.0 copy-done.7
  25.2 0.1 shard_map.130
  25.4 23.6 %all_to_all.35 = bf16[16,8,1024]{2,1,0:T(8,128)(2,1)S(1)} all-to-all(bf16[16,8,1024]{2,1,0:T(8,128)(2,1)S(1)} %get-tuple-element.28), channel_id=1, replica_groups={{0,2,4,6,16,18,20,22,32,34,36,38,48,50,52,54},{1,3,5,7,17,19,21,23,33,3..., dimensions={0} | all-to-all | bytes 524288 | tf_op jit(solution)/shard_map/all_to_all | solution.py:78
  48.9 0.0 collective-permute-done.other_weights
  48.9 0.1 shard_map.131
  49.0 13.8 %all_to_all.36 = bf16[4,64,2048]{2,1,0:T(8,128)(2,1)S(1)} all-to-all(bf16[4,64,2048]{2,1,0:T(8,128)(2,1)S(1)} %shard_map.131), channel_id=1, replica_groups={{0,1,8,9},{2,3,10,11},{4,5,12,13},{6,7,14,15},{16,17,24,25},{18,19,26,2..., dimensions={0} | all-to-all | bytes 2097152 | tf_op jit(solution)/shard_map/all_to_all | solution.py:78
  62.8 0.0 copy-done
  62.8 1.0 shard_map.132
  63.8 25.0 %all_to_all.37.parts = bf16[8,32,1536]{2,1,0:T(8,128)(2,1)S(1)} all-to-all(bf16[8,32,1536]{2,1,0:T(8,128)(2,1)S(1)} %bitcast.14), channel_id=1, replica_groups=mesh['z'=8,'core'=2,'x'=4,'y'=8] {'z'}, dimensions={0} | all-to-all | bytes 1572864 | tf_op jit(solution)/shard_map/all_to_all | solution.py:46
  88.8 0.2 shard_map.133
  88.9 26.1 %all_to_all.38 = bf16[8,32,1536]{2,1,0:T(8,128)(2,1)S(1)} all-to-all(bf16[8,32,1536]{2,1,0:T(8,128)(2,1)S(1)} %shard_map.133), channel_id=1, replica_groups=mesh['z'=8,'core'=2,'x'=4,'y'=8] {'z'}, dimensions={0} | all-to-all | bytes 1572864 | tf_op jit(solution)/shard_map/all_to_all | solution.py:46
  115.0 2.0 %shard_map.134 = bf16[256,2048]{1,0:T(8,128)(2,1)} custom-call(s32[1]{0:T(128)} %bitcast.core, bf16[256,1536]{1,0:T(8,128)(2,1)S(1)} %bitcast.11, bf16[512,1536]{1,0:T(8,128)(2,1)S(1)} %copy-done, bf16[512,1536]{1,0:T(8,128)(2,1)S(1)} %collective-permute-done.other_weights), custom_call_target="tpu_custom_call" | custom-call | flops 805306368 | bytes 4980740 | tf_op jit(solution)/shard_map/pallas_call | solution.py:96
  116.9 3.5 %all-to-all-start.5 = ((bf16[4,64,2048]{2,1,0:T(8,128)(2,1)}), bf16[4,64,2048]{2,1,0:T(8,128)(2,1)S(1)}, u32[]{:S(2)}, u32[]{:S(2)}) async-start(bf16[4,64,2048]{2,1,0:T(8,128)(2,1)} %bitcast.6), calls=%async_computation.5 | async-start | bytes 2097152 | tf_op jit(solution)/shard_map/all_to_all | solution.py:78
  120.5 1.2 shard_map.137
  121.6 2.5 %collective-permute-start.1 = (bf16[256,2560]{1,0:T(8,128)(2,1)}, bf16[256,2560]{1,0:T(8,128)(2,1)}, u32[]{:S(2)}, u32[]{:S(2)}) collective-permute-start(bf16[256,2560]{1,0:T(8,128)(2,1)} %shard_map.137), channel_id=1, source_target_pairs={{0,32},{32,0},{1,33},{33,1},{2,34},{34,2},{3,35},{35,3},{4,36},{36... | collective-permute-start | bytes 3932168 | tf_op jit(solution)/shard_map/ppermute | solution.py:42
  124.1 5.8 %all-to-all-done.5.parts = bf16[4,64,2048]{2,1,0:T(8,128)(2,1)S(1)} async-done(((bf16[4,64,2048]{2,1,0:T(8,128)(2,1)}), bf16[4,64,2048]{2,1,0:T(8,128)(2,1)S(1)}, u32[]{:S(2)}, u32[]{:S(2)}) %all-to-all-start.5) | async-done | bytes 1048608 | tf_op jit(solution)/shard_map/all_to_all | solution.py:78
  129.9 0.9 shard_map.135
  130.8 3.7 %all-to-all-start.6 = ((bf16[16,8,1024]{2,1,0:T(8,128)(2,1)}), bf16[16,8,1024]{2,1,0:T(8,128)(2,1)S(1)}, u32[]{:S(2)}, u32[]{:S(2)}) async-start(bf16[16,8,1024]{2,1,0:T(8,128)(2,1)} %bitcast.7), calls=%async_computation.6 | async-start | bytes 524288 | tf_op jit(solution)/shard_map/all_to_all | solution.py:78
  134.5 0.0 collective-permute-done.1.parcel
  134.5 3.3 %shard_map.138 = (bf16[512,512]{1,0:T(8,128)(2,1)}, bf16[512,512]{1,0:T(8,128)(2,1)}, bf16[512,512]{1,0:T(8,128)(2,1)}) custom-call(s32[1]{0:T(128)} %bitcast.core, s32[4,4]{1,0:T(4,128)S(1)} %copy-done.4, s32[4,4]{1,0:T(4,128)S(1)} %copy-done.5, s32[4,4]{1,0:T(4,128)S(1)} %copy-done.6, bf16[256,2048]{1,0:T(8,128)(2,1)S(1)} %bitcast.10, ...), custom_call_target="tpu_custom_call" | custom-call | flops 805306368 | bytes 4980932 | tf_op jit(solution)/shard_map/pallas_call | solution.py:96
  137.8 11.2 %all-to-all-done.6.parts = bf16[16,8,1024]{2,1,0:T(8,128)(2,1)S(1)} async-done(((bf16[16,8,1024]{2,1,0:T(8,128)(2,1)}), bf16[16,8,1024]{2,1,0:T(8,128)(2,1)S(1)}, u32[]{:S(2)}, u32[]{:S(2)}) %all-to-all-start.6) | async-done | bytes 262176 | tf_op jit(solution)/shard_map/all_to_all | solution.py:78
  149.0 0.6 shard_map.136
  (9 shorter events, 0.0 us)
Async XLA Ops:
  2.1 23.1 %copy-start.2 = (f32[16,512]{1,0:T(8,128)S(1)}, f32[16,512]{1,0:T(8,128)}, u32[]{:S(2)}) copy-start(f32[16,512]{1,0:T(8,128)} %get-tuple-element.26.smoothed) | copy-start | bytes 98308
  2.1 23.1 %copy-start.3 = (bf16[16,512]{1,0:T(8,128)(2,1)S(1)}, bf16[16,512]{1,0:T(8,128)(2,1)}, u32[]{:S(2)}) copy-start(bf16[16,512]{1,0:T(8,128)(2,1)} %get-tuple-element.27.cotangent) | copy-start | bytes 49156
  2.1 23.1 %copy-start.7 = (f32[1,512]{1,0:T(1,128)S(1)}, f32[1,512]{1,0:T(1,128)}, u32[]{:S(2)}) copy-start(f32[1,512]{1,0:T(1,128)} %get-tuple-element.23.scales) | copy-start | bytes 6148
  2.1 21.1 %all-to-all-start = ((f32[16,16,128]{2,1,0:T(8,128)}), f32[16,16,128]{2,1,0:T(8,128)S(1)}, u32[]{:S(2)}, u32[]{:S(2)}) async-start(f32[16,16,128]{2,1,0:T(8,128)} %get-tuple-element.22), calls=%async_computation | async-start | bytes 262144 | tf_op jit(solution)/shard_map/all_to_all | solution.py:46
  23.3 25.7 %collective-permute-start = (bf16[512,1536]{1,0:T(8,128)(2,1)}, bf16[512,1536]{1,0:T(8,128)(2,1)S(1)}, u32[]{:S(2)}, u32[]{:S(2)}) collective-permute-start(bf16[512,1536]{1,0:T(8,128)(2,1)} %get-tuple-element.29.own_weights), channel_id=1, source_target_pairs={{0,32},{32,0},{1,33},{33,1},{2,34},{34,2},{3,35},{35,3},{4,36},{36... | collective-permute-start | bytes 4718600 | tf_op jit(solution)/shard_map/ppermute | solution.py:42
  48.9 13.8 %copy-start = (bf16[512,1536]{1,0:T(8,128)(2,1)S(1)}, bf16[512,1536]{1,0:T(8,128)(2,1)}, u32[]{:S(2)}) copy-start(bf16[512,1536]{1,0:T(8,128)(2,1)} %get-tuple-element.29.own_weights) | copy-start | bytes 4718596
  116.9 13.0 %all-to-all-start.5 = ((bf16[4,64,2048]{2,1,0:T(8,128)(2,1)}), bf16[4,64,2048]{2,1,0:T(8,128)(2,1)S(1)}, u32[]{:S(2)}, u32[]{:S(2)}) async-start(bf16[4,64,2048]{2,1,0:T(8,128)(2,1)} %bitcast.6), calls=%async_computation.5 | async-start | bytes 2097152 | tf_op jit(solution)/shard_map/all_to_all | solution.py:78
  121.6 12.9 %copy-start.1 = (f32[512,128]{1,0:T(8,128)S(1)}, f32[512,128]{1,0:T(8,128)}, u32[]{:S(2)}) copy-start(f32[512,128]{1,0:T(8,128)} %get-tuple-element.35.scales) | copy-start | bytes 786436
  121.6 12.9 %copy-start.4 = (s32[4,4]{1,0:T(4,128)S(1)}, s32[4,4]{1,0:T(4,128)}, u32[]{:S(2)}) copy-start(s32[4,4]{1,0:T(4,128)} %gate_mask.3) | copy-start | bytes 196
  121.6 12.9 %copy-start.5 = (s32[4,4]{1,0:T(4,128)S(1)}, s32[4,4]{1,0:T(4,128)}, u32[]{:S(2)}) copy-start(s32[4,4]{1,0:T(4,128)} %up_mask.3) | copy-start | bytes 196
  121.6 12.9 %copy-start.6 = (s32[4,4]{1,0:T(4,128)S(1)}, s32[4,4]{1,0:T(4,128)}, u32[]{:S(2)}) copy-start(s32[4,4]{1,0:T(4,128)} %down_mask.3) | copy-start | bytes 196
  121.6 12.9 %collective-permute-start.1 = (bf16[256,2560]{1,0:T(8,128)(2,1)}, bf16[256,2560]{1,0:T(8,128)(2,1)}, u32[]{:S(2)}, u32[]{:S(2)}) collective-permute-start(bf16[256,2560]{1,0:T(8,128)(2,1)} %shard_map.137), channel_id=1, source_target_pairs={{0,32},{32,0},{1,33},{33,1},{2,34},{34,2},{3,35},{35,3},{4,36},{36... | collective-permute-start | bytes 3932168 | tf_op jit(solution)/shard_map/ppermute | solution.py:42
  130.8 18.2 %all-to-all-start.6 = ((bf16[16,8,1024]{2,1,0:T(8,128)(2,1)}), bf16[16,8,1024]{2,1,0:T(8,128)(2,1)S(1)}, u32[]{:S(2)}, u32[]{:S(2)}) async-start(bf16[16,8,1024]{2,1,0:T(8,128)(2,1)} %bitcast.7), calls=%async_computation.6 | async-start | bytes 524288 | tf_op jit(solution)/shard_map/all_to_all | solution.py:78

commit v8 on v7

--- a/solution.py
+++ b/solution.py
@@ -108,6 +108,11 @@
     return jax.ShapeDtypeStruct(dims, dtype)
 
 
+def on_diagonal(rows, lanes):
+    row = lax.broadcasted_iota(jnp.int32, (rows, lanes), 0)
+    return row == lax.broadcasted_iota(jnp.int32, (rows, lanes), 1)
+
+
 def squares_kernel(
     core, tokens, scales, cotangent, copies, smoothed, scales_here, cotangent_here, tokens_here, arrived
 ):
@@ -123,11 +128,9 @@
         move.wait()
     value = tokens_here[...].astype(jnp.float32) / scales_here[...]
     smoothed[...] = value
-    squares = value * value
-    lanes = copies.shape[2]
-    total = squares[:, :lanes]
-    for start in range(lanes, squares.shape[1], lanes):
-        total = total + squares[:, start : start + lanes]
+    squares = jnp.sum(value * value, axis=1, keepdims=True)
+    rows, lanes = value.shape[0], copies.shape[2]
+    total = jnp.sum(jnp.where(on_diagonal(rows, lanes), squares, 0.0), axis=0, keepdims=True)
     for i in range(copies.shape[0]):
         copies[i] = total
 
@@ -191,7 +194,8 @@
 
 def quantize_kernel(squares, smoothed, scales, cotangent, copies, slope):
     rows, width = copies.shape[1], smoothed.shape[1]
-    mean_square = jnp.sum(add_parts(squares), axis=1, keepdims=True) / D
+    total = jnp.where(on_diagonal(smoothed.shape[0], TILE), add_parts(squares), 0.0)
+    mean_square = jnp.sum(total, axis=1, keepdims=True) / D
     limits = clip_ratio * jnp.sqrt(mean_square + 1e-06)
     squashed = jnp.tanh(smoothed[...] / limits)
     quantized = limits * squashed
@@ -339,7 +343,7 @@
     squares, smoothed, scales_here, cotangent_here = local_kernel(
         squares_kernel,
         [
-            shape((N_ROW, own_tokens, TILE), f32),
+            shape((N_ROW, 1, TILE), f32),
             shape((own_tokens, width), f32),
             shape((1, width), f32),
             shape((own_tokens, width), bf16),
@@ -364,7 +368,6 @@
         + [pltpu.SemaphoreType.DMA((7,))],
     )
     squares, own_weights = lax.optimization_barrier((squares, own_weights))
-    other_weights = swap_cores(own_weights)
     copies, slope = local_kernel(
         quantize_kernel,
         [
@@ -374,11 +377,12 @@
         [squares, smoothed, scales_here, cotangent_here],
     )
     gathered = exchange_in(copies, far_groups())
-    gathered, other_weights = lax.optimization_barrier((gathered, other_weights))
     gathered = gathered.reshape(N_CORE, half_tokens // N_NEAR, 2 * width)
     copies = local_kernel(
         copy_kernel, [shape((N_NEAR, half_tokens // N_NEAR, 4 * width), bf16)], [gathered]
     )
+    copies, own_weights = lax.optimization_barrier((copies, own_weights))
+    other_weights = swap_cores(own_weights)
     both_in = exchange_in(copies, near_groups()).reshape(half_tokens, 4 * width)
 
     flops = 12 * half_tokens * width * hidden_width

time: 150 us -> 150 us (level)
  blocking collectives: 88.4 us -> 75.7 us
  waiting for transfers between devices: 23.4 us -> 28.2 us
  starting transfers between devices: 23.6 us -> 27.7 us
  local copies, waits for them, and re-layouts: 0.04 us -> 1.99 us
  Pallas kernels: 13.4 us -> 15.2 us
    all_to_all x2 -> x1, blocking collectives: 37.3 us -> 23.7 us  [exchange_in(): lax.all_to_all(parts, PLANE, 0, 0, axis_index_groups=groups, tiled=True)]
    all_to_all x2 -> x3, waiting for transfers between devices: 17 us -> 24 us  [exchange_in(): lax.all_to_all(parts, PLANE, 0, 0, axis_index_groups=groups, tiled=True)]
    all_to_all x2 -> x3, starting transfers between devices: 7.25 us -> 11.2 us  [exchange_in(): lax.all_to_all(parts, PLANE, 0, 0, axis_index_groups=groups, tiled=True)]
    all_to_all x1, waiting for transfers between devices: 6.41 us -> 4.2 us  [exchange(): return lax.all_to_all(parts, axis, 0, 0, tiled=True)]
    unnamed x16 -> x20, local copies, waits for them, and re-layouts: 0.04 us -> 1.99 us
    pallas_call x11, Pallas kernels: 13.4 us -> 15.2 us  [local_kernel(): pl.pallas_call(body, out_shape=outs if len(outs) > 1 else outs[0], in_spe...]
  transfers between devices with their start and end apart: 5 -> 6, of which waited for: 3 -> 4; matrix products, arithmetic and copies ran while one was open for 0% -> 0% of each run, Pallas kernels for 5% -> 5%
where the time goes in v8:
time: 150 us
  blocking collectives  75.7 us (50%)
  waiting for transfers between devices  28.2 us (19%)
  starting transfers between devices  27.7 us (18%)
  Pallas kernels  15.2 us (10%)
  local copies, waits for them, and re-layouts  1.99 us (1%)
    all_to_all x2, blocking collectives, exchange(): return lax.all_to_all(parts, axis, 0, 0, tiled=True)  52 us
    all_to_all x3, waiting for transfers between devices, exchange_in(): lax.all_to_all(parts, PLANE, 0, 0, axis_index_groups=groups, tiled=True)  24 us
    all_to_all x1, blocking collectives, exchange_in(): lax.all_to_all(parts, PLANE, 0, 0, axis_index_groups=groups, tiled=True)  23.7 us
    pallas_call x11, Pallas kernels, local_kernel(): pl.pallas_call(body, out_shape=outs if len(outs) > 1 else outs[0], in_spe...  15.2 us
    all_to_all x1, starting transfers between devices, exchange(): return lax.all_to_all(parts, axis, 0, 0, tiled=True)  12 us
    all_to_all x3, starting transfers between devices, exchange_in(): lax.all_to_all(parts, PLANE, 0, 0, axis_index_groups=groups, tiled=True)  11.2 us
    ppermute x2, starting transfers between devices, swap_cores(): return lax.ppermute(block, 'core', [(0, 1), (1, 0)])  4.5 us
    all_to_all x1, waiting for transfers between devices, exchange(): return lax.all_to_all(parts, axis, 0, 0, tiled=True)  4.2 us
  transfers between devices with their start and end apart: 6, of which 4 were waited for; matrix products, arithmetic and copies ran while one was open for 0% of the time, Pallas kernels for 5%

profile of v8, /device:TPU:1, one launch (start us, length us, event | category | flops | bytes accessed | tf_op | source)
XLA Modules:
  0.0 149.7 jit_solution(13246023875183930791)
XLA Ops:
  0.6 1.5 shard_map.128
  2.1 0.0 copy-start.4
  2.1 0.0 copy-start.5
  2.1 0.0 copy-start.9
  2.2 12.0 %all-to-all-start = ((f32[16,1,128]{2,1,0:T(1,128)}), f32[16,1,128]{2,1,0:T(1,128)S(1)}, u32[]{:S(2)}, u32[]{:S(2)}) async-start(f32[16,1,128]{2,1,0:T(1,128)} %get-tuple-element.22), calls=%async_computation | async-start | bytes 16384 | tf_op jit(solution)/shard_map/all_to_all | solution.py:46
  14.1 2.7 %shard_map.129 = (bf16[512,1536]{1,0:T(8,128)(2,1)}, f32[512,128]{1,0:T(8,128)}) custom-call(s32[4,4]{1,0:T(4,128)} %gate_mask.3, s32[4,4]{1,0:T(4,128)} %up_mask.3, s32[4,4]{1,0:T(4,128)} %down_mask.3, f32[1,512]{1,0:T(1,128)} %get-tuple-element.23.scales, bf16[512,512]{1,0:T(8,128)(2,1)} %gate.1, bf16[512,512]{1,0:T(8,128)(2,1)} %up.1, bf16[512,512]{1,0:T(8,128)(2,1)} %down.1), custom_call_target="tpu_custom_call" | custom-call | bytes 3410112 | tf_op jit(solution)/shard_map/pallas_call | solution.py:96
  16.9 4.2 %all-to-all-done.squares = f32[16,1,128]{2,1,0:T(1,128)S(1)} async-done(((f32[16,1,128]{2,1,0:T(1,128)}), f32[16,1,128]{2,1,0:T(1,128)S(1)}, u32[]{:S(2)}, u32[]{:S(2)}) %all-to-all-start) | async-done | bytes 8224 | tf_op jit(solution)/shard_map/all_to_all | solution.py:46
  21.1 0.0 copy-done.9
  21.1 0.1 shard_map.130
  21.2 23.7 %all_to_all.35 = bf16[16,8,1024]{2,1,0:T(8,128)(2,1)S(1)} all-to-all(bf16[16,8,1024]{2,1,0:T(8,128)(2,1)S(1)} %get-tuple-element.28), channel_id=1, replica_groups={{0,2,4,6,16,18,20,22,32,34,36,38,48,50,52,54},{1,3,5,7,17,19,21,23,33,3..., dimensions={0} | all-to-all | bytes 524288 | tf_op jit(solution)/shard_map/all_to_all | solution.py:78
  45.0 0.1 shard_map.131
  45.0 1.0 copy-done.2
  46.0 3.5 %all-to-all-start.2 = ((bf16[4,64,2048]{2,1,0:T(8,128)(2,1)}), bf16[4,64,2048]{2,1,0:T(8,128)(2,1)S(1)}, u32[]{:S(2)}, u32[]{:S(2)}) async-start(bf16[4,64,2048]{2,1,0:T(8,128)(2,1)} %copy-done.2), calls=%async_computation.2 | async-start | bytes 2097152 | tf_op jit(solution)/shard_map/all_to_all | solution.py:78
  49.6 1.9 %collective-permute-start = (bf16[512,1536]{1,0:T(8,128)(2,1)S(1)}, bf16[512,1536]{1,0:T(8,128)(2,1)}, u32[]{:S(2)}, u32[]{:S(2)}) collective-permute-start(bf16[512,1536]{1,0:T(8,128)(2,1)S(1)} %copy-done), channel_id=1, source_target_pairs={{0,32},{32,0},{1,33},{33,1},{2,34},{34,2},{3,35},{35,3},{4,36},{36... | collective-permute-start | bytes 4718600 | tf_op jit(solution)/shard_map/ppermute | solution.py:42
  51.5 7.5 %all-to-all-done.2 = bf16[4,64,2048]{2,1,0:T(8,128)(2,1)S(1)} async-done(((bf16[4,64,2048]{2,1,0:T(8,128)(2,1)}), bf16[4,64,2048]{2,1,0:T(8,128)(2,1)S(1)}, u32[]{:S(2)}, u32[]{:S(2)}) %all-to-all-start.2) | async-done | bytes 1048608 | tf_op jit(solution)/shard_map/all_to_all | solution.py:78
  59.0 0.0 collective-permute-done.other_weights
  59.0 2.4 %shard_map.132 = bf16[256,1536]{1,0:T(8,128)(2,1)S(1)} custom-call(s32[1]{0:T(128)} %bitcast.core, bf16[256,2048]{1,0:T(8,128)(2,1)S(1)} %bitcast.8, bf16[512,1536]{1,0:T(8,128)(2,1)S(1)} %copy-done, bf16[512,1536]{1,0:T(8,128)(2,1)} %collective-permute-done.other_weights), custom_call_target="tpu_custom_call" | custom-call | flops 805306368 | bytes 4980740 | tf_op jit(solution)/shard_map/pallas_call | solution.py:96
  61.4 26.0 %all_to_all.36.parts = bf16[8,32,1536]{2,1,0:T(8,128)(2,1)S(1)} all-to-all(bf16[8,32,1536]{2,1,0:T(8,128)(2,1)S(1)} %bitcast.15), channel_id=1, replica_groups=mesh['z'=8,'core'=2,'x'=4,'y'=8] {'z'}, dimensions={0} | all-to-all | bytes 1572864 | tf_op jit(solution)/shard_map/all_to_all | solution.py:46
  87.4 0.2 shard_map.133
  87.6 25.9 %all_to_all.37 = bf16[8,32,1536]{2,1,0:T(8,128)(2,1)S(1)} all-to-all(bf16[8,32,1536]{2,1,0:T(8,128)(2,1)S(1)} %shard_map.133), channel_id=1, replica_groups=mesh['z'=8,'core'=2,'x'=4,'y'=8] {'z'}, dimensions={0} | all-to-all | bytes 1572864 | tf_op jit(solution)/shard_map/all_to_all | solution.py:46
  113.5 2.4 %shard_map.134 = bf16[256,2048]{1,0:T(8,128)(2,1)S(1)} custom-call(s32[1]{0:T(128)} %bitcast.core, bf16[256,1536]{1,0:T(8,128)(2,1)S(1)} %bitcast.11, bf16[512,1536]{1,0:T(8,128)(2,1)S(1)} %copy-done, bf16[512,1536]{1,0:T(8,128)(2,1)} %collective-permute-done.other_weights), custom_call_target="tpu_custom_call" | custom-call | flops 805306368 | bytes 4980740 | tf_op jit(solution)/shard_map/pallas_call | solution.py:96
  115.9 1.0 copy-done.1
  116.9 3.5 %all-to-all-start.5 = ((bf16[4,64,2048]{2,1,0:T(8,128)(2,1)}), bf16[4,64,2048]{2,1,0:T(8,128)(2,1)S(1)}, u32[]{:S(2)}, u32[]{:S(2)}) async-start(bf16[4,64,2048]{2,1,0:T(8,128)(2,1)} %bitcast.14), calls=%async_computation.5 | async-start | bytes 2097152 | tf_op jit(solution)/shard_map/all_to_all | solution.py:78
  120.4 1.2 shard_map.137
  121.6 2.6 %collective-permute-start.1 = (bf16[256,2560]{1,0:T(8,128)(2,1)}, bf16[256,2560]{1,0:T(8,128)(2,1)}, u32[]{:S(2)}, u32[]{:S(2)}) collective-permute-start(bf16[256,2560]{1,0:T(8,128)(2,1)} %shard_map.137), channel_id=1, source_target_pairs={{0,32},{32,0},{1,33},{33,1},{2,34},{34,2},{3,35},{35,3},{4,36},{36... | collective-permute-start | bytes 3932168 | tf_op jit(solution)/shard_map/ppermute | solution.py:42
  124.2 5.7 %all-to-all-done.5.parts = bf16[4,64,2048]{2,1,0:T(8,128)(2,1)S(1)} async-done(((bf16[4,64,2048]{2,1,0:T(8,128)(2,1)}), bf16[4,64,2048]{2,1,0:T(8,128)(2,1)S(1)}, u32[]{:S(2)}, u32[]{:S(2)}) %all-to-all-start.5) | async-done | bytes 1048608 | tf_op jit(solution)/shard_map/all_to_all | solution.py:78
  129.9 0.8 shard_map.135
  130.7 4.2 %all-to-all-start.6 = ((bf16[16,8,1024]{2,1,0:T(8,128)(2,1)}), bf16[16,8,1024]{2,1,0:T(8,128)(2,1)S(1)}, u32[]{:S(2)}, u32[]{:S(2)}) async-start(bf16[16,8,1024]{2,1,0:T(8,128)(2,1)} %bitcast.7), calls=%async_computation.6 | async-start | bytes 524288 | tf_op jit(solution)/shard_map/all_to_all | solution.py:78
  135.0 0.0 collective-permute-done.1.parcel
  135.0 3.2 %shard_map.138 = (bf16[512,512]{1,0:T(8,128)(2,1)}, bf16[512,512]{1,0:T(8,128)(2,1)}, bf16[512,512]{1,0:T(8,128)(2,1)}) custom-call(s32[1]{0:T(128)} %bitcast.core, s32[4,4]{1,0:T(4,128)S(1)} %copy-done.6, s32[4,4]{1,0:T(4,128)S(1)} %copy-done.7, s32[4,4]{1,0:T(4,128)S(1)} %copy-done.8, bf16[256,2048]{1,0:T(8,128)(2,1)S(1)} %bitcast.10, ...), custom_call_target="tpu_custom_call" | custom-call | flops 805306368 | bytes 4980932 | tf_op jit(solution)/shard_map/pallas_call | solution.py:96
  138.2 10.8 %all-to-all-done.6.parts = bf16[16,8,1024]{2,1,0:T(8,128)(2,1)S(1)} async-done(((bf16[16,8,1024]{2,1,0:T(8,128)(2,1)}), bf16[16,8,1024]{2,1,0:T(8,128)(2,1)S(1)}, u32[]{:S(2)}, u32[]{:S(2)}) %all-to-all-start.6) | async-done | bytes 262176 | tf_op jit(solution)/shard_map/all_to_all | solution.py:78
  149.1 0.6 shard_map.136
  (14 shorter events, 0.0 us)
Async XLA Ops:
  2.1 19.0 %copy-start.4 = (f32[16,512]{1,0:T(8,128)S(1)}, f32[16,512]{1,0:T(8,128)}, u32[]{:S(2)}) copy-start(f32[16,512]{1,0:T(8,128)} %get-tuple-element.26.smoothed) | copy-start | bytes 98308
  2.1 18.9 %copy-start.5 = (bf16[16,512]{1,0:T(8,128)(2,1)S(1)}, bf16[16,512]{1,0:T(8,128)(2,1)}, u32[]{:S(2)}) copy-start(bf16[16,512]{1,0:T(8,128)(2,1)} %get-tuple-element.27.cotangent) | copy-start | bytes 49156
  2.1 18.9 %copy-start.9 = (f32[1,512]{1,0:T(1,128)S(1)}, f32[1,512]{1,0:T(1,128)}, u32[]{:S(2)}) copy-start(f32[1,512]{1,0:T(1,128)} %get-tuple-element.23.scales) | copy-start | bytes 6148
  2.2 18.9 %all-to-all-start = ((f32[16,1,128]{2,1,0:T(1,128)}), f32[16,1,128]{2,1,0:T(1,128)S(1)}, u32[]{:S(2)}, u32[]{:S(2)}) async-start(f32[16,1,128]{2,1,0:T(1,128)} %get-tuple-element.22), calls=%async_computation | async-start | bytes 16384 | tf_op jit(solution)/shard_map/all_to_all | solution.py:46
  45.0 4.6 %copy-start = (bf16[512,1536]{1,0:T(8,128)(2,1)S(1)}, bf16[512,1536]{1,0:T(8,128)(2,1)}, u32[]{:S(2)}) copy-start(bf16[512,1536]{1,0:T(8,128)(2,1)} %get-tuple-element.31.own_weights) | copy-start | bytes 4718596
  45.0 1.0 copy-start.2
  46.0 13.0 %all-to-all-start.2 = ((bf16[4,64,2048]{2,1,0:T(8,128)(2,1)}), bf16[4,64,2048]{2,1,0:T(8,128)(2,1)S(1)}, u32[]{:S(2)}, u32[]{:S(2)}) async-start(bf16[4,64,2048]{2,1,0:T(8,128)(2,1)} %copy-done.2), calls=%async_computation.2 | async-start | bytes 2097152 | tf_op jit(solution)/shard_map/all_to_all | solution.py:78
  49.6 9.4 %collective-permute-start = (bf16[512,1536]{1,0:T(8,128)(2,1)S(1)}, bf16[512,1536]{1,0:T(8,128)(2,1)}, u32[]{:S(2)}, u32[]{:S(2)}) collective-permute-start(bf16[512,1536]{1,0:T(8,128)(2,1)S(1)} %copy-done), channel_id=1, source_target_pairs={{0,32},{32,0},{1,33},{33,1},{2,34},{34,2},{3,35},{35,3},{4,36},{36... | collective-permute-start | bytes 4718600 | tf_op jit(solution)/shard_map/ppermute | solution.py:42
  115.9 1.0 copy-start.1
  116.9 13.0 %all-to-all-start.5 = ((bf16[4,64,2048]{2,1,0:T(8,128)(2,1)}), bf16[4,64,2048]{2,1,0:T(8,128)(2,1)S(1)}, u32[]{:S(2)}, u32[]{:S(2)}) async-start(bf16[4,64,2048]{2,1,0:T(8,128)(2,1)} %bitcast.14), calls=%async_computation.5 | async-start | bytes 2097152 | tf_op jit(solution)/shard_map/all_to_all | solution.py:78
  121.6 13.4 %copy-start.3 = (f32[512,128]{1,0:T(8,128)S(1)}, f32[512,128]{1,0:T(8,128)}, u32[]{:S(2)}) copy-start(f32[512,128]{1,0:T(8,128)} %get-tuple-element.35.scales) | copy-start | bytes 786436
  121.6 13.4 %copy-start.6 = (s32[4,4]{1,0:T(4,128)S(1)}, s32[4,4]{1,0:T(4,128)}, u32[]{:S(2)}) copy-start(s32[4,4]{1,0:T(4,128)} %gate_mask.3) | copy-start | bytes 196
  121.6 13.4 %copy-start.7 = (s32[4,4]{1,0:T(4,128)S(1)}, s32[4,4]{1,0:T(4,128)}, u32[]{:S(2)}) copy-start(s32[4,4]{1,0:T(4,128)} %up_mask.3) | copy-start | bytes 196
  121.6 13.4 %copy-start.8 = (s32[4,4]{1,0:T(4,128)S(1)}, s32[4,4]{1,0:T(4,128)}, u32[]{:S(2)}) copy-start(s32[4,4]{1,0:T(4,128)} %down_mask.3) | copy-start | bytes 196
  121.6 13.4 %collective-permute-start.1 = (bf16[256,2560]{1,0:T(8,128)(2,1)}, bf16[256,2560]{1,0:T(8,128)(2,1)}, u32[]{:S(2)}, u32[]{:S(2)}) collective-permute-start(bf16[256,2560]{1,0:T(8,128)(2,1)} %shard_map.137), channel_id=1, source_target_pairs={{0,32},{32,0},{1,33},{33,1},{2,34},{34,2},{3,35},{35,3},{4,36},{36... | collective-permute-start | bytes 3932168 | tf_op jit(solution)/shard_map/ppermute | solution.py:42
  130.7 18.3 %all-to-all-start.6 = ((bf16[16,8,1024]{2,1,0:T(8,128)(2,1)}), bf16[16,8,1024]{2,1,0:T(8,128)(2,1)S(1)}, u32[]{:S(2)}, u32[]{:S(2)}) async-start(bf16[16,8,1024]{2,1,0:T(8,128)(2,1)} %bitcast.7), calls=%async_computation.6 | async-start | bytes 524288 | tf_op jit(solution)/shard_map/all_to_all | solution.py:78

commit v9 on v8

--- a/solution.py
+++ b/solution.py
@@ -113,23 +113,38 @@
     return row == lax.broadcasted_iota(jnp.int32, (rows, lanes), 1)
 
 
-def squares_kernel(
-    core, tokens, scales, cotangent, copies, smoothed, scales_here, cotangent_here, tokens_here, arrived
-):
+def spread_kernel(core, tokens, cotangent, copies, tokens_here, cotangent_here, arrived):
     del core
     moves = [
         pltpu.make_async_copy(tokens, tokens_here, arrived.at[0]),
-        pltpu.make_async_copy(scales, scales_here, arrived.at[1]),
-        pltpu.make_async_copy(cotangent, cotangent_here, arrived.at[2]),
+        pltpu.make_async_copy(cotangent, cotangent_here, arrived.at[1]),
     ]
     for move in moves:
         move.start()
     for move in moves:
         move.wait()
-    value = tokens_here[...].astype(jnp.float32) / scales_here[...]
-    smoothed[...] = value
-    squares = jnp.sum(value * value, axis=1, keepdims=True)
-    rows, lanes = value.shape[0], copies.shape[2]
+    rows, width = copies.shape[1], tokens.shape[1]
+    for k, source in enumerate((tokens_here, cotangent_here)):
+        value = source[...].astype(jnp.float32)
+        for half in range(N_CORE):
+            block = value[half * rows : (half + 1) * rows].astype(copies.dtype)
+            for i in range(N_FAR):
+                copies[half * N_FAR + i, :, k * width : (k + 1) * width] = block
+
+
+def smoothed_of(core, blocks, scales, other_scales, place):
+    width = scales.shape[1]
+    scale = jnp.where(core[0] == place, scales[...], other_scales[...])
+    return blocks[place, :, :width].astype(jnp.float32) / scale, scale
+
+
+def squares_kernel(core, blocks, scales, other_scales, copies):
+    squares = None
+    for place in range(N_CORE):
+        value, _ = smoothed_of(core, blocks, scales, other_scales, place)
+        added = jnp.sum(value * value, axis=1, keepdims=True)
+        squares = added if squares is None else squares + added
+    rows, lanes = blocks.shape[1], copies.shape[2]
     total = jnp.sum(jnp.where(on_diagonal(rows, lanes), squares, 0.0), axis=0, keepdims=True)
     for i in range(copies.shape[0]):
         copies[i] = total
@@ -143,6 +158,7 @@
     gate,
     up,
     down,
+    order,
     weights,
     scale_lanes,
     gate_keeps,
@@ -154,6 +170,7 @@
     down_here,
     arrived,
 ):
+    del order
     sources = (gate_mask, up_mask, down_mask, scales, gate, up, down)
     places = (gate_keeps, up_keeps, down_keeps, scales_here, gate_here, up_here, down_here)
     moves = [
@@ -192,29 +209,20 @@
         weights[rows, shifted] = kept.astype(weights.dtype)
 
 
-def quantize_kernel(squares, smoothed, scales, cotangent, copies, slope):
-    rows, width = copies.shape[1], smoothed.shape[1]
-    total = jnp.where(on_diagonal(smoothed.shape[0], TILE), add_parts(squares), 0.0)
+def quantize_kernel(core, squares, blocks, scales, other_scales, copies, slope):
+    rows, width = blocks.shape[1], scales.shape[1]
+    total = jnp.where(on_diagonal(rows, TILE), add_parts(squares), 0.0)
     mean_square = jnp.sum(total, axis=1, keepdims=True) / D
     limits = clip_ratio * jnp.sqrt(mean_square + 1e-06)
-    squashed = jnp.tanh(smoothed[...] / limits)
-    quantized = limits * squashed
-    slope[...] = (1.0 - squashed * squashed) / scales[...]
-    gradient = cotangent[...].astype(jnp.float32)
-    for core in range(N_CORE):
-        own = slice(core * rows, (core + 1) * rows)
-        quantized_half = quantized[own].astype(copies.dtype)
-        gradient_half = gradient[own].astype(copies.dtype)
-        for i in range(N_FAR):
-            copies[core * N_FAR + i, :, :width] = quantized_half
-            copies[core * N_FAR + i, :, width:] = gradient_half
-
-
-def copy_kernel(blocks, copies):
-    width = blocks.shape[2]
-    for i in range(copies.shape[0]):
-        for core in range(blocks.shape[0]):
-            copies[i, :, core * width : (core + 1) * width] = blocks[core]
+    for place in range(N_CORE):
+        value, scale = smoothed_of(core, blocks, scales, other_scales, place)
+        squashed = jnp.tanh(value / limits)
+        quantized = (limits * squashed).astype(copies.dtype)
+        slope[:, place * width : (place + 1) * width] = (1.0 - squashed * squashed) / scale
+        start = 2 * place * width
+        for i in range(copies.shape[0]):
+            copies[i, :, start : start + width] = quantized
+            copies[i, :, start + width : start + 2 * width] = blocks[place, :, width:]
 
 
 def lanes_of(core, start, width, count=1):
@@ -314,18 +322,23 @@
             )
 
 
-def add_kernel(parts, totals):
-    total = add_parts(parts).astype(totals.dtype)
-    width = totals.shape[2]
+def add_kernel(parts, slope, totals):
+    total = add_parts(parts)
+    width = totals.shape[2] // 2
     for core in range(totals.shape[0]):
-        totals[core] = total[:, core * width : (core + 1) * width]
-
-
-def finish_kernel(parts, slope, output, input_grad):
+        start = 2 * core * width
+        output = total[:, start : start + width]
+        quant_grad = total[:, start + width : start + 2 * width]
+        factor = slope[:, core * width : (core + 1) * width]
+        totals[core, :, :width] = output.astype(totals.dtype)
+        totals[core, :, width:] = (quant_grad * factor).astype(totals.dtype)
+
+
+def finish_kernel(parts, output, input_grad):
     total = jnp.concatenate([add_parts(parts[:N_FAR]), add_parts(parts[N_FAR:])], axis=0)
     width = output.shape[1]
     output[...] = total[:, :width].astype(output.dtype)
-    input_grad[...] = (total[:, width:] * slope[...]).astype(input_grad.dtype)
+    input_grad[...] = total[:, width:].astype(input_grad.dtype)
 
 
 def per_device(
@@ -340,49 +353,53 @@
     core = lax.axis_index("core").astype(jnp.int32).reshape(1)
     masks = [gate_mask, up_mask, down_mask]
 
-    squares, smoothed, scales_here, cotangent_here = local_kernel(
-        squares_kernel,
-        [
-            shape((N_ROW, 1, TILE), f32),
-            shape((own_tokens, width), f32),
-            shape((1, width), f32),
-            shape((own_tokens, width), bf16),
-        ],
-        [core, tokens, scales[None, :], cotangent],
-        1,
-        stored=(1, 2, 3),
+    class_tokens = half_tokens // N_NEAR
+    copies = local_kernel(
+        spread_kernel,
+        [shape((N_CORE * N_FAR, own_tokens // N_CORE, 2 * width), bf16)],
+        [core, tokens, cotangent],
+        1,
+        stored=(1, 2),
         room=60,
-        scratch=[pltpu.VMEM((own_tokens, width), bf16), pltpu.SemaphoreType.DMA((3,))],
-    )
-    squares = exchange(squares, ROW)
+        scratch=[pltpu.VMEM(tokens.shape, bf16)] * 2 + [pltpu.SemaphoreType.DMA((2,))],
+    )
+    scale_row = scales[None, :]
     weights = (gate_weight, up_weight, down_weight)
     own_weights, scale_lanes = local_kernel(
         prepare_kernel,
         [shape((width, 3 * hidden_width), bf16), shape((width, TILE), f32)],
-        masks + [scales_here] + list(weights),
-        stored=range(7),
+        masks + [scale_row] + list(weights) + [copies],
+        stored=range(8),
         room=60,
         scratch=[pltpu.SMEM(mask.shape, mask.dtype) for mask in masks]
         + [pltpu.VMEM((1, width), f32)]
         + [pltpu.VMEM(w.shape, w.dtype) for w in weights]
         + [pltpu.SemaphoreType.DMA((7,))],
     )
-    squares, own_weights = lax.optimization_barrier((squares, own_weights))
+    blocks = exchange_in(copies, far_groups())
+    other_scales = swap_cores(scale_row)
+    blocks, own_weights, other_scales = lax.optimization_barrier(
+        (blocks, own_weights, other_scales)
+    )
+    other_weights = swap_cores(own_weights)
+    blocks = blocks.reshape(N_CORE, class_tokens, 2 * width)
+    squares = local_kernel(
+        squares_kernel,
+        [shape((N_Z, 1, TILE), f32)],
+        [core, blocks, scale_row, other_scales],
+        1,
+    )
+    squares = exchange(squares, "z")
     copies, slope = local_kernel(
         quantize_kernel,
         [
-            shape((N_CORE * N_FAR, own_tokens // N_CORE, 2 * width), bf16),
-            shape((own_tokens, width), f32),
+            shape((N_NEAR, class_tokens, 4 * width), bf16),
+            shape((class_tokens, N_CORE * width), f32),
         ],
-        [squares, smoothed, scales_here, cotangent_here],
-    )
-    gathered = exchange_in(copies, far_groups())
-    gathered = gathered.reshape(N_CORE, half_tokens // N_NEAR, 2 * width)
-    copies = local_kernel(
-        copy_kernel, [shape((N_NEAR, half_tokens // N_NEAR, 4 * width), bf16)], [gathered]
-    )
-    copies, own_weights = lax.optimization_barrier((copies, own_weights))
-    other_weights = swap_cores(own_weights)
+        [core, squares, blocks, scale_row, other_scales],
+        1,
+    )
+    copies, other_weights = lax.optimization_barrier((copies, other_weights))
     both_in = exchange_in(copies, near_groups()).reshape(half_tokens, 4 * width)
 
     flops = 12 * half_tokens * width * hidden_width
@@ -409,10 +426,10 @@
         [core, both_in, mid],
         1,
     )
-    back = exchange_in(back.reshape(N_NEAR, half_tokens // N_NEAR, -1), near_groups())
+    back = exchange_in(back.reshape(N_NEAR, class_tokens, -1), near_groups())
     parcel = swap_cores(parcel)
     back = local_kernel(
-        add_kernel, [shape((N_CORE, half_tokens // N_NEAR, 2 * width), bf16)], [back]
+        add_kernel, [shape((N_CORE, class_tokens, 2 * width), bf16)], [back, slope]
     )
     back = exchange_in(back.reshape(N_CORE * N_FAR, -1, 2 * width), far_groups())
     gate_grad, up_grad, down_grad = local_kernel(
@@ -423,7 +440,7 @@
         flops,
     )
     output, input_grad = local_kernel(
-        finish_kernel, [shape((own_tokens, width), bf16)] * 2, [back, slope]
+        finish_kernel, [shape((own_tokens, width), bf16)] * 2, [back]
     )
     return (output, input_grad, gate_grad, up_grad, down_grad)
 

time: 150 us -> 152 us (1.013)
  waiting for transfers between devices: 28.2 us -> 24.1 us
  starting transfers between devices: 27.7 us -> 31.2 us
  blocking collectives: 75.7 us -> 77.5 us
    all_to_all x3, starting transfers between devices: 11.2 us -> 23.8 us  [exchange_in(): lax.all_to_all(parts, PLANE, 0, 0, axis_index_groups=groups, tiled=True)]
    all_to_all x1 -> x0, starting transfers between devices: 12 us -> none  [exchange(): return lax.all_to_all(parts, axis, 0, 0, tiled=True)]
    all_to_all x2 -> x3, blocking collectives: 52 us -> 63.9 us  [exchange(): return lax.all_to_all(parts, axis, 0, 0, tiled=True)]
    all_to_all x1, blocking collectives: 23.7 us -> 13.6 us  [exchange_in(): lax.all_to_all(parts, PLANE, 0, 0, axis_index_groups=groups, tiled=True)]
    all_to_all x1 -> x0, waiting for transfers between devices: 4.2 us -> none  [exchange(): return lax.all_to_all(parts, axis, 0, 0, tiled=True)]
    ppermute x2 -> x3, starting transfers between devices: 4.5 us -> 7.39 us  [swap_cores(): return lax.ppermute(block, 'core', [(0, 1), (1, 0)])]
  transfers between devices with their start and end apart: 6 -> 6, of which waited for: 4 -> 3; matrix products, arithmetic and copies ran while one was open for 0% -> 0% of each run, Pallas kernels for 5% -> 6%
where the time goes in v9:
time: 152 us; the launch traced here: 151 us
  blocking collectives  77.5 us (51%)
  starting transfers between devices  31.2 us (21%)
  waiting for transfers between devices  24.1 us (16%)
  Pallas kernels  14.7 us (10%)
  local copies, waits for them, and re-layouts  2.9 us (2%)
    all_to_all x3, blocking collectives, exchange(): return lax.all_to_all(parts, axis, 0, 0, tiled=True)  63.9 us
    all_to_all x3, waiting for transfers between devices, exchange_in(): lax.all_to_all(parts, PLANE, 0, 0, axis_index_groups=groups, tiled=True)  24.1 us
    all_to_all x3, starting transfers between devices, exchange_in(): lax.all_to_all(parts, PLANE, 0, 0, axis_index_groups=groups, tiled=True)  23.8 us
    pallas_call x11, Pallas kernels, local_kernel(): pl.pallas_call(body, out_shape=outs if len(outs) > 1 else outs[0], in_spe...  14.7 us
    all_to_all x1, blocking collectives, exchange_in(): lax.all_to_all(parts, PLANE, 0, 0, axis_index_groups=groups, tiled=True)  13.6 us
    ppermute x3, starting transfers between devices, swap_cores(): return lax.ppermute(block, 'core', [(0, 1), (1, 0)])  7.39 us
  transfers between devices with their start and end apart: 6, of which 3 were waited for; matrix products, arithmetic and copies ran while one was open for 0% of the time, Pallas kernels for 6%

profile of v9, /device:TPU:1, one launch (start us, length us, event | category | flops | bytes accessed | tf_op | source)
XLA Modules:
  0.0 151.3 jit_solution(14804352846180336768)
XLA Ops:
  0.6 0.0 copy-start.5
  0.6 1.5 shard_map.128.order
  2.1 11.1 %all-to-all-start = ((bf16[16,8,1024]{2,1,0:T(8,128)(2,1)}), bf16[16,8,1024]{2,1,0:T(8,128)(2,1)S(1)}, u32[]{:S(2)}, u32[]{:S(2)}) async-start(bf16[16,8,1024]{2,1,0:T(8,128)(2,1)} %shard_map.128.order), calls=%async_computation | async-start | bytes 524288 | tf_op jit(solution)/shard_map/all_to_all | solution.py:78
  13.2 2.0 %collective-permute-start = (f32[1,512]{1,0:T(1,128)}, f32[1,512]{1,0:T(1,128)S(1)}, u32[]{:S(2)}, u32[]{:S(2)}) collective-permute-start(f32[1,512]{1,0:T(1,128)} %bitcast.18), channel_id=1, source_target_pairs={{0,32},{32,0},{1,33},{33,1},{2,34},{34,2},{3,35},{35,3},{4,36},{36... | collective-permute-start | bytes 6152 | tf_op jit(solution)/shard_map/ppermute | solution.py:42
  15.2 2.8 %shard_map.129 = (bf16[512,1536]{1,0:T(8,128)(2,1)}, f32[512,128]{1,0:T(8,128)}) custom-call(s32[4,4]{1,0:T(4,128)} %gate_mask.3, s32[4,4]{1,0:T(4,128)} %up_mask.3, s32[4,4]{1,0:T(4,128)} %down_mask.3, f32[1,512]{1,0:T(1,128)} %bitcast.19, bf16[512,512]{1,0:T(8,128)(2,1)} %gate.1, bf16[512,512]{1,0:T(8,128)(2,1)} %up.1, bf16[512,512]{1,0:T(8,128)(2,1)} %down.1, ...), custom_call_target="tpu_custom_call" | custom-call | bytes 3672256 | tf_op jit(solution)/shard_map/pallas_call | solution.py:96
  18.0 0.0 collective-permute-done.other_scales
  18.0 8.9 %all-to-all-done = bf16[16,8,1024]{2,1,0:T(8,128)(2,1)S(1)} async-done(((bf16[16,8,1024]{2,1,0:T(8,128)(2,1)}), bf16[16,8,1024]{2,1,0:T(8,128)(2,1)S(1)}, u32[]{:S(2)}, u32[]{:S(2)}) %all-to-all-start) | async-done | bytes 262176 | tf_op jit(solution)/shard_map/all_to_all | solution.py:78
  26.9 1.9 %collective-permute-start.1 = (bf16[512,1536]{1,0:T(8,128)(2,1)}, bf16[512,1536]{1,0:T(8,128)(2,1)S(1)}, u32[]{:S(2)}, u32[]{:S(2)}) collective-permute-start(bf16[512,1536]{1,0:T(8,128)(2,1)} %get-tuple-element.23.own_weights), channel_id=1, source_target_pairs={{0,32},{32,0},{1,33},{33,1},{2,34},{34,2},{3,35},{35,3},{4,36},{36... | collective-permute-start | bytes 4718600 | tf_op jit(solution)/shard_map/ppermute | solution.py:42
  28.9 0.1 shard_map.130
  29.0 16.4 %all_to_all.35.squares = f32[8,1,128]{2,1,0:T(1,128)S(1)} all-to-all(f32[8,1,128]{2,1,0:T(1,128)S(1)} %shard_map.130), channel_id=1, replica_groups=mesh['z'=8,'core'=2,'x'=4,'y'=8] {'z'}, dimensions={0} | all-to-all | bytes 8192 | tf_op jit(solution)/shard_map/all_to_all | solution.py:46
  45.4 0.2 shard_map.131
  45.6 0.0 copy-start.3
  45.6 0.0 collective-permute-done.1.other_weights
  45.6 13.6 %all_to_all.36 = bf16[4,64,2048]{2,1,0:T(8,128)(2,1)S(1)} all-to-all(bf16[4,64,2048]{2,1,0:T(8,128)(2,1)S(1)} %get-tuple-element.24), channel_id=1, replica_groups={{0,1,8,9},{2,3,10,11},{4,5,12,13},{6,7,14,15},{16,17,24,25},{18,19,26,2..., dimensions={0} | all-to-all | bytes 2097152 | tf_op jit(solution)/shard_map/all_to_all | solution.py:78
  59.2 1.0 shard_map.132
  60.2 24.7 %all_to_all.37.parts = bf16[8,32,1536]{2,1,0:T(8,128)(2,1)S(1)} all-to-all(bf16[8,32,1536]{2,1,0:T(8,128)(2,1)S(1)} %bitcast.15), channel_id=1, replica_groups=mesh['z'=8,'core'=2,'x'=4,'y'=8] {'z'}, dimensions={0} | all-to-all | bytes 1572864 | tf_op jit(solution)/shard_map/all_to_all | solution.py:46
  84.9 0.2 shard_map.133
  85.1 22.8 %all_to_all.38 = bf16[8,32,1536]{2,1,0:T(8,128)(2,1)S(1)} all-to-all(bf16[8,32,1536]{2,1,0:T(8,128)(2,1)S(1)} %shard_map.133), channel_id=1, replica_groups=mesh['z'=8,'core'=2,'x'=4,'y'=8] {'z'}, dimensions={0} | all-to-all | bytes 1572864 | tf_op jit(solution)/shard_map/all_to_all | solution.py:46
  107.9 1.0 shard_map.134
  108.9 1.0 copy-done.1
  109.9 6.3 %all-to-all-start.5 = ((bf16[4,64,2048]{2,1,0:T(8,128)(2,1)}), bf16[4,64,2048]{2,1,0:T(8,128)(2,1)}, u32[]{:S(2)}, u32[]{:S(2)}) async-start(bf16[4,64,2048]{2,1,0:T(8,128)(2,1)} %bitcast.14), calls=%async_computation.5 | async-start | bytes 2097152 | tf_op jit(solution)/shard_map/all_to_all | solution.py:78
  116.3 1.2 shard_map.137
  117.4 3.5 %collective-permute-start.2 = (bf16[256,2560]{1,0:T(8,128)(2,1)}, bf16[256,2560]{1,0:T(8,128)(2,1)}, u32[]{:S(2)}, u32[]{:S(2)}) collective-permute-start(bf16[256,2560]{1,0:T(8,128)(2,1)} %shard_map.137), channel_id=1, source_target_pairs={{0,32},{32,0},{1,33},{33,1},{2,34},{34,2},{3,35},{35,3},{4,36},{36... | collective-permute-start | bytes 3932168 | tf_op jit(solution)/shard_map/ppermute | solution.py:42
  120.9 5.2 %all-to-all-done.5.parts = bf16[4,64,2048]{2,1,0:T(8,128)(2,1)} async-done(((bf16[4,64,2048]{2,1,0:T(8,128)(2,1)}), bf16[4,64,2048]{2,1,0:T(8,128)(2,1)}, u32[]{:S(2)}, u32[]{:S(2)}) %all-to-all-start.5) | async-done | bytes 1048608 | tf_op jit(solution)/shard_map/all_to_all | solution.py:78
  126.1 0.9 copy-done.4
  127.1 2.1 %shard_map.135 = bf16[2,64,1024]{2,1,0:T(8,128)(2,1)} custom-call(bf16[4,64,2048]{2,1,0:T(8,128)(2,1)} %all-to-all-done.5.parts, f32[64,1024]{1,0:T(8,128)S(1)} %copy-done.4), custom_call_target="tpu_custom_call" | custom-call | bytes 1572864 | tf_op jit(solution)/shard_map/pallas_call | solution.py:96
  129.1 6.4 %all-to-all-start.6 = ((bf16[16,8,1024]{2,1,0:T(8,128)(2,1)}), bf16[16,8,1024]{2,1,0:T(8,128)(2,1)}, u32[]{:S(2)}, u32[]{:S(2)}) async-start(bf16[16,8,1024]{2,1,0:T(8,128)(2,1)} %bitcast.7), calls=%async_computation.6 | async-start | bytes 524288 | tf_op jit(solution)/shard_map/all_to_all | solution.py:78
  135.6 0.0 copy-start.2
  135.6 0.9 copy-done.2
  136.5 3.2 %shard_map.138 = (bf16[512,512]{1,0:T(8,128)(2,1)}, bf16[512,512]{1,0:T(8,128)(2,1)}, bf16[512,512]{1,0:T(8,128)(2,1)}) custom-call(s32[1]{0:T(128)} %bitcast.core, s32[4,4]{1,0:T(4,128)S(1)} %copy-done.6, s32[4,4]{1,0:T(4,128)S(1)} %copy-done.7, s32[4,4]{1,0:T(4,128)S(1)} %copy-done.8, bf16[256,2048]{1,0:T(8,128)(2,1)S(1)} %bitcast.10, ...), custom_call_target="tpu_custom_call" | custom-call | flops 805306368 | bytes 4980932 | tf_op jit(solution)/shard_map/pallas_call | solution.py:96
  139.8 10.0 %all-to-all-done.6.parts = bf16[16,8,1024]{2,1,0:T(8,128)(2,1)} async-done(((bf16[16,8,1024]{2,1,0:T(8,128)(2,1)}), bf16[16,8,1024]{2,1,0:T(8,128)(2,1)}, u32[]{:S(2)}, u32[]{:S(2)}) %all-to-all-start.6) | async-done | bytes 262176 | tf_op jit(solution)/shard_map/all_to_all | solution.py:78
  149.7 1.6 %shard_map.136 = (bf16[16,512]{1,0:T(8,128)(2,1)}, bf16[16,512]{1,0:T(8,128)(2,1)}) custom-call(bf16[16,8,1024]{2,1,0:T(8,128)(2,1)} %all-to-all-done.6.parts), custom_call_target="tpu_custom_call" | custom-call | bytes 294912 | tf_op jit(solution)/shard_map/pallas_call | solution.py:96
  (13 shorter events, 0.0 us)
Async XLA Ops:
  0.6 28.2 %copy-start.5 = (f32[512]{0:T(512)S(1)}, f32[512]{0:T(512)}, u32[]{:S(2)}) copy-start(f32[512]{0:T(512)} %param.10) | copy-start | bytes 6148
  2.1 24.8 %all-to-all-start = ((bf16[16,8,1024]{2,1,0:T(8,128)(2,1)}), bf16[16,8,1024]{2,1,0:T(8,128)(2,1)S(1)}, u32[]{:S(2)}, u32[]{:S(2)}) async-start(bf16[16,8,1024]{2,1,0:T(8,128)(2,1)} %shard_map.128.order), calls=%async_computation | async-start | bytes 524288 | tf_op jit(solution)/shard_map/all_to_all | solution.py:78
  13.2 4.8 %collective-permute-start = (f32[1,512]{1,0:T(1,128)}, f32[1,512]{1,0:T(1,128)S(1)}, u32[]{:S(2)}, u32[]{:S(2)}) collective-permute-start(f32[1,512]{1,0:T(1,128)} %bitcast.18), channel_id=1, source_target_pairs={{0,32},{32,0},{1,33},{33,1},{2,34},{34,2},{3,35},{35,3},{4,36},{36... | collective-permute-start | bytes 6152 | tf_op jit(solution)/shard_map/ppermute | solution.py:42
  18.0 41.2 %copy-start = (bf16[512,1536]{1,0:T(8,128)(2,1)S(1)}, bf16[512,1536]{1,0:T(8,128)(2,1)}, u32[]{:S(2)}) copy-start(bf16[512,1536]{1,0:T(8,128)(2,1)} %get-tuple-element.23.own_weights) | copy-start | bytes 4718596
  26.9 18.7 %collective-permute-start.1 = (bf16[512,1536]{1,0:T(8,128)(2,1)}, bf16[512,1536]{1,0:T(8,128)(2,1)S(1)}, u32[]{:S(2)}, u32[]{:S(2)}) collective-permute-start(bf16[512,1536]{1,0:T(8,128)(2,1)} %get-tuple-element.23.own_weights), channel_id=1, source_target_pairs={{0,32},{32,0},{1,33},{33,1},{2,34},{34,2},{3,35},{35,3},{4,36},{36... | collective-permute-start | bytes 4718600 | tf_op jit(solution)/shard_map/ppermute | solution.py:42
  45.6 14.6 %copy-start.3 = (f32[64,1024]{1,0:T(8,128)}, f32[64,1024]{1,0:T(8,128)S(1)}, u32[]{:S(2)}) copy-start(f32[64,1024]{1,0:T(8,128)S(1)} %get-tuple-element.26.slope) | copy-start | bytes 786436
  108.9 1.0 copy-start.1
  109.9 16.2 %all-to-all-start.5 = ((bf16[4,64,2048]{2,1,0:T(8,128)(2,1)}), bf16[4,64,2048]{2,1,0:T(8,128)(2,1)}, u32[]{:S(2)}, u32[]{:S(2)}) async-start(bf16[4,64,2048]{2,1,0:T(8,128)(2,1)} %bitcast.14), calls=%async_computation.5 | async-start | bytes 2097152 | tf_op jit(solution)/shard_map/all_to_all | solution.py:78
  116.2 19.3 %copy-start.6 = (s32[4,4]{1,0:T(4,128)S(1)}, s32[4,4]{1,0:T(4,128)}, u32[]{:S(2)}) copy-start(s32[4,4]{1,0:T(4,128)} %gate_mask.3) | copy-start | bytes 196
  116.2 19.3 %copy-start.7 = (s32[4,4]{1,0:T(4,128)S(1)}, s32[4,4]{1,0:T(4,128)}, u32[]{:S(2)}) copy-start(s32[4,4]{1,0:T(4,128)} %up_mask.3) | copy-start | bytes 196
  116.2 19.3 %copy-start.8 = (s32[4,4]{1,0:T(4,128)S(1)}, s32[4,4]{1,0:T(4,128)}, u32[]{:S(2)}) copy-start(s32[4,4]{1,0:T(4,128)} %down_mask.3) | copy-start | bytes 196
  117.4 18.1 %collective-permute-start.2 = (bf16[256,2560]{1,0:T(8,128)(2,1)}, bf16[256,2560]{1,0:T(8,128)(2,1)}, u32[]{:S(2)}, u32[]{:S(2)}) collective-permute-start(bf16[256,2560]{1,0:T(8,128)(2,1)} %shard_map.137), channel_id=1, source_target_pairs={{0,32},{32,0},{1,33},{33,1},{2,34},{34,2},{3,35},{35,3},{4,36},{36... | collective-permute-start | bytes 3932168 | tf_op jit(solution)/shard_map/ppermute | solution.py:42
  126.1 1.0 copy-start.4
  129.1 20.6 %all-to-all-start.6 = ((bf16[16,8,1024]{2,1,0:T(8,128)(2,1)}), bf16[16,8,1024]{2,1,0:T(8,128)(2,1)}, u32[]{:S(2)}, u32[]{:S(2)}) async-start(bf16[16,8,1024]{2,1,0:T(8,128)(2,1)} %bitcast.7), calls=%async_computation.6 | async-start | bytes 524288 | tf_op jit(solution)/shard_map/all_to_all | solution.py:78
  135.6 1.0 copy-start.2

commit v10 on v9

--- a/solution.py
+++ b/solution.py
@@ -209,16 +209,19 @@
         weights[rows, shifted] = kept.astype(weights.dtype)
 
 
-def quantize_kernel(core, squares, blocks, scales, other_scales, copies, slope):
-    rows, width = blocks.shape[1], scales.shape[1]
+def limits_of(squares, rows):
     total = jnp.where(on_diagonal(rows, TILE), add_parts(squares), 0.0)
     mean_square = jnp.sum(total, axis=1, keepdims=True) / D
-    limits = clip_ratio * jnp.sqrt(mean_square + 1e-06)
+    return clip_ratio * jnp.sqrt(mean_square + 1e-06)
+
+
+def quantize_kernel(core, squares, blocks, scales, other_scales, copies):
+    rows, width = blocks.shape[1], scales.shape[1]
+    limits = limits_of(squares, rows)
     for place in range(N_CORE):
-        value, scale = smoothed_of(core, blocks, scales, other_scales, place)
+        value, _ = smoothed_of(core, blocks, scales, other_scales, place)
         squashed = jnp.tanh(value / limits)
         quantized = (limits * squashed).astype(copies.dtype)
-        slope[:, place * width : (place + 1) * width] = (1.0 - squashed * squashed) / scale
         start = 2 * place * width
         for i in range(copies.shape[0]):
             copies[i, :, start : start + width] = quantized
@@ -322,16 +325,19 @@
             )
 
 
-def add_kernel(parts, slope, totals):
+def add_kernel(core, parts, squares, blocks, scales, other_scales, totals):
     total = add_parts(parts)
+    limits = limits_of(squares, blocks.shape[1])
     width = totals.shape[2] // 2
-    for core in range(totals.shape[0]):
-        start = 2 * core * width
+    for place in range(totals.shape[0]):
+        start = 2 * place * width
         output = total[:, start : start + width]
         quant_grad = total[:, start + width : start + 2 * width]
-        factor = slope[:, core * width : (core + 1) * width]
-        totals[core, :, :width] = output.astype(totals.dtype)
-        totals[core, :, width:] = (quant_grad * factor).astype(totals.dtype)
+        value, scale = smoothed_of(core, blocks, scales, other_scales, place)
+        squashed = jnp.tanh(value / limits)
+        factor = (1.0 - squashed * squashed) / scale
+        totals[place, :, :width] = output.astype(totals.dtype)
+        totals[place, :, width:] = (quant_grad * factor).astype(totals.dtype)
 
 
 def finish_kernel(parts, output, input_grad):
@@ -390,12 +396,9 @@
         1,
     )
     squares = exchange(squares, "z")
-    copies, slope = local_kernel(
+    copies = local_kernel(
         quantize_kernel,
-        [
-            shape((N_NEAR, class_tokens, 4 * width), bf16),
-            shape((class_tokens, N_CORE * width), f32),
-        ],
+        [shape((N_NEAR, class_tokens, 4 * width), bf16)],
         [core, squares, blocks, scale_row, other_scales],
         1,
     )
@@ -429,7 +432,9 @@
     back = exchange_in(back.reshape(N_NEAR, class_tokens, -1), near_groups())
     parcel = swap_cores(parcel)
     back = local_kernel(
-        add_kernel, [shape((N_CORE, class_tokens, 2 * width), bf16)], [back, slope]
+        add_kernel, [shape((N_CORE, class_tokens, 2 * width), bf16)],
+        [core, back, squares, blocks, scale_row, other_scales],
+        1,
     )
     back = exchange_in(back.reshape(N_CORE * N_FAR, -1, 2 * width), far_groups())
     gate_grad, up_grad, down_grad = local_kernel(

time: 152 us -> 148 us (0.974)
  local copies, waits for them, and re-layouts: 2.9 us -> 0.02 us
    unnamed x18 -> x12, local copies, waits for them, and re-layouts: 2.9 us -> 0.02 us
where the time goes in v10:
time: 148 us
  blocking collectives  77.6 us (52%)
  starting transfers between devices  30.2 us (20%)
  waiting for transfers between devices  25.2 us (17%)
  Pallas kernels  13.7 us (9%)
    all_to_all x3, blocking collectives, exchange(): return lax.all_to_all(parts, axis, 0, 0, tiled=True)  63.8 us
    all_to_all x3, waiting for transfers between devices, exchange_in(): lax.all_to_all(parts, PLANE, 0, 0, axis_index_groups=groups, tiled=True)  25.2 us
    all_to_all x3, starting transfers between devices, exchange_in(): lax.all_to_all(parts, PLANE, 0, 0, axis_index_groups=groups, tiled=True)  23.4 us
    all_to_all x1, blocking collectives, exchange_in(): lax.all_to_all(parts, PLANE, 0, 0, axis_index_groups=groups, tiled=True)  13.8 us
    pallas_call x11, Pallas kernels, local_kernel(): pl.pallas_call(body, out_shape=outs if len(outs) > 1 else outs[0], in_spe...  13.7 us
    ppermute x3, starting transfers between devices, swap_cores(): return lax.ppermute(block, 'core', [(0, 1), (1, 0)])  6.75 us
  transfers between devices with their start and end apart: 6, of which 3 were waited for; matrix products, arithmetic and copies ran while one was open for 0% of the time, Pallas kernels for 6%

profile of v10, /device:TPU:1, one launch (start us, length us, event | category | flops | bytes accessed | tf_op | source)
XLA Modules:
  0.0 147.5 jit_solution(4475101271096753114)
XLA Ops:
  0.6 0.0 copy-start.2
  0.6 1.5 shard_map.128.order
  2.1 11.1 %all-to-all-start = ((bf16[16,8,1024]{2,1,0:T(8,128)(2,1)}), bf16[16,8,1024]{2,1,0:T(8,128)(2,1)S(1)}, u32[]{:S(2)}, u32[]{:S(2)}) async-start(bf16[16,8,1024]{2,1,0:T(8,128)(2,1)} %shard_map.128.order), calls=%async_computation | async-start | bytes 524288 | tf_op jit(solution)/shard_map/all_to_all | solution.py:78
  13.2 2.0 %collective-permute-start = (f32[1,512]{1,0:T(1,128)}, f32[1,512]{1,0:T(1,128)S(1)}, u32[]{:S(2)}, u32[]{:S(2)}) collective-permute-start(f32[1,512]{1,0:T(1,128)} %bitcast.18), channel_id=1, source_target_pairs={{0,32},{32,0},{1,33},{33,1},{2,34},{34,2},{3,35},{35,3},{4,36},{36... | collective-permute-start | bytes 6152 | tf_op jit(solution)/shard_map/ppermute | solution.py:42
  15.2 2.8 %shard_map.129 = (bf16[512,1536]{1,0:T(8,128)(2,1)}, f32[512,128]{1,0:T(8,128)}) custom-call(s32[4,4]{1,0:T(4,128)} %gate_mask.3, s32[4,4]{1,0:T(4,128)} %up_mask.3, s32[4,4]{1,0:T(4,128)} %down_mask.3, f32[1,512]{1,0:T(1,128)} %bitcast.19, bf16[512,512]{1,0:T(8,128)(2,1)} %gate.1, bf16[512,512]{1,0:T(8,128)(2,1)} %up.1, bf16[512,512]{1,0:T(8,128)(2,1)} %down.1, ...), custom_call_target="tpu_custom_call" | custom-call | bytes 3672256 | tf_op jit(solution)/shard_map/pallas_call | solution.py:96
  18.0 0.0 collective-permute-done.other_scales
  18.0 8.9 %all-to-all-done = bf16[16,8,1024]{2,1,0:T(8,128)(2,1)S(1)} async-done(((bf16[16,8,1024]{2,1,0:T(8,128)(2,1)}), bf16[16,8,1024]{2,1,0:T(8,128)(2,1)S(1)}, u32[]{:S(2)}, u32[]{:S(2)}) %all-to-all-start) | async-done | bytes 262176 | tf_op jit(solution)/shard_map/all_to_all | solution.py:78
  26.9 1.9 %collective-permute-start.1 = (bf16[512,1536]{1,0:T(8,128)(2,1)}, bf16[512,1536]{1,0:T(8,128)(2,1)S(1)}, u32[]{:S(2)}, u32[]{:S(2)}) collective-permute-start(bf16[512,1536]{1,0:T(8,128)(2,1)} %get-tuple-element.20.own_weights), channel_id=1, source_target_pairs={{0,32},{32,0},{1,33},{33,1},{2,34},{34,2},{3,35},{35,3},{4,36},{36... | collective-permute-start | bytes 4718600 | tf_op jit(solution)/shard_map/ppermute | solution.py:42
  28.8 0.0 copy-done.2
  28.9 0.1 shard_map.130
  29.0 16.4 %all_to_all.35.squares = f32[8,1,128]{2,1,0:T(1,128)S(1)} all-to-all(f32[8,1,128]{2,1,0:T(1,128)S(1)} %shard_map.130), channel_id=1, replica_groups=mesh['z'=8,'core'=2,'x'=4,'y'=8] {'z'}, dimensions={0} | all-to-all | bytes 8192 | tf_op jit(solution)/shard_map/all_to_all | solution.py:46
  45.4 0.2 shard_map.131
  45.5 0.0 collective-permute-done.1.other_weights
  45.5 13.8 %all_to_all.36 = bf16[4,64,2048]{2,1,0:T(8,128)(2,1)S(1)} all-to-all(bf16[4,64,2048]{2,1,0:T(8,128)(2,1)S(1)} %shard_map.131), channel_id=1, replica_groups={{0,1,8,9},{2,3,10,11},{4,5,12,13},{6,7,14,15},{16,17,24,25},{18,19,26,2..., dimensions={0} | all-to-all | bytes 2097152 | tf_op jit(solution)/shard_map/all_to_all | solution.py:78
  59.3 0.0 copy-done
  59.3 1.0 shard_map.132
  60.3 24.7 %all_to_all.37.parts = bf16[8,32,1536]{2,1,0:T(8,128)(2,1)S(1)} all-to-all(bf16[8,32,1536]{2,1,0:T(8,128)(2,1)S(1)} %bitcast.17), channel_id=1, replica_groups=mesh['z'=8,'core'=2,'x'=4,'y'=8] {'z'}, dimensions={0} | all-to-all | bytes 1572864 | tf_op jit(solution)/shard_map/all_to_all | solution.py:46
  84.9 0.2 shard_map.133
  85.1 22.8 %all_to_all.38 = bf16[8,32,1536]{2,1,0:T(8,128)(2,1)S(1)} all-to-all(bf16[8,32,1536]{2,1,0:T(8,128)(2,1)S(1)} %shard_map.133), channel_id=1, replica_groups=mesh['z'=8,'core'=2,'x'=4,'y'=8] {'z'}, dimensions={0} | all-to-all | bytes 1572864 | tf_op jit(solution)/shard_map/all_to_all | solution.py:46
  107.9 2.0 %shard_map.134 = bf16[256,2048]{1,0:T(8,128)(2,1)} custom-call(s32[1]{0:T(128)} %bitcast.core, bf16[256,1536]{1,0:T(8,128)(2,1)S(1)} %bitcast.11, bf16[512,1536]{1,0:T(8,128)(2,1)S(1)} %copy-done, bf16[512,1536]{1,0:T(8,128)(2,1)S(1)} %collective-permute-done.1.other_weights), custom_call_target="tpu_custom_call" | custom-call | flops 805306368 | bytes 4980740 | tf_op jit(solution)/shard_map/pallas_call | solution.py:96
  109.9 6.4 %all-to-all-start.5 = ((bf16[4,64,2048]{2,1,0:T(8,128)(2,1)}), bf16[4,64,2048]{2,1,0:T(8,128)(2,1)S(1)}, u32[]{:S(2)}, u32[]{:S(2)}) async-start(bf16[4,64,2048]{2,1,0:T(8,128)(2,1)} %bitcast.6), calls=%async_computation.5 | async-start | bytes 2097152 | tf_op jit(solution)/shard_map/all_to_all | solution.py:78
  116.3 1.2 shard_map.137
  117.5 2.8 %collective-permute-start.2 = (bf16[256,2560]{1,0:T(8,128)(2,1)}, bf16[256,2560]{1,0:T(8,128)(2,1)}, u32[]{:S(2)}, u32[]{:S(2)}) collective-permute-start(bf16[256,2560]{1,0:T(8,128)(2,1)} %shard_map.137), channel_id=1, source_target_pairs={{0,32},{32,0},{1,33},{33,1},{2,34},{34,2},{3,35},{35,3},{4,36},{36... | collective-permute-start | bytes 3932168 | tf_op jit(solution)/shard_map/ppermute | solution.py:42
  120.3 5.5 %all-to-all-done.5.parts = bf16[4,64,2048]{2,1,0:T(8,128)(2,1)S(1)} async-done(((bf16[4,64,2048]{2,1,0:T(8,128)(2,1)}), bf16[4,64,2048]{2,1,0:T(8,128)(2,1)S(1)}, u32[]{:S(2)}, u32[]{:S(2)}) %all-to-all-start.5) | async-done | bytes 1048608 | tf_op jit(solution)/shard_map/all_to_all | solution.py:78
  125.8 1.0 shard_map.135
  126.8 5.9 %all-to-all-start.6 = ((bf16[16,8,1024]{2,1,0:T(8,128)(2,1)}), bf16[16,8,1024]{2,1,0:T(8,128)(2,1)S(1)}, u32[]{:S(2)}, u32[]{:S(2)}) async-start(bf16[16,8,1024]{2,1,0:T(8,128)(2,1)} %bitcast.7), calls=%async_computation.6 | async-start | bytes 524288 | tf_op jit(solution)/shard_map/all_to_all | solution.py:78
  132.8 0.0 collective-permute-done.2.parcel
  132.8 0.0 copy-done.1
  132.8 0.0 copy-done.3
  132.8 3.3 %shard_map.138 = (bf16[512,512]{1,0:T(8,128)(2,1)}, bf16[512,512]{1,0:T(8,128)(2,1)}, bf16[512,512]{1,0:T(8,128)(2,1)}) custom-call(s32[1]{0:T(128)} %bitcast.core, s32[4,4]{1,0:T(4,128)S(1)} %copy-done.3, s32[4,4]{1,0:T(4,128)S(1)} %copy-done.4, s32[4,4]{1,0:T(4,128)S(1)} %copy-done.5, bf16[256,2048]{1,0:T(8,128)(2,1)S(1)} %bitcast.10, ...), custom_call_target="tpu_custom_call" | custom-call | flops 805306368 | bytes 4980932 | tf_op jit(solution)/shard_map/pallas_call | solution.py:96
  136.1 10.8 %all-to-all-done.6.parts = bf16[16,8,1024]{2,1,0:T(8,128)(2,1)S(1)} async-done(((bf16[16,8,1024]{2,1,0:T(8,128)(2,1)}), bf16[16,8,1024]{2,1,0:T(8,128)(2,1)S(1)}, u32[]{:S(2)}, u32[]{:S(2)}) %all-to-all-start.6) | async-done | bytes 262176 | tf_op jit(solution)/shard_map/all_to_all | solution.py:78
  146.9 0.6 shard_map.136
  (7 shorter events, 0.0 us)
Async XLA Ops:
  0.6 28.2 %copy-start.2 = (f32[512]{0:T(512)S(1)}, f32[512]{0:T(512)}, u32[]{:S(2)}) copy-start(f32[512]{0:T(512)} %param.10) | copy-start | bytes 6148
  2.1 24.8 %all-to-all-start = ((bf16[16,8,1024]{2,1,0:T(8,128)(2,1)}), bf16[16,8,1024]{2,1,0:T(8,128)(2,1)S(1)}, u32[]{:S(2)}, u32[]{:S(2)}) async-start(bf16[16,8,1024]{2,1,0:T(8,128)(2,1)} %shard_map.128.order), calls=%async_computation | async-start | bytes 524288 | tf_op jit(solution)/shard_map/all_to_all | solution.py:78
  13.2 4.8 %collective-permute-start = (f32[1,512]{1,0:T(1,128)}, f32[1,512]{1,0:T(1,128)S(1)}, u32[]{:S(2)}, u32[]{:S(2)}) collective-permute-start(f32[1,512]{1,0:T(1,128)} %bitcast.18), channel_id=1, source_target_pairs={{0,32},{32,0},{1,33},{33,1},{2,34},{34,2},{3,35},{35,3},{4,36},{36... | collective-permute-start | bytes 6152 | tf_op jit(solution)/shard_map/ppermute | solution.py:42
  26.9 18.6 %collective-permute-start.1 = (bf16[512,1536]{1,0:T(8,128)(2,1)}, bf16[512,1536]{1,0:T(8,128)(2,1)S(1)}, u32[]{:S(2)}, u32[]{:S(2)}) collective-permute-start(bf16[512,1536]{1,0:T(8,128)(2,1)} %get-tuple-element.20.own_weights), channel_id=1, source_target_pairs={{0,32},{32,0},{1,33},{33,1},{2,34},{34,2},{3,35},{35,3},{4,36},{36... | collective-permute-start | bytes 4718600 | tf_op jit(solution)/shard_map/ppermute | solution.py:42
  45.4 13.9 %copy-start = (bf16[512,1536]{1,0:T(8,128)(2,1)S(1)}, bf16[512,1536]{1,0:T(8,128)(2,1)}, u32[]{:S(2)}) copy-start(bf16[512,1536]{1,0:T(8,128)(2,1)} %get-tuple-element.20.own_weights) | copy-start | bytes 4718596
  109.9 15.9 %all-to-all-start.5 = ((bf16[4,64,2048]{2,1,0:T(8,128)(2,1)}), bf16[4,64,2048]{2,1,0:T(8,128)(2,1)S(1)}, u32[]{:S(2)}, u32[]{:S(2)}) async-start(bf16[4,64,2048]{2,1,0:T(8,128)(2,1)} %bitcast.6), calls=%async_computation.5 | async-start | bytes 2097152 | tf_op jit(solution)/shard_map/all_to_all | solution.py:78
  117.5 15.3 %copy-start.1 = (f32[512,128]{1,0:T(8,128)S(1)}, f32[512,128]{1,0:T(8,128)}, u32[]{:S(2)}) copy-start(f32[512,128]{1,0:T(8,128)} %get-tuple-element.25.scales) | copy-start | bytes 786436
  117.5 15.3 %copy-start.3 = (s32[4,4]{1,0:T(4,128)S(1)}, s32[4,4]{1,0:T(4,128)}, u32[]{:S(2)}) copy-start(s32[4,4]{1,0:T(4,128)} %gate_mask.3) | copy-start | bytes 196
  117.5 15.3 %copy-start.4 = (s32[4,4]{1,0:T(4,128)S(1)}, s32[4,4]{1,0:T(4,128)}, u32[]{:S(2)}) copy-start(s32[4,4]{1,0:T(4,128)} %up_mask.3) | copy-start | bytes 196
  117.5 15.3 %copy-start.5 = (s32[4,4]{1,0:T(4,128)S(1)}, s32[4,4]{1,0:T(4,128)}, u32[]{:S(2)}) copy-start(s32[4,4]{1,0:T(4,128)} %down_mask.3) | copy-start | bytes 196
  117.5 15.3 %collective-permute-start.2 = (bf16[256,2560]{1,0:T(8,128)(2,1)}, bf16[256,2560]{1,0:T(8,128)(2,1)}, u32[]{:S(2)}, u32[]{:S(2)}) collective-permute-start(bf16[256,2560]{1,0:T(8,128)(2,1)} %shard_map.137), channel_id=1, source_target_pairs={{0,32},{32,0},{1,33},{33,1},{2,34},{34,2},{3,35},{35,3},{4,36},{36... | collective-permute-start | bytes 3932168 | tf_op jit(solution)/shard_map/ppermute | solution.py:42
  126.8 20.1 %all-to-all-start.6 = ((bf16[16,8,1024]{2,1,0:T(8,128)(2,1)}), bf16[16,8,1024]{2,1,0:T(8,128)(2,1)S(1)}, u32[]{:S(2)}, u32[]{:S(2)}) async-start(bf16[16,8,1024]{2,1,0:T(8,128)(2,1)} %bitcast.7), calls=%async_computation.6 | async-start | bytes 524288 | tf_op jit(solution)/shard_map/all_to_all | solution.py:78

commit v11 on v10

--- a/solution.py
+++ b/solution.py
@@ -232,11 +232,15 @@
     return pl.ds(pl.multiple_of(core * 2 * width + start, TILE), count * width)
 
 
-def forward_kernel(core, both_in, own_weights, other_weights, sums):
+def forward_kernel(core, both_in, own_weights, other_stored, sums, other_weights, arrived):
+    move = pltpu.make_async_copy(other_stored, other_weights, arrived)
+    move.start()
     width = own_weights.shape[0]
     split = sums.shape[1] - width
     gate_up = None
     for place, weights in ((core[0], own_weights), (1 - core[0], other_weights)):
+        if weights is other_weights:
+            move.wait()
         quantized = both_in[:, lanes_of(place, 0, width)]
         gradient = both_in[:, lanes_of(place, width, width)]
         first = matmul(quantized, weights[:, :split])
@@ -272,10 +276,14 @@
     parcel[:, 2 * width :] = mid[...]
 
 
-def back_kernel(core, mid, own_weights, other_weights, back):
+def back_kernel(core, mid, own_weights, other_stored, back, other_weights, arrived):
+    move = pltpu.make_async_copy(other_stored, other_weights, arrived)
+    move.start()
     width = own_weights.shape[0]
     split = mid.shape[1] - width
     for place, weights in ((core[0], own_weights), (1 - core[0], other_weights)):
+        if weights is other_weights:
+            move.wait()
         output = matmul(mid[:, split:], weights[:, split:])
         back[:, lanes_of(place, 0, width)] = output.astype(back.dtype)
         quant_grad = contract_last(mid[:, :split], weights[:, :split])
@@ -387,7 +395,6 @@
     blocks, own_weights, other_scales = lax.optimization_barrier(
         (blocks, own_weights, other_scales)
     )
-    other_weights = swap_cores(own_weights)
     blocks = blocks.reshape(N_CORE, class_tokens, 2 * width)
     squares = local_kernel(
         squares_kernel,
@@ -402,7 +409,8 @@
         [core, squares, blocks, scale_row, other_scales],
         1,
     )
-    copies, other_weights = lax.optimization_barrier((copies, other_weights))
+    copies, own_weights = lax.optimization_barrier((copies, own_weights))
+    other_weights = swap_cores(own_weights)
     both_in = exchange_in(copies, near_groups()).reshape(half_tokens, 4 * width)
 
     flops = 12 * half_tokens * width * hidden_width
@@ -412,6 +420,8 @@
         [core, both_in, own_weights, other_weights],
         1,
         flops,
+        stored=(3,),
+        scratch=[pltpu.VMEM(own_weights.shape, bf16), pltpu.SemaphoreType.DMA],
     )
     parts = exchange(sums.reshape(N_Z, mid_tokens, -1), "z")
     mid = local_kernel(swiglu_kernel, [shape(parts.shape, bf16)], [parts])
@@ -422,6 +432,8 @@
         [core, mid, own_weights, other_weights],
         1,
         flops,
+        stored=(3,),
+        scratch=[pltpu.VMEM(own_weights.shape, bf16), pltpu.SemaphoreType.DMA],
     )
     parcel = local_kernel(
         parcel_kernel,

time: 148 us -> 149 us (level)
  blocking collectives: 77.6 us -> 62.8 us
  waiting for transfers between devices: 25.2 us -> 32.1 us
  starting transfers between devices: 30.2 us -> 35.2 us
  local copies, waits for them, and re-layouts: 0.02 us -> 1.96 us
  Pallas kernels: 13.7 us -> 15.2 us
    all_to_all x1 -> x0, blocking collectives: 13.8 us -> none  [exchange_in(): lax.all_to_all(parts, PLANE, 0, 0, axis_index_groups=groups, tiled=True)]
    all_to_all x3 -> x4, waiting for transfers between devices: 25.2 us -> 32.1 us  [exchange_in(): lax.all_to_all(parts, PLANE, 0, 0, axis_index_groups=groups, tiled=True)]
    all_to_all x3 -> x4, starting transfers between devices: 23.4 us -> 27.8 us  [exchange_in(): lax.all_to_all(parts, PLANE, 0, 0, axis_index_groups=groups, tiled=True)]
    unnamed x12 -> x20, local copies, waits for them, and re-layouts: 0.02 us -> 1.96 us
  transfers between devices with their start and end apart: 6 -> 7, of which waited for: 3 -> 4; matrix products, arithmetic and copies ran while one was open for 0% -> 0% of each run, Pallas kernels for 6% -> 6%
where the time goes in v11:
time: 149 us; the launch traced here: 148 us
  blocking collectives  62.8 us (42%)
  starting transfers between devices  35.2 us (24%)
  waiting for transfers between devices  32.1 us (22%)
  Pallas kernels  15.2 us (10%)
  local copies, waits for them, and re-layouts  1.96 us (1%)
    all_to_all x3, blocking collectives, exchange(): return lax.all_to_all(parts, axis, 0, 0, tiled=True)  62.8 us
    all_to_all x4, waiting for transfers between devices, exchange_in(): lax.all_to_all(parts, PLANE, 0, 0, axis_index_groups=groups, tiled=True)  32.1 us
    all_to_all x4, starting transfers between devices, exchange_in(): lax.all_to_all(parts, PLANE, 0, 0, axis_index_groups=groups, tiled=True)  27.8 us
    pallas_call x11, Pallas kernels, local_kernel(): pl.pallas_call(body, out_shape=outs if len(outs) > 1 else outs[0], in_spe...  15.2 us
    ppermute x3, starting transfers between devices, swap_cores(): return lax.ppermute(block, 'core', [(0, 1), (1, 0)])  7.41 us
  transfers between devices with their start and end apart: 7, of which 4 were waited for; matrix products, arithmetic and copies ran while one was open for 0% of the time, Pallas kernels for 6%

profile of v11, /device:TPU:1, one launch (start us, length us, event | category | flops | bytes accessed | tf_op | source)
XLA Modules:
  0.0 148.1 jit_solution(15111848403721378197)
XLA Ops:
  0.6 0.0 copy-start.6
  0.6 1.5 shard_map.128.order
  2.1 11.1 %all-to-all-start = ((bf16[16,8,1024]{2,1,0:T(8,128)(2,1)}), bf16[16,8,1024]{2,1,0:T(8,128)(2,1)S(1)}, u32[]{:S(2)}, u32[]{:S(2)}) async-start(bf16[16,8,1024]{2,1,0:T(8,128)(2,1)} %shard_map.128.order), calls=%async_computation | async-start | bytes 524288 | tf_op jit(solution)/shard_map/all_to_all | solution.py:78
  13.2 2.0 %collective-permute-start = (f32[1,512]{1,0:T(1,128)}, f32[1,512]{1,0:T(1,128)S(1)}, u32[]{:S(2)}, u32[]{:S(2)}) collective-permute-start(f32[1,512]{1,0:T(1,128)} %bitcast.19), channel_id=1, source_target_pairs={{0,32},{32,0},{1,33},{33,1},{2,34},{34,2},{3,35},{35,3},{4,36},{36... | collective-permute-start | bytes 6152 | tf_op jit(solution)/shard_map/ppermute | solution.py:42
  15.2 2.7 %shard_map.129 = (bf16[512,1536]{1,0:T(8,128)(2,1)}, f32[512,128]{1,0:T(8,128)}) custom-call(s32[4,4]{1,0:T(4,128)} %gate_mask.3, s32[4,4]{1,0:T(4,128)} %up_mask.3, s32[4,4]{1,0:T(4,128)} %down_mask.3, f32[1,512]{1,0:T(1,128)} %bitcast.20, bf16[512,512]{1,0:T(8,128)(2,1)} %gate.1, bf16[512,512]{1,0:T(8,128)(2,1)} %up.1, bf16[512,512]{1,0:T(8,128)(2,1)} %down.1, ...), custom_call_target="tpu_custom_call" | custom-call | bytes 3672256 | tf_op jit(solution)/shard_map/pallas_call | solution.py:96
  18.0 0.0 collective-permute-done.other_scales
  18.0 8.9 %all-to-all-done = bf16[16,8,1024]{2,1,0:T(8,128)(2,1)S(1)} async-done(((bf16[16,8,1024]{2,1,0:T(8,128)(2,1)}), bf16[16,8,1024]{2,1,0:T(8,128)(2,1)S(1)}, u32[]{:S(2)}, u32[]{:S(2)}) %all-to-all-start) | async-done | bytes 262176 | tf_op jit(solution)/shard_map/all_to_all | solution.py:78
  26.9 0.1 shard_map.130
  27.1 16.4 %all_to_all.35.squares = f32[8,1,128]{2,1,0:T(1,128)S(1)} all-to-all(f32[8,1,128]{2,1,0:T(1,128)S(1)} %shard_map.130), channel_id=1, replica_groups=mesh['z'=8,'core'=2,'x'=4,'y'=8] {'z'}, dimensions={0} | all-to-all | bytes 8192 | tf_op jit(solution)/shard_map/all_to_all | solution.py:46
  43.4 0.2 shard_map.131
  43.6 0.0 copy-start.2
  43.6 1.0 copy-done.2
  44.6 3.5 %all-to-all-start.2 = ((bf16[4,64,2048]{2,1,0:T(8,128)(2,1)}), bf16[4,64,2048]{2,1,0:T(8,128)(2,1)S(1)}, u32[]{:S(2)}, u32[]{:S(2)}) async-start(bf16[4,64,2048]{2,1,0:T(8,128)(2,1)} %copy-done.2), calls=%async_computation.2 | async-start | bytes 2097152 | tf_op jit(solution)/shard_map/all_to_all | solution.py:78
  48.1 3.3 %collective-permute-start.1 = (bf16[512,1536]{1,0:T(8,128)(2,1)S(1)}, bf16[512,1536]{1,0:T(8,128)(2,1)}, u32[]{:S(2)}, u32[]{:S(2)}) collective-permute-start(bf16[512,1536]{1,0:T(8,128)(2,1)S(1)} %copy-done), channel_id=1, source_target_pairs={{0,32},{32,0},{1,33},{33,1},{2,34},{34,2},{3,35},{35,3},{4,36},{36... | collective-permute-start | bytes 4718600 | tf_op jit(solution)/shard_map/ppermute | solution.py:42
  51.5 6.1 %all-to-all-done.2 = bf16[4,64,2048]{2,1,0:T(8,128)(2,1)S(1)} async-done(((bf16[4,64,2048]{2,1,0:T(8,128)(2,1)}), bf16[4,64,2048]{2,1,0:T(8,128)(2,1)S(1)}, u32[]{:S(2)}, u32[]{:S(2)}) %all-to-all-start.2) | async-done | bytes 1048608 | tf_op jit(solution)/shard_map/all_to_all | solution.py:78
  57.5 0.0 collective-permute-done.1.other_stored
  57.5 2.4 %shard_map.132 = bf16[256,1536]{1,0:T(8,128)(2,1)S(1)} custom-call(s32[1]{0:T(128)} %bitcast.core, bf16[256,2048]{1,0:T(8,128)(2,1)S(1)} %bitcast.8, bf16[512,1536]{1,0:T(8,128)(2,1)S(1)} %copy-done, bf16[512,1536]{1,0:T(8,128)(2,1)} %collective-permute-done.1.other_stored), custom_call_target="tpu_custom_call" | custom-call | flops 805306368 | bytes 4980740 | tf_op jit(solution)/shard_map/pallas_call | solution.py:96
  59.9 23.5 %all_to_all.36.parts = bf16[8,32,1536]{2,1,0:T(8,128)(2,1)S(1)} all-to-all(bf16[8,32,1536]{2,1,0:T(8,128)(2,1)S(1)} %bitcast.18), channel_id=1, replica_groups=mesh['z'=8,'core'=2,'x'=4,'y'=8] {'z'}, dimensions={0} | all-to-all | bytes 1572864 | tf_op jit(solution)/shard_map/all_to_all | solution.py:46
  83.4 0.2 shard_map.133
  83.6 23.0 %all_to_all.37 = bf16[8,32,1536]{2,1,0:T(8,128)(2,1)S(1)} all-to-all(bf16[8,32,1536]{2,1,0:T(8,128)(2,1)S(1)} %shard_map.133), channel_id=1, replica_groups=mesh['z'=8,'core'=2,'x'=4,'y'=8] {'z'}, dimensions={0} | all-to-all | bytes 1572864 | tf_op jit(solution)/shard_map/all_to_all | solution.py:46
  106.6 2.0 %shard_map.134 = bf16[256,2048]{1,0:T(8,128)(2,1)S(1)} custom-call(s32[1]{0:T(128)} %bitcast.core, bf16[256,1536]{1,0:T(8,128)(2,1)S(1)} %bitcast.11, bf16[512,1536]{1,0:T(8,128)(2,1)S(1)} %copy-done, bf16[512,1536]{1,0:T(8,128)(2,1)} %collective-permute-done.1.other_stored), custom_call_target="tpu_custom_call" | custom-call | flops 805306368 | bytes 4980740 | tf_op jit(solution)/shard_map/pallas_call | solution.py:96
  108.6 1.0 copy-done.1
  109.6 9.2 %all-to-all-start.5 = ((bf16[4,64,2048]{2,1,0:T(8,128)(2,1)}), bf16[4,64,2048]{2,1,0:T(8,128)(2,1)S(1)}, u32[]{:S(2)}, u32[]{:S(2)}) async-start(bf16[4,64,2048]{2,1,0:T(8,128)(2,1)} %bitcast.14), calls=%async_computation.5 | async-start | bytes 2097152 | tf_op jit(solution)/shard_map/all_to_all | solution.py:78
  118.8 1.2 shard_map.137
  119.9 2.1 %collective-permute-start.2 = (bf16[256,2560]{1,0:T(8,128)(2,1)}, bf16[256,2560]{1,0:T(8,128)(2,1)}, u32[]{:S(2)}, u32[]{:S(2)}) collective-permute-start(bf16[256,2560]{1,0:T(8,128)(2,1)} %shard_map.137), channel_id=1, source_target_pairs={{0,32},{32,0},{1,33},{33,1},{2,34},{34,2},{3,35},{35,3},{4,36},{36... | collective-permute-start | bytes 3932168 | tf_op jit(solution)/shard_map/ppermute | solution.py:42
  122.0 6.3 %all-to-all-done.5.parts = bf16[4,64,2048]{2,1,0:T(8,128)(2,1)S(1)} async-done(((bf16[4,64,2048]{2,1,0:T(8,128)(2,1)}), bf16[4,64,2048]{2,1,0:T(8,128)(2,1)S(1)}, u32[]{:S(2)}, u32[]{:S(2)}) %all-to-all-start.5) | async-done | bytes 1048608 | tf_op jit(solution)/shard_map/all_to_all | solution.py:78
  128.3 1.0 shard_map.135
  129.3 4.0 %all-to-all-start.6 = ((bf16[16,8,1024]{2,1,0:T(8,128)(2,1)}), bf16[16,8,1024]{2,1,0:T(8,128)(2,1)S(1)}, u32[]{:S(2)}, u32[]{:S(2)}) async-start(bf16[16,8,1024]{2,1,0:T(8,128)(2,1)} %bitcast.7), calls=%async_computation.6 | async-start | bytes 524288 | tf_op jit(solution)/shard_map/all_to_all | solution.py:78
  133.3 0.0 collective-permute-done.2.parcel
  133.3 3.3 %shard_map.138 = (bf16[512,512]{1,0:T(8,128)(2,1)}, bf16[512,512]{1,0:T(8,128)(2,1)}, bf16[512,512]{1,0:T(8,128)(2,1)}) custom-call(s32[1]{0:T(128)} %bitcast.core, s32[4,4]{1,0:T(4,128)S(1)} %copy-done.7, s32[4,4]{1,0:T(4,128)S(1)} %copy-done.8, s32[4,4]{1,0:T(4,128)S(1)} %copy-done.9, bf16[256,2048]{1,0:T(8,128)(2,1)S(1)} %bitcast.10, ...), custom_call_target="tpu_custom_call" | custom-call | flops 805306368 | bytes 4980932 | tf_op jit(solution)/shard_map/pallas_call | solution.py:96
  136.6 10.8 %all-to-all-done.6.parts = bf16[16,8,1024]{2,1,0:T(8,128)(2,1)S(1)} async-done(((bf16[16,8,1024]{2,1,0:T(8,128)(2,1)}), bf16[16,8,1024]{2,1,0:T(8,128)(2,1)S(1)}, u32[]{:S(2)}, u32[]{:S(2)}) %all-to-all-start.6) | async-done | bytes 262176 | tf_op jit(solution)/shard_map/all_to_all | solution.py:78
  147.5 0.6 shard_map.136
  (16 shorter events, 0.0 us)
Async XLA Ops:
  0.6 26.3 %copy-start.6 = (f32[512]{0:T(512)S(1)}, f32[512]{0:T(512)}, u32[]{:S(2)}) copy-start(f32[512]{0:T(512)} %param.10) | copy-start | bytes 6148
  2.1 24.8 %all-to-all-start = ((bf16[16,8,1024]{2,1,0:T(8,128)(2,1)}), bf16[16,8,1024]{2,1,0:T(8,128)(2,1)S(1)}, u32[]{:S(2)}, u32[]{:S(2)}) async-start(bf16[16,8,1024]{2,1,0:T(8,128)(2,1)} %shard_map.128.order), calls=%async_computation | async-start | bytes 524288 | tf_op jit(solution)/shard_map/all_to_all | solution.py:78
  13.2 4.8 %collective-permute-start = (f32[1,512]{1,0:T(1,128)}, f32[1,512]{1,0:T(1,128)S(1)}, u32[]{:S(2)}, u32[]{:S(2)}) collective-permute-start(f32[1,512]{1,0:T(1,128)} %bitcast.19), channel_id=1, source_target_pairs={{0,32},{32,0},{1,33},{33,1},{2,34},{34,2},{3,35},{35,3},{4,36},{36... | collective-permute-start | bytes 6152 | tf_op jit(solution)/shard_map/ppermute | solution.py:42
  26.9 17.6 %copy-start.3 = (bf16[16,8,1024]{2,1,0:T(8,128)(2,1)}, bf16[16,8,1024]{2,1,0:T(8,128)(2,1)S(1)}, u32[]{:S(2)}) copy-start(bf16[16,8,1024]{2,1,0:T(8,128)(2,1)S(1)} %all-to-all-done) | copy-start | bytes 786436
  43.4 4.7 %copy-start = (bf16[512,1536]{1,0:T(8,128)(2,1)S(1)}, bf16[512,1536]{1,0:T(8,128)(2,1)}, u32[]{:S(2)}) copy-start(bf16[512,1536]{1,0:T(8,128)(2,1)} %get-tuple-element.22.own_weights) | copy-start | bytes 4718596
  43.6 1.0 copy-start.2
  44.6 13.0 %all-to-all-start.2 = ((bf16[4,64,2048]{2,1,0:T(8,128)(2,1)}), bf16[4,64,2048]{2,1,0:T(8,128)(2,1)S(1)}, u32[]{:S(2)}, u32[]{:S(2)}) async-start(bf16[4,64,2048]{2,1,0:T(8,128)(2,1)} %copy-done.2), calls=%async_computation.2 | async-start | bytes 2097152 | tf_op jit(solution)/shard_map/all_to_all | solution.py:78
  48.1 9.4 %collective-permute-start.1 = (bf16[512,1536]{1,0:T(8,128)(2,1)S(1)}, bf16[512,1536]{1,0:T(8,128)(2,1)}, u32[]{:S(2)}, u32[]{:S(2)}) collective-permute-start(bf16[512,1536]{1,0:T(8,128)(2,1)S(1)} %copy-done), channel_id=1, source_target_pairs={{0,32},{32,0},{1,33},{33,1},{2,34},{34,2},{3,35},{35,3},{4,36},{36... | collective-permute-start | bytes 4718600 | tf_op jit(solution)/shard_map/ppermute | solution.py:42
  108.6 1.0 copy-start.1
  109.6 18.7 %all-to-all-start.5 = ((bf16[4,64,2048]{2,1,0:T(8,128)(2,1)}), bf16[4,64,2048]{2,1,0:T(8,128)(2,1)S(1)}, u32[]{:S(2)}, u32[]{:S(2)}) async-start(bf16[4,64,2048]{2,1,0:T(8,128)(2,1)} %bitcast.14), calls=%async_computation.5 | async-start | bytes 2097152 | tf_op jit(solution)/shard_map/all_to_all | solution.py:78
  118.8 9.5 %copy-start.4 = (bf16[16,8,1024]{2,1,0:T(8,128)(2,1)S(1)}, bf16[16,8,1024]{2,1,0:T(8,128)(2,1)}, u32[]{:S(2)}) copy-start(bf16[16,8,1024]{2,1,0:T(8,128)(2,1)} %copy-done.3) | copy-start | bytes 786436
  119.9 13.4 %copy-start.5 = (f32[512,128]{1,0:T(8,128)S(1)}, f32[512,128]{1,0:T(8,128)}, u32[]{:S(2)}) copy-start(f32[512,128]{1,0:T(8,128)} %get-tuple-element.25.scales) | copy-start | bytes 786436
  119.9 13.4 %copy-start.7 = (s32[4,4]{1,0:T(4,128)S(1)}, s32[4,4]{1,0:T(4,128)}, u32[]{:S(2)}) copy-start(s32[4,4]{1,0:T(4,128)} %gate_mask.3) | copy-start | bytes 196
  119.9 13.4 %copy-start.8 = (s32[4,4]{1,0:T(4,128)S(1)}, s32[4,4]{1,0:T(4,128)}, u32[]{:S(2)}) copy-start(s32[4,4]{1,0:T(4,128)} %up_mask.3) | copy-start | bytes 196
  119.9 13.4 %copy-start.9 = (s32[4,4]{1,0:T(4,128)S(1)}, s32[4,4]{1,0:T(4,128)}, u32[]{:S(2)}) copy-start(s32[4,4]{1,0:T(4,128)} %down_mask.3) | copy-start | bytes 196
  119.9 13.4 %collective-permute-start.2 = (bf16[256,2560]{1,0:T(8,128)(2,1)}, bf16[256,2560]{1,0:T(8,128)(2,1)}, u32[]{:S(2)}, u32[]{:S(2)}) collective-permute-start(bf16[256,2560]{1,0:T(8,128)(2,1)} %shard_map.137), channel_id=1, source_target_pairs={{0,32},{32,0},{1,33},{33,1},{2,34},{34,2},{3,35},{35,3},{4,36},{36... | collective-permute-start | bytes 3932168 | tf_op jit(solution)/shard_map/ppermute | solution.py:42
  129.3 18.2 %all-to-all-start.6 = ((bf16[16,8,1024]{2,1,0:T(8,128)(2,1)}), bf16[16,8,1024]{2,1,0:T(8,128)(2,1)S(1)}, u32[]{:S(2)}, u32[]{:S(2)}) async-start(bf16[16,8,1024]{2,1,0:T(8,128)(2,1)} %bitcast.7), calls=%async_computation.6 | async-start | bytes 524288 | tf_op jit(solution)/shard_map/all_to_all | solution.py:78

commit v12 on v11

--- a/solution.py
+++ b/solution.py
@@ -232,15 +232,27 @@
     return pl.ds(pl.multiple_of(core * 2 * width + start, TILE), count * width)
 
 
+def fetch(source, place, arrived):
+    pieces = arrived.shape[0]
+    rows = source.shape[0] // pieces
+    moves = []
+    for k in range(pieces):
+        piece = pl.ds(k * rows, rows)
+        moves.append(pltpu.make_async_copy(source.at[piece], place.at[piece], arrived.at[k]))
+    for move in moves:
+        move.start()
+    return moves
+
+
 def forward_kernel(core, both_in, own_weights, other_stored, sums, other_weights, arrived):
-    move = pltpu.make_async_copy(other_stored, other_weights, arrived)
-    move.start()
+    moves = fetch(other_stored, other_weights, arrived)
     width = own_weights.shape[0]
     split = sums.shape[1] - width
     gate_up = None
     for place, weights in ((core[0], own_weights), (1 - core[0], other_weights)):
         if weights is other_weights:
-            move.wait()
+            for move in moves:
+                move.wait()
         quantized = both_in[:, lanes_of(place, 0, width)]
         gradient = both_in[:, lanes_of(place, width, width)]
         first = matmul(quantized, weights[:, :split])
@@ -277,13 +289,13 @@
 
 
 def back_kernel(core, mid, own_weights, other_stored, back, other_weights, arrived):
-    move = pltpu.make_async_copy(other_stored, other_weights, arrived)
-    move.start()
+    moves = fetch(other_stored, other_weights, arrived)
     width = own_weights.shape[0]
     split = mid.shape[1] - width
     for place, weights in ((core[0], own_weights), (1 - core[0], other_weights)):
         if weights is other_weights:
-            move.wait()
+            for move in moves:
+                move.wait()
         output = matmul(mid[:, split:], weights[:, split:])
         back[:, lanes_of(place, 0, width)] = output.astype(back.dtype)
         quant_grad = contract_last(mid[:, :split], weights[:, :split])
@@ -421,7 +433,7 @@
         1,
         flops,
         stored=(3,),
-        scratch=[pltpu.VMEM(own_weights.shape, bf16), pltpu.SemaphoreType.DMA],
+        scratch=[pltpu.VMEM(own_weights.shape, bf16), pltpu.SemaphoreType.DMA((8,))],
     )
     parts = exchange(sums.reshape(N_Z, mid_tokens, -1), "z")
     mid = local_kernel(swiglu_kernel, [shape(parts.shape, bf16)], [parts])
@@ -433,7 +445,7 @@
         1,
         flops,
         stored=(3,),
-        scratch=[pltpu.VMEM(own_weights.shape, bf16), pltpu.SemaphoreType.DMA],
+        scratch=[pltpu.VMEM(own_weights.shape, bf16), pltpu.SemaphoreType.DMA((8,))],
     )
     parcel = local_kernel(
         parcel_kernel,

time: 149 us -> 149 us (level)
  no operation moved by 1% of the time
where the time goes in v12:
time: 149 us; the launch traced here: 148 us
  blocking collectives  62.8 us (42%)
  starting transfers between devices  35.2 us (24%)
  waiting for transfers between devices  32.1 us (22%)
  Pallas kernels  15.4 us (10%)
  local copies, waits for them, and re-layouts  1.96 us (1%)
    all_to_all x3, blocking collectives, exchange(): return lax.all_to_all(parts, axis, 0, 0, tiled=True)  62.8 us
    all_to_all x4, waiting for transfers between devices, exchange_in(): lax.all_to_all(parts, PLANE, 0, 0, axis_index_groups=groups, tiled=True)  32.1 us
    all_to_all x4, starting transfers between devices, exchange_in(): lax.all_to_all(parts, PLANE, 0, 0, axis_index_groups=groups, tiled=True)  27.8 us
    pallas_call x11, Pallas kernels, local_kernel(): pl.pallas_call(body, out_shape=outs if len(outs) > 1 else outs[0], in_spe...  15.4 us
    ppermute x3, starting transfers between devices, swap_cores(): return lax.ppermute(block, 'core', [(0, 1), (1, 0)])  7.41 us
  transfers between devices with their start and end apart: 7, of which 4 were waited for; matrix products, arithmetic and copies ran while one was open for 0% of the time, Pallas kernels for 6%

profile of v12, /device:TPU:1, one launch (start us, length us, event | category | flops | bytes accessed | tf_op | source)
XLA Modules:
  0.0 148.3 jit_solution(618897348208697872)
XLA Ops:
  0.6 0.0 copy-start.6
  0.6 1.5 shard_map.128.order
  2.1 11.1 %all-to-all-start = ((bf16[16,8,1024]{2,1,0:T(8,128)(2,1)}), bf16[16,8,1024]{2,1,0:T(8,128)(2,1)S(1)}, u32[]{:S(2)}, u32[]{:S(2)}) async-start(bf16[16,8,1024]{2,1,0:T(8,128)(2,1)} %shard_map.128.order), calls=%async_computation | async-start | bytes 524288 | tf_op jit(solution)/shard_map/all_to_all | solution.py:78
  13.2 2.0 %collective-permute-start = (f32[1,512]{1,0:T(1,128)}, f32[1,512]{1,0:T(1,128)S(1)}, u32[]{:S(2)}, u32[]{:S(2)}) collective-permute-start(f32[1,512]{1,0:T(1,128)} %bitcast.19), channel_id=1, source_target_pairs={{0,32},{32,0},{1,33},{33,1},{2,34},{34,2},{3,35},{35,3},{4,36},{36... | collective-permute-start | bytes 6152 | tf_op jit(solution)/shard_map/ppermute | solution.py:42
  15.2 2.7 %shard_map.129 = (bf16[512,1536]{1,0:T(8,128)(2,1)}, f32[512,128]{1,0:T(8,128)}) custom-call(s32[4,4]{1,0:T(4,128)} %gate_mask.3, s32[4,4]{1,0:T(4,128)} %up_mask.3, s32[4,4]{1,0:T(4,128)} %down_mask.3, f32[1,512]{1,0:T(1,128)} %bitcast.20, bf16[512,512]{1,0:T(8,128)(2,1)} %gate.1, bf16[512,512]{1,0:T(8,128)(2,1)} %up.1, bf16[512,512]{1,0:T(8,128)(2,1)} %down.1, ...), custom_call_target="tpu_custom_call" | custom-call | bytes 3672256 | tf_op jit(solution)/shard_map/pallas_call | solution.py:96
  18.0 0.0 collective-permute-done.other_scales
  18.0 8.9 %all-to-all-done = bf16[16,8,1024]{2,1,0:T(8,128)(2,1)S(1)} async-done(((bf16[16,8,1024]{2,1,0:T(8,128)(2,1)}), bf16[16,8,1024]{2,1,0:T(8,128)(2,1)S(1)}, u32[]{:S(2)}, u32[]{:S(2)}) %all-to-all-start) | async-done | bytes 262176 | tf_op jit(solution)/shard_map/all_to_all | solution.py:78
  26.9 0.1 shard_map.130
  27.1 16.4 %all_to_all.35.squares = f32[8,1,128]{2,1,0:T(1,128)S(1)} all-to-all(f32[8,1,128]{2,1,0:T(1,128)S(1)} %shard_map.130), channel_id=1, replica_groups=mesh['z'=8,'core'=2,'x'=4,'y'=8] {'z'}, dimensions={0} | all-to-all | bytes 8192 | tf_op jit(solution)/shard_map/all_to_all | solution.py:46
  43.4 0.2 shard_map.131
  43.6 0.0 copy-start.2
  43.6 1.0 copy-done.2
  44.6 3.5 %all-to-all-start.2 = ((bf16[4,64,2048]{2,1,0:T(8,128)(2,1)}), bf16[4,64,2048]{2,1,0:T(8,128)(2,1)S(1)}, u32[]{:S(2)}, u32[]{:S(2)}) async-start(bf16[4,64,2048]{2,1,0:T(8,128)(2,1)} %copy-done.2), calls=%async_computation.2 | async-start | bytes 2097152 | tf_op jit(solution)/shard_map/all_to_all | solution.py:78
  48.1 3.3 %collective-permute-start.1 = (bf16[512,1536]{1,0:T(8,128)(2,1)S(1)}, bf16[512,1536]{1,0:T(8,128)(2,1)}, u32[]{:S(2)}, u32[]{:S(2)}) collective-permute-start(bf16[512,1536]{1,0:T(8,128)(2,1)S(1)} %copy-done), channel_id=1, source_target_pairs={{0,32},{32,0},{1,33},{33,1},{2,34},{34,2},{3,35},{35,3},{4,36},{36... | collective-permute-start | bytes 4718600 | tf_op jit(solution)/shard_map/ppermute | solution.py:42
  51.5 6.1 %all-to-all-done.2 = bf16[4,64,2048]{2,1,0:T(8,128)(2,1)S(1)} async-done(((bf16[4,64,2048]{2,1,0:T(8,128)(2,1)}), bf16[4,64,2048]{2,1,0:T(8,128)(2,1)S(1)}, u32[]{:S(2)}, u32[]{:S(2)}) %all-to-all-start.2) | async-done | bytes 1048608 | tf_op jit(solution)/shard_map/all_to_all | solution.py:78
  57.5 0.0 collective-permute-done.1.other_stored
  57.5 2.5 %shard_map.132 = bf16[256,1536]{1,0:T(8,128)(2,1)S(1)} custom-call(s32[1]{0:T(128)} %bitcast.core, bf16[256,2048]{1,0:T(8,128)(2,1)S(1)} %bitcast.8, bf16[512,1536]{1,0:T(8,128)(2,1)S(1)} %copy-done, bf16[512,1536]{1,0:T(8,128)(2,1)} %collective-permute-done.1.other_stored), custom_call_target="tpu_custom_call" | custom-call | flops 805306368 | bytes 4980740 | tf_op jit(solution)/shard_map/pallas_call | solution.py:96
  60.1 23.5 %all_to_all.36.parts = bf16[8,32,1536]{2,1,0:T(8,128)(2,1)S(1)} all-to-all(bf16[8,32,1536]{2,1,0:T(8,128)(2,1)S(1)} %bitcast.18), channel_id=1, replica_groups=mesh['z'=8,'core'=2,'x'=4,'y'=8] {'z'}, dimensions={0} | all-to-all | bytes 1572864 | tf_op jit(solution)/shard_map/all_to_all | solution.py:46
  83.5 0.2 shard_map.133
  83.7 23.0 %all_to_all.37 = bf16[8,32,1536]{2,1,0:T(8,128)(2,1)S(1)} all-to-all(bf16[8,32,1536]{2,1,0:T(8,128)(2,1)S(1)} %shard_map.133), channel_id=1, replica_groups=mesh['z'=8,'core'=2,'x'=4,'y'=8] {'z'}, dimensions={0} | all-to-all | bytes 1572864 | tf_op jit(solution)/shard_map/all_to_all | solution.py:46
  106.7 2.1 %shard_map.134 = bf16[256,2048]{1,0:T(8,128)(2,1)S(1)} custom-call(s32[1]{0:T(128)} %bitcast.core, bf16[256,1536]{1,0:T(8,128)(2,1)S(1)} %bitcast.11, bf16[512,1536]{1,0:T(8,128)(2,1)S(1)} %copy-done, bf16[512,1536]{1,0:T(8,128)(2,1)} %collective-permute-done.1.other_stored), custom_call_target="tpu_custom_call" | custom-call | flops 805306368 | bytes 4980740 | tf_op jit(solution)/shard_map/pallas_call | solution.py:96
  108.8 1.0 copy-done.1
  109.8 9.2 %all-to-all-start.5 = ((bf16[4,64,2048]{2,1,0:T(8,128)(2,1)}), bf16[4,64,2048]{2,1,0:T(8,128)(2,1)S(1)}, u32[]{:S(2)}, u32[]{:S(2)}) async-start(bf16[4,64,2048]{2,1,0:T(8,128)(2,1)} %bitcast.14), calls=%async_computation.5 | async-start | bytes 2097152 | tf_op jit(solution)/shard_map/all_to_all | solution.py:78
  119.0 1.2 shard_map.137
  120.1 2.1 %collective-permute-start.2 = (bf16[256,2560]{1,0:T(8,128)(2,1)}, bf16[256,2560]{1,0:T(8,128)(2,1)}, u32[]{:S(2)}, u32[]{:S(2)}) collective-permute-start(bf16[256,2560]{1,0:T(8,128)(2,1)} %shard_map.137), channel_id=1, source_target_pairs={{0,32},{32,0},{1,33},{33,1},{2,34},{34,2},{3,35},{35,3},{4,36},{36... | collective-permute-start | bytes 3932168 | tf_op jit(solution)/shard_map/ppermute | solution.py:42
  122.2 6.3 %all-to-all-done.5.parts = bf16[4,64,2048]{2,1,0:T(8,128)(2,1)S(1)} async-done(((bf16[4,64,2048]{2,1,0:T(8,128)(2,1)}), bf16[4,64,2048]{2,1,0:T(8,128)(2,1)S(1)}, u32[]{:S(2)}, u32[]{:S(2)}) %all-to-all-start.5) | async-done | bytes 1048608 | tf_op jit(solution)/shard_map/all_to_all | solution.py:78
  128.5 1.0 shard_map.135
  129.5 4.0 %all-to-all-start.6 = ((bf16[16,8,1024]{2,1,0:T(8,128)(2,1)}), bf16[16,8,1024]{2,1,0:T(8,128)(2,1)S(1)}, u32[]{:S(2)}, u32[]{:S(2)}) async-start(bf16[16,8,1024]{2,1,0:T(8,128)(2,1)} %bitcast.7), calls=%async_computation.6 | async-start | bytes 524288 | tf_op jit(solution)/shard_map/all_to_all | solution.py:78
  133.5 0.0 collective-permute-done.2.parcel
  133.6 3.3 %shard_map.138 = (bf16[512,512]{1,0:T(8,128)(2,1)}, bf16[512,512]{1,0:T(8,128)(2,1)}, bf16[512,512]{1,0:T(8,128)(2,1)}) custom-call(s32[1]{0:T(128)} %bitcast.core, s32[4,4]{1,0:T(4,128)S(1)} %copy-done.7, s32[4,4]{1,0:T(4,128)S(1)} %copy-done.8, s32[4,4]{1,0:T(4,128)S(1)} %copy-done.9, bf16[256,2048]{1,0:T(8,128)(2,1)S(1)} %bitcast.10, ...), custom_call_target="tpu_custom_call" | custom-call | flops 805306368 | bytes 4980932 | tf_op jit(solution)/shard_map/pallas_call | solution.py:96
  136.8 10.8 %all-to-all-done.6.parts = bf16[16,8,1024]{2,1,0:T(8,128)(2,1)S(1)} async-done(((bf16[16,8,1024]{2,1,0:T(8,128)(2,1)}), bf16[16,8,1024]{2,1,0:T(8,128)(2,1)S(1)}, u32[]{:S(2)}, u32[]{:S(2)}) %all-to-all-start.6) | async-done | bytes 262176 | tf_op jit(solution)/shard_map/all_to_all | solution.py:78
  147.7 0.6 shard_map.136
  (16 shorter events, 0.0 us)
Async XLA Ops:
  0.6 26.3 %copy-start.6 = (f32[512]{0:T(512)S(1)}, f32[512]{0:T(512)}, u32[]{:S(2)}) copy-start(f32[512]{0:T(512)} %param.10) | copy-start | bytes 6148
  2.1 24.8 %all-to-all-start = ((bf16[16,8,1024]{2,1,0:T(8,128)(2,1)}), bf16[16,8,1024]{2,1,0:T(8,128)(2,1)S(1)}, u32[]{:S(2)}, u32[]{:S(2)}) async-start(bf16[16,8,1024]{2,1,0:T(8,128)(2,1)} %shard_map.128.order), calls=%async_computation | async-start | bytes 524288 | tf_op jit(solution)/shard_map/all_to_all | solution.py:78
  13.2 4.8 %collective-permute-start = (f32[1,512]{1,0:T(1,128)}, f32[1,512]{1,0:T(1,128)S(1)}, u32[]{:S(2)}, u32[]{:S(2)}) collective-permute-start(f32[1,512]{1,0:T(1,128)} %bitcast.19), channel_id=1, source_target_pairs={{0,32},{32,0},{1,33},{33,1},{2,34},{34,2},{3,35},{35,3},{4,36},{36... | collective-permute-start | bytes 6152 | tf_op jit(solution)/shard_map/ppermute | solution.py:42
  26.9 17.6 %copy-start.3 = (bf16[16,8,1024]{2,1,0:T(8,128)(2,1)}, bf16[16,8,1024]{2,1,0:T(8,128)(2,1)S(1)}, u32[]{:S(2)}) copy-start(bf16[16,8,1024]{2,1,0:T(8,128)(2,1)S(1)} %all-to-all-done) | copy-start | bytes 786436
  43.4 4.7 %copy-start = (bf16[512,1536]{1,0:T(8,128)(2,1)S(1)}, bf16[512,1536]{1,0:T(8,128)(2,1)}, u32[]{:S(2)}) copy-start(bf16[512,1536]{1,0:T(8,128)(2,1)} %get-tuple-element.22.own_weights) | copy-start | bytes 4718596
  43.6 1.0 copy-start.2
  44.6 13.0 %all-to-all-start.2 = ((bf16[4,64,2048]{2,1,0:T(8,128)(2,1)}), bf16[4,64,2048]{2,1,0:T(8,128)(2,1)S(1)}, u32[]{:S(2)}, u32[]{:S(2)}) async-start(bf16[4,64,2048]{2,1,0:T(8,128)(2,1)} %copy-done.2), calls=%async_computation.2 | async-start | bytes 2097152 | tf_op jit(solution)/shard_map/all_to_all | solution.py:78
  48.1 9.4 %collective-permute-start.1 = (bf16[512,1536]{1,0:T(8,128)(2,1)S(1)}, bf16[512,1536]{1,0:T(8,128)(2,1)}, u32[]{:S(2)}, u32[]{:S(2)}) collective-permute-start(bf16[512,1536]{1,0:T(8,128)(2,1)S(1)} %copy-done), channel_id=1, source_target_pairs={{0,32},{32,0},{1,33},{33,1},{2,34},{34,2},{3,35},{35,3},{4,36},{36... | collective-permute-start | bytes 4718600 | tf_op jit(solution)/shard_map/ppermute | solution.py:42
  108.8 1.0 copy-start.1
  109.8 18.7 %all-to-all-start.5 = ((bf16[4,64,2048]{2,1,0:T(8,128)(2,1)}), bf16[4,64,2048]{2,1,0:T(8,128)(2,1)S(1)}, u32[]{:S(2)}, u32[]{:S(2)}) async-start(bf16[4,64,2048]{2,1,0:T(8,128)(2,1)} %bitcast.14), calls=%async_computation.5 | async-start | bytes 2097152 | tf_op jit(solution)/shard_map/all_to_all | solution.py:78
  119.0 9.5 %copy-start.4 = (bf16[16,8,1024]{2,1,0:T(8,128)(2,1)S(1)}, bf16[16,8,1024]{2,1,0:T(8,128)(2,1)}, u32[]{:S(2)}) copy-start(bf16[16,8,1024]{2,1,0:T(8,128)(2,1)} %copy-done.3) | copy-start | bytes 786436
  120.1 13.4 %copy-start.5 = (f32[512,128]{1,0:T(8,128)S(1)}, f32[512,128]{1,0:T(8,128)}, u32[]{:S(2)}) copy-start(f32[512,128]{1,0:T(8,128)} %get-tuple-element.25.scales) | copy-start | bytes 786436
  120.1 13.4 %copy-start.7 = (s32[4,4]{1,0:T(4,128)S(1)}, s32[4,4]{1,0:T(4,128)}, u32[]{:S(2)}) copy-start(s32[4,4]{1,0:T(4,128)} %gate_mask.3) | copy-start | bytes 196
  120.1 13.4 %copy-start.8 = (s32[4,4]{1,0:T(4,128)S(1)}, s32[4,4]{1,0:T(4,128)}, u32[]{:S(2)}) copy-start(s32[4,4]{1,0:T(4,128)} %up_mask.3) | copy-start | bytes 196
  120.1 13.4 %copy-start.9 = (s32[4,4]{1,0:T(4,128)S(1)}, s32[4,4]{1,0:T(4,128)}, u32[]{:S(2)}) copy-start(s32[4,4]{1,0:T(4,128)} %down_mask.3) | copy-start | bytes 196
  120.1 13.4 %collective-permute-start.2 = (bf16[256,2560]{1,0:T(8,128)(2,1)}, bf16[256,2560]{1,0:T(8,128)(2,1)}, u32[]{:S(2)}, u32[]{:S(2)}) collective-permute-start(bf16[256,2560]{1,0:T(8,128)(2,1)} %shard_map.137), channel_id=1, source_target_pairs={{0,32},{32,0},{1,33},{33,1},{2,34},{34,2},{3,35},{35,3},{4,36},{36... | collective-permute-start | bytes 3932168 | tf_op jit(solution)/shard_map/ppermute | solution.py:42
  129.5 18.2 %all-to-all-start.6 = ((bf16[16,8,1024]{2,1,0:T(8,128)(2,1)}), bf16[16,8,1024]{2,1,0:T(8,128)(2,1)S(1)}, u32[]{:S(2)}, u32[]{:S(2)}) async-start(bf16[16,8,1024]{2,1,0:T(8,128)(2,1)} %bitcast.7), calls=%async_computation.6 | async-start | bytes 524288 | tf_op jit(solution)/shard_map/all_to_all | solution.py:78

commit v13 on v10

--- a/solution.py
+++ b/solution.py
@@ -121,10 +121,9 @@
     ]
     for move in moves:
         move.start()
-    for move in moves:
-        move.wait()
     rows, width = copies.shape[1], tokens.shape[1]
     for k, source in enumerate((tokens_here, cotangent_here)):
+        moves[k].wait()
         value = source[...].astype(jnp.float32)
         for half in range(N_CORE):
             block = value[half * rows : (half + 1) * rows].astype(copies.dtype)

time: 148 us -> 148 us (level)
  no operation moved by 1% of the time
where the time goes in v13:
time: 148 us
  blocking collectives  77.7 us (52%)
  starting transfers between devices  30.1 us (20%)
  waiting for transfers between devices  25.2 us (17%)
  Pallas kernels  13.7 us (9%)
    all_to_all x3, blocking collectives, exchange(): return lax.all_to_all(parts, axis, 0, 0, tiled=True)  63.9 us
    all_to_all x3, waiting for transfers between devices, exchange_in(): lax.all_to_all(parts, PLANE, 0, 0, axis_index_groups=groups, tiled=True)  25.2 us
    all_to_all x3, starting transfers between devices, exchange_in(): lax.all_to_all(parts, PLANE, 0, 0, axis_index_groups=groups, tiled=True)  23.4 us
    all_to_all x1, blocking collectives, exchange_in(): lax.all_to_all(parts, PLANE, 0, 0, axis_index_groups=groups, tiled=True)  13.8 us
    pallas_call x11, Pallas kernels, local_kernel(): pl.pallas_call(body, out_shape=outs if len(outs) > 1 else outs[0], in_spe...  13.7 us
    ppermute x3, starting transfers between devices, swap_cores(): return lax.ppermute(block, 'core', [(0, 1), (1, 0)])  6.77 us
  transfers between devices with their start and end apart: 6, of which 3 were waited for; matrix products, arithmetic and copies ran while one was open for 0% of the time, Pallas kernels for 6%

profile of v13, /device:TPU:1, one launch (start us, length us, event | category | flops | bytes accessed | tf_op | source)
XLA Modules:
  0.0 147.5 jit_solution(5254215144554809618)
XLA Ops:
  0.6 0.0 copy-start.2
  0.6 1.5 shard_map.128.order
  2.1 11.1 %all-to-all-start = ((bf16[16,8,1024]{2,1,0:T(8,128)(2,1)}), bf16[16,8,1024]{2,1,0:T(8,128)(2,1)S(1)}, u32[]{:S(2)}, u32[]{:S(2)}) async-start(bf16[16,8,1024]{2,1,0:T(8,128)(2,1)} %shard_map.128.order), calls=%async_computation | async-start | bytes 524288 | tf_op jit(solution)/shard_map/all_to_all | solution.py:78
  13.2 2.0 %collective-permute-start = (f32[1,512]{1,0:T(1,128)}, f32[1,512]{1,0:T(1,128)S(1)}, u32[]{:S(2)}, u32[]{:S(2)}) collective-permute-start(f32[1,512]{1,0:T(1,128)} %bitcast.18), channel_id=1, source_target_pairs={{0,32},{32,0},{1,33},{33,1},{2,34},{34,2},{3,35},{35,3},{4,36},{36... | collective-permute-start | bytes 6152 | tf_op jit(solution)/shard_map/ppermute | solution.py:42
  15.2 2.8 %shard_map.129 = (bf16[512,1536]{1,0:T(8,128)(2,1)}, f32[512,128]{1,0:T(8,128)}) custom-call(s32[4,4]{1,0:T(4,128)} %gate_mask.3, s32[4,4]{1,0:T(4,128)} %up_mask.3, s32[4,4]{1,0:T(4,128)} %down_mask.3, f32[1,512]{1,0:T(1,128)} %bitcast.19, bf16[512,512]{1,0:T(8,128)(2,1)} %gate.1, bf16[512,512]{1,0:T(8,128)(2,1)} %up.1, bf16[512,512]{1,0:T(8,128)(2,1)} %down.1, ...), custom_call_target="tpu_custom_call" | custom-call | bytes 3672256 | tf_op jit(solution)/shard_map/pallas_call | solution.py:96
  18.0 0.0 collective-permute-done.other_scales
  18.0 8.9 %all-to-all-done = bf16[16,8,1024]{2,1,0:T(8,128)(2,1)S(1)} async-done(((bf16[16,8,1024]{2,1,0:T(8,128)(2,1)}), bf16[16,8,1024]{2,1,0:T(8,128)(2,1)S(1)}, u32[]{:S(2)}, u32[]{:S(2)}) %all-to-all-start) | async-done | bytes 262176 | tf_op jit(solution)/shard_map/all_to_all | solution.py:78
  26.9 1.9 %collective-permute-start.1 = (bf16[512,1536]{1,0:T(8,128)(2,1)}, bf16[512,1536]{1,0:T(8,128)(2,1)S(1)}, u32[]{:S(2)}, u32[]{:S(2)}) collective-permute-start(bf16[512,1536]{1,0:T(8,128)(2,1)} %get-tuple-element.20.own_weights), channel_id=1, source_target_pairs={{0,32},{32,0},{1,33},{33,1},{2,34},{34,2},{3,35},{35,3},{4,36},{36... | collective-permute-start | bytes 4718600 | tf_op jit(solution)/shard_map/ppermute | solution.py:42
  28.8 0.0 copy-done.2
  28.8 0.1 shard_map.130
  29.0 16.4 %all_to_all.35.squares = f32[8,1,128]{2,1,0:T(1,128)S(1)} all-to-all(f32[8,1,128]{2,1,0:T(1,128)S(1)} %shard_map.130), channel_id=1, replica_groups=mesh['z'=8,'core'=2,'x'=4,'y'=8] {'z'}, dimensions={0} | all-to-all | bytes 8192 | tf_op jit(solution)/shard_map/all_to_all | solution.py:46
  45.3 0.2 shard_map.131
  45.5 0.0 collective-permute-done.1.other_weights
  45.5 13.8 %all_to_all.36 = bf16[4,64,2048]{2,1,0:T(8,128)(2,1)S(1)} all-to-all(bf16[4,64,2048]{2,1,0:T(8,128)(2,1)S(1)} %shard_map.131), channel_id=1, replica_groups={{0,1,8,9},{2,3,10,11},{4,5,12,13},{6,7,14,15},{16,17,24,25},{18,19,26,2..., dimensions={0} | all-to-all | bytes 2097152 | tf_op jit(solution)/shard_map/all_to_all | solution.py:78
  59.3 0.0 copy-done
  59.3 1.0 shard_map.132
  60.3 24.7 %all_to_all.37.parts = bf16[8,32,1536]{2,1,0:T(8,128)(2,1)S(1)} all-to-all(bf16[8,32,1536]{2,1,0:T(8,128)(2,1)S(1)} %bitcast.17), channel_id=1, replica_groups=mesh['z'=8,'core'=2,'x'=4,'y'=8] {'z'}, dimensions={0} | all-to-all | bytes 1572864 | tf_op jit(solution)/shard_map/all_to_all | solution.py:46
  85.0 0.2 shard_map.133
  85.1 22.8 %all_to_all.38 = bf16[8,32,1536]{2,1,0:T(8,128)(2,1)S(1)} all-to-all(bf16[8,32,1536]{2,1,0:T(8,128)(2,1)S(1)} %shard_map.133), channel_id=1, replica_groups=mesh['z'=8,'core'=2,'x'=4,'y'=8] {'z'}, dimensions={0} | all-to-all | bytes 1572864 | tf_op jit(solution)/shard_map/all_to_all | solution.py:46
  108.0 2.0 %shard_map.134 = bf16[256,2048]{1,0:T(8,128)(2,1)} custom-call(s32[1]{0:T(128)} %bitcast.core, bf16[256,1536]{1,0:T(8,128)(2,1)S(1)} %bitcast.11, bf16[512,1536]{1,0:T(8,128)(2,1)S(1)} %copy-done, bf16[512,1536]{1,0:T(8,128)(2,1)S(1)} %collective-permute-done.1.other_weights), custom_call_target="tpu_custom_call" | custom-call | flops 805306368 | bytes 4980740 | tf_op jit(solution)/shard_map/pallas_call | solution.py:96
  110.0 6.3 %all-to-all-start.5 = ((bf16[4,64,2048]{2,1,0:T(8,128)(2,1)}), bf16[4,64,2048]{2,1,0:T(8,128)(2,1)S(1)}, u32[]{:S(2)}, u32[]{:S(2)}) async-start(bf16[4,64,2048]{2,1,0:T(8,128)(2,1)} %bitcast.6), calls=%async_computation.5 | async-start | bytes 2097152 | tf_op jit(solution)/shard_map/all_to_all | solution.py:78
  116.3 1.2 shard_map.137
  117.5 2.9 %collective-permute-start.2 = (bf16[256,2560]{1,0:T(8,128)(2,1)}, bf16[256,2560]{1,0:T(8,128)(2,1)}, u32[]{:S(2)}, u32[]{:S(2)}) collective-permute-start(bf16[256,2560]{1,0:T(8,128)(2,1)} %shard_map.137), channel_id=1, source_target_pairs={{0,32},{32,0},{1,33},{33,1},{2,34},{34,2},{3,35},{35,3},{4,36},{36... | collective-permute-start | bytes 3932168 | tf_op jit(solution)/shard_map/ppermute | solution.py:42
  120.3 5.5 %all-to-all-done.5.parts = bf16[4,64,2048]{2,1,0:T(8,128)(2,1)S(1)} async-done(((bf16[4,64,2048]{2,1,0:T(8,128)(2,1)}), bf16[4,64,2048]{2,1,0:T(8,128)(2,1)S(1)}, u32[]{:S(2)}, u32[]{:S(2)}) %all-to-all-start.5) | async-done | bytes 1048608 | tf_op jit(solution)/shard_map/all_to_all | solution.py:78
  125.8 1.0 shard_map.135
  126.8 5.9 %all-to-all-start.6 = ((bf16[16,8,1024]{2,1,0:T(8,128)(2,1)}), bf16[16,8,1024]{2,1,0:T(8,128)(2,1)S(1)}, u32[]{:S(2)}, u32[]{:S(2)}) async-start(bf16[16,8,1024]{2,1,0:T(8,128)(2,1)} %bitcast.7), calls=%async_computation.6 | async-start | bytes 524288 | tf_op jit(solution)/shard_map/all_to_all | solution.py:78
  132.8 0.0 collective-permute-done.2.parcel
  132.8 0.0 copy-done.1
  132.8 0.0 copy-done.3
  132.8 3.3 %shard_map.138 = (bf16[512,512]{1,0:T(8,128)(2,1)}, bf16[512,512]{1,0:T(8,128)(2,1)}, bf16[512,512]{1,0:T(8,128)(2,1)}) custom-call(s32[1]{0:T(128)} %bitcast.core, s32[4,4]{1,0:T(4,128)S(1)} %copy-done.3, s32[4,4]{1,0:T(4,128)S(1)} %copy-done.4, s32[4,4]{1,0:T(4,128)S(1)} %copy-done.5, bf16[256,2048]{1,0:T(8,128)(2,1)S(1)} %bitcast.10, ...), custom_call_target="tpu_custom_call" | custom-call | flops 805306368 | bytes 4980932 | tf_op jit(solution)/shard_map/pallas_call | solution.py:96
  136.1 10.8 %all-to-all-done.6.parts = bf16[16,8,1024]{2,1,0:T(8,128)(2,1)S(1)} async-done(((bf16[16,8,1024]{2,1,0:T(8,128)(2,1)}), bf16[16,8,1024]{2,1,0:T(8,128)(2,1)S(1)}, u32[]{:S(2)}, u32[]{:S(2)}) %all-to-all-start.6) | async-done | bytes 262176 | tf_op jit(solution)/shard_map/all_to_all | solution.py:78
  146.9 0.6 shard_map.136
  (7 shorter events, 0.0 us)
Async XLA Ops:
  0.6 28.2 %copy-start.2 = (f32[512]{0:T(512)S(1)}, f32[512]{0:T(512)}, u32[]{:S(2)}) copy-start(f32[512]{0:T(512)} %param.10) | copy-start | bytes 6148
  2.1 24.8 %all-to-all-start = ((bf16[16,8,1024]{2,1,0:T(8,128)(2,1)}), bf16[16,8,1024]{2,1,0:T(8,128)(2,1)S(1)}, u32[]{:S(2)}, u32[]{:S(2)}) async-start(bf16[16,8,1024]{2,1,0:T(8,128)(2,1)} %shard_map.128.order), calls=%async_computation | async-start | bytes 524288 | tf_op jit(solution)/shard_map/all_to_all | solution.py:78
  13.2 4.8 %collective-permute-start = (f32[1,512]{1,0:T(1,128)}, f32[1,512]{1,0:T(1,128)S(1)}, u32[]{:S(2)}, u32[]{:S(2)}) collective-permute-start(f32[1,512]{1,0:T(1,128)} %bitcast.18), channel_id=1, source_target_pairs={{0,32},{32,0},{1,33},{33,1},{2,34},{34,2},{3,35},{35,3},{4,36},{36... | collective-permute-start | bytes 6152 | tf_op jit(solution)/shard_map/ppermute | solution.py:42
  26.9 18.6 %collective-permute-start.1 = (bf16[512,1536]{1,0:T(8,128)(2,1)}, bf16[512,1536]{1,0:T(8,128)(2,1)S(1)}, u32[]{:S(2)}, u32[]{:S(2)}) collective-permute-start(bf16[512,1536]{1,0:T(8,128)(2,1)} %get-tuple-element.20.own_weights), channel_id=1, source_target_pairs={{0,32},{32,0},{1,33},{33,1},{2,34},{34,2},{3,35},{35,3},{4,36},{36... | collective-permute-start | bytes 4718600 | tf_op jit(solution)/shard_map/ppermute | solution.py:42
  45.3 13.9 %copy-start = (bf16[512,1536]{1,0:T(8,128)(2,1)S(1)}, bf16[512,1536]{1,0:T(8,128)(2,1)}, u32[]{:S(2)}) copy-start(bf16[512,1536]{1,0:T(8,128)(2,1)} %get-tuple-element.20.own_weights) | copy-start | bytes 4718596
  110.0 15.8 %all-to-all-start.5 = ((bf16[4,64,2048]{2,1,0:T(8,128)(2,1)}), bf16[4,64,2048]{2,1,0:T(8,128)(2,1)S(1)}, u32[]{:S(2)}, u32[]{:S(2)}) async-start(bf16[4,64,2048]{2,1,0:T(8,128)(2,1)} %bitcast.6), calls=%async_computation.5 | async-start | bytes 2097152 | tf_op jit(solution)/shard_map/all_to_all | solution.py:78
  117.5 15.3 %copy-start.1 = (f32[512,128]{1,0:T(8,128)S(1)}, f32[512,128]{1,0:T(8,128)}, u32[]{:S(2)}) copy-start(f32[512,128]{1,0:T(8,128)} %get-tuple-element.25.scales) | copy-start | bytes 786436
  117.5 15.3 %copy-start.3 = (s32[4,4]{1,0:T(4,128)S(1)}, s32[4,4]{1,0:T(4,128)}, u32[]{:S(2)}) copy-start(s32[4,4]{1,0:T(4,128)} %gate_mask.3) | copy-start | bytes 196
  117.5 15.3 %copy-start.4 = (s32[4,4]{1,0:T(4,128)S(1)}, s32[4,4]{1,0:T(4,128)}, u32[]{:S(2)}) copy-start(s32[4,4]{1,0:T(4,128)} %up_mask.3) | copy-start | bytes 196
  117.5 15.3 %copy-start.5 = (s32[4,4]{1,0:T(4,128)S(1)}, s32[4,4]{1,0:T(4,128)}, u32[]{:S(2)}) copy-start(s32[4,4]{1,0:T(4,128)} %down_mask.3) | copy-start | bytes 196
  117.5 15.3 %collective-permute-start.2 = (bf16[256,2560]{1,0:T(8,128)(2,1)}, bf16[256,2560]{1,0:T(8,128)(2,1)}, u32[]{:S(2)}, u32[]{:S(2)}) collective-permute-start(bf16[256,2560]{1,0:T(8,128)(2,1)} %shard_map.137), channel_id=1, source_target_pairs={{0,32},{32,0},{1,33},{33,1},{2,34},{34,2},{3,35},{35,3},{4,36},{36... | collective-permute-start | bytes 3932168 | tf_op jit(solution)/shard_map/ppermute | solution.py:42
  126.8 20.1 %all-to-all-start.6 = ((bf16[16,8,1024]{2,1,0:T(8,128)(2,1)}), bf16[16,8,1024]{2,1,0:T(8,128)(2,1)S(1)}, u32[]{:S(2)}, u32[]{:S(2)}) async-start(bf16[16,8,1024]{2,1,0:T(8,128)(2,1)} %bitcast.7), calls=%async_computation.6 | async-start | bytes 524288 | tf_op jit(solution)/shard_map/all_to_all | solution.py:78
